TPU v7x, 32 devices: a whole 2x2x4 slice. The times are simulated.
32 devices in a mesh: tx: 2 (over core), ty: 16 (over z, y, x).
Axes of the slice: x: 2, y: 2, z: 4, core: 2. Of those that a mesh axis runs over, the one named last changes fastest.
Arguments:
- handoff: int32 [2, 16, 48, 1], P('tx', 'ty'), may hold values from 0 to 8, as said below
- cells: int32 [2, 16, 48, 128], P('tx', 'ty'), may hold values from 0 to 32767
- offsets: int32 [2, 16, 48, 3, 128], P('tx', 'ty'), may hold values from 0 to 15
- drag: float32 [2, 16, 48, 3, 128], P('tx', 'ty'), may hold values from -6 to 6
- bubble_velocity: float32 [2, 16, 48, 3, 128], P('tx', 'ty'), may hold values from -6 to 6
- gas: float32 [3, 32, 256, 128], P(None, 'tx', 'ty'), may hold values from -6 to 6
Outputs:
- gas_new: float32 [3, 32, 256, 128], P(None, 'tx', 'ty')
- slip: float32 [2, 16, 64, 3, 128], P('tx', 'ty')
Inputs may be any that keep to these rules, and one draw needn't show every extreme that they name: `handoff`: of one tile's 48 blocks at most 2 carry the same code other than 4, and in every draw some tile has exactly 2 blocks with one such code. How many blocks keep code 4 varies from tile to tile. `cells`: linear index ix * 16 * 128 + iy * 128 + iz of the bubble's cell within the tile that holds its block after the handoff. `offsets`: position of the bubble inside its cell along each dimension, in sixteenths.
All inputs are finite; a program needn't handle non-finite values.
Results may differ from a plain program's by a relative error of at most 0.0003.
Values sent between devices are 32-bit elements; how exact they have to be, the bound alone decides.
No kernel may reach another device: no remote copies, remote signals or barrier semaphores. Data moves between devices by JAX's collectives and lax.ppermute only.
A program may use at most 64 MiB of HBM per device.

v0:
```python
import jax
import jax.numpy as jnp
from jax import lax
from jax.sharding import PartitionSpec as P

SWEEPS = 4
CAP = 2


DIFFUSE = 1.0
STEP_SIZE = 2.0
HIGHEST = lax.Precision.HIGHEST


def with_halo(block, sides, width):
    for axis, dim in sides:
        count = lax.axis_size(axis)
        forward = [(i, i + 1) for i in range(count - 1)]
        forward.append((count - 1, 0))
        backward = [(target, source) for source, target in forward]
        low = lax.ppermute(
            lax.slice_in_dim(block, block.shape[dim] - width, None, axis=dim), axis, forward
        )
        high = lax.ppermute(lax.slice_in_dim(block, 0, width, axis=dim), axis, backward)
        block = jnp.concatenate([low, block, high], axis=dim)
    return block


def tsc_weights(sixteenths):
    fraction = (sixteenths.astype(jnp.float32) + 0.5) / 16.0 - 0.5
    return (0.5 * (0.5 - fraction) ** 2, 0.75 - fraction * fraction, 0.5 * (0.5 + fraction) ** 2)


def weighted_rows(count, position, along):
    rows_all = jnp.arange(count, dtype=jnp.int32)[:, None]
    table = jnp.where(rows_all == position[None, :] - 1, along[0][None, :], 0.0)
    table = table + jnp.where(rows_all == position[None, :], along[1][None, :], 0.0)
    return table + jnp.where(rows_all == position[None, :] + 1, along[2][None, :], 0.0)


def tables(flattened, width_x, width_y, column_depth):
    cell_index = flattened[6].astype(jnp.int32)
    cell_x = cell_index // (width_y * column_depth)
    cell_y = cell_index // column_depth % width_y
    cell_z = cell_index % column_depth
    along_x = tsc_weights(flattened[7].astype(jnp.int32))
    along_y = tsc_weights(flattened[8].astype(jnp.int32))
    along_z = tsc_weights(flattened[9].astype(jnp.int32))
    table_x = weighted_rows(width_x + 2, cell_x + 1, along_x)
    table_y = weighted_rows(width_y + 2, cell_y + 1, along_y)
    rows_z = jnp.arange(column_depth, dtype=jnp.int32)[:, None]
    table_z = jnp.where(rows_z == (cell_z[None, :] - 1) % column_depth, along_z[0][None, :], 0.0)
    table_z = table_z + jnp.where(rows_z == cell_z[None, :], along_z[1][None, :], 0.0)
    table_z = table_z + jnp.where(
        rows_z == (cell_z[None, :] + 1) % column_depth, along_z[2][None, :], 0.0
    )
    planar = (table_x[:, None, :] * table_y[None, :, :]).reshape((width_x + 2) * (width_y + 2), -1)
    return (planar, table_z)


def relax(padded, source):
    centre = padded[:, 1:-1, 1:-1]
    beside_all = (
        padded[:, 2:, 1:-1] + padded[:, :-2, 1:-1] + padded[:, 1:-1, 2:] + padded[:, 1:-1, :-2]
    )
    beside_all = beside_all + jnp.roll(centre, 1, axis=3) + jnp.roll(centre, -1, axis=3)
    return (source + DIFFUSE * beside_all) / (1.0 + 6.0 * DIFFUSE)


def on_device(handoff, cells, offsets, drag, bubble_velocity, gas):
    width_x, width_y, column_depth = (gas.shape[1], gas.shape[2], gas.shape[3])
    per_block = cells.shape[3]
    dest_codes = handoff[0, 0, :, 0]
    slot_count = dest_codes.shape[0]
    matches = (dest_codes[:, None] == jnp.arange(9, dtype=jnp.int32)[None, :]).astype(jnp.int32)
    rank_in = jnp.sum((jnp.cumsum(matches, axis=0) - 1) * matches, axis=1)
    target = jnp.where(dest_codes == 4, -1, dest_codes * CAP + rank_in)
    placed = (target[None, :] == jnp.arange(9 * CAP, dtype=jnp.int32)[:, None]).astype(jnp.int32)
    source_slot = jnp.sum(placed * jnp.arange(slot_count, dtype=jnp.int32)[None, :], axis=1)
    occupied = jnp.sum(placed, axis=1).astype(jnp.float32)
    stay = (dest_codes == 4).astype(jnp.float32)
    fields = jnp.concatenate(
        [
            drag[0, 0],
            bubble_velocity[0, 0],
            cells[0, 0][:, None, :].astype(jnp.float32),
            offsets[0, 0].astype(jnp.float32),
        ],
        axis=1,
    )
    payload = jnp.concatenate([fields, jnp.ones((slot_count, 1, per_block), jnp.float32)], axis=1)
    own_rows = jnp.concatenate(
        [fields, jnp.broadcast_to(stay[:, None, None], (slot_count, 1, per_block))], axis=1
    )
    outgoing = jnp.take(payload, source_slot, axis=0) * occupied[:, None, None]
    outgoing = outgoing.reshape(3, 3, CAP, 11, per_block)
    extended = with_halo(outgoing, (("tx", 0), ("ty", 1)), 1)
    arrivals = extended[0::2, 0::2]
    arrivals = arrivals.reshape(9, CAP, 11, per_block)
    arrivals = jnp.concatenate([arrivals[:4], arrivals[5:]], axis=0).reshape(8 * CAP, 11, per_block)
    received = jnp.concatenate([own_rows, arrivals], axis=0)
    total_slots = received.shape[0]
    blocks_per_step = 8
    step_count = total_slots // blocks_per_step
    grouped = received.reshape(step_count, blocks_per_step, 11, per_block)
    planar_cells = (width_x + 2) * (width_y + 2)

    def deposit(deposited, block_group):
        flattened = jnp.moveaxis(block_group, 1, 0).reshape(11, blocks_per_step * per_block)
        planar, table_z = tables(flattened, width_x, width_y, column_depth)
        forces = flattened[0:3] * flattened[10][None, :]
        slabs = [
            lax.dot_general(
                planar * forces[component][None, :],
                table_z,
                (((1,), (1,)), ((), ())),
                precision=HIGHEST,
            )
            for component in range(3)
        ]
        return (deposited + jnp.stack(slabs), None)

    deposited, _ = lax.scan(
        deposit, jnp.zeros((3, planar_cells, column_depth), jnp.float32), grouped
    )
    deposited = deposited.reshape(3, width_x + 2, width_y + 2, column_depth)
    halo_sum = with_halo(deposited, (("tx", 1), ("ty", 2)), 1)
    source = halo_sum[:, 2 : width_x + 2, 2 : width_y + 2]
    source = source.at[:, 0].add(halo_sum[:, 0, 2 : width_y + 2])
    source = source.at[:, -1].add(halo_sum[:, width_x + 3, 2 : width_y + 2])
    source = source.at[:, :, 0].add(halo_sum[:, 2 : width_x + 2, 0])
    source = source.at[:, :, -1].add(halo_sum[:, 2 : width_x + 2, width_y + 3])
    source = source.at[:, 0, 0].add(halo_sum[:, 0, 0])
    source = source.at[:, 0, -1].add(halo_sum[:, 0, width_y + 3])
    source = source.at[:, -1, 0].add(halo_sum[:, width_x + 3, 0])
    source = source.at[:, -1, -1].add(halo_sum[:, width_x + 3, width_y + 3])
    widened = with_halo(jnp.concatenate([source, gas], axis=0), (("tx", 1), ("ty", 2)), SWEEPS + 1)
    filtered = widened[:3]
    for sweep in range(SWEEPS):
        margin_cut = sweep + 1
        filtered = relax(filtered, widened[:3, margin_cut:-margin_cut, margin_cut:-margin_cut])
    gas_ext = widened[3:, SWEEPS:-SWEEPS, SWEEPS:-SWEEPS] + STEP_SIZE * filtered
    gas_new = gas_ext[:, 1:-1, 1:-1]
    field_ext = gas_ext.reshape(3, planar_cells, column_depth)

    def resample(carried, block_group):
        flattened = jnp.moveaxis(block_group, 1, 0).reshape(11, blocks_per_step * per_block)
        planar, table_z = tables(flattened, width_x, width_y, column_depth)
        values = []
        for component in range(3):
            column = lax.dot_general(
                field_ext[component], planar, (((0,), (0,)), ((), ())), precision=HIGHEST
            )
            values.append(jnp.sum(column * table_z, axis=0))
        slip_group = (jnp.stack(values) - flattened[3:6]) * flattened[10][None, :]
        return (carried, jnp.moveaxis(slip_group.reshape(3, blocks_per_step, per_block), 0, 1))

    _, slip_steps = lax.scan(resample, None, grouped)
    slip = slip_steps.reshape(1, 1, total_slots, 3, per_block)
    return (gas_new, slip)


def solution(mesh):
    return jax.shard_map(
        on_device,
        mesh=mesh,
        in_specs=(
            P("tx", "ty", None, None),
            P("tx", "ty", None, None),
            P("tx", "ty", None, None, None),
            P("tx", "ty", None, None, None),
            P("tx", "ty", None, None, None),
            P(None, "tx", "ty", None),
        ),
        out_specs=(P(None, "tx", "ty", None), P("tx", "ty", None, None, None)),
        check_vma=False,
    )
```

profile of v0, /device:TPU:0, one launch (start us, length us, event | category | flops | bytes accessed | tf_op | source)
XLA Modules:
  0.0 161.2 jit_solution(12575052620377164309)
XLA Ops:
  4.1 0.9 copy.56
  5.7 1.0 copy_bitcast_fusion
  9.8 2.8 %collective-permute-start.2 = (f32[5,1,2,11,128]{4,3,2,1,0:T(8,128)S(1)}, f32[5,1,2,11,128]{4,3,2,1,0:T(8,128)S(1)}, u32[]{:S(2)}, u32[]{:S(2)}) collective-permute-start(f32[5,1,2,11,128]{4,3,2,1,0:T(8,128)S(1)} %get-tuple-element.473), channel_id=1, source_target_pairs={{0,1},{1,2},{2,3},{3,4},{4,5},{5,6},{6,7},{7,8},{8,9},{9,10},{10,1... | collective-permute-start | bytes 168968 | tf_op jit(solution)/shard_map/ppermute | solution.py:21
  12.6 4.1 %collective-permute-start.3 = (f32[5,1,2,11,128]{4,3,2,1,0:T(8,128)S(1)}, f32[5,1,2,11,128]{4,3,2,1,0:T(8,128)S(1)}, u32[]{:S(2)}, u32[]{:S(2)}) collective-permute-start(f32[5,1,2,11,128]{4,3,2,1,0:T(8,128)S(1)} %get-tuple-element.474), channel_id=1, source_target_pairs={{1,0},{2,1},{3,2},{4,3},{5,4},{6,5},{7,6},{8,7},{9,8},{10,9},{11,1... | collective-permute-start | bytes 168968 | tf_op jit(solution)/shard_map/ppermute | solution.py:24
  17.4 2.1 %collective-permute-done.2 = f32[5,1,2,11,128]{4,3,2,1,0:T(8,128)S(1)} collective-permute-done((f32[5,1,2,11,128]{4,3,2,1,0:T(8,128)S(1)}, f32[5,1,2,11,128]{4,3,2,1,0:T(8,128)S(1)}, u32[]{:S(2)}, u32[]{:S(2)}) %collective-permute-start.2) | collective-permute-done | bytes 56352 | tf_op jit(solution)/shard_map/ppermute | solution.py:21
  19.8 45.5 %while.40 = (s32[]{:T(128)}, f32[3,324,128]{2,1,0:T(8,128)}, f32[8,8,11,128]{3,1,2,0:T(8,128)S(1)}, s32[]{:T(128)}, s32[]{:T(128)}) while((s32[]{:T(128)}, f32[3,324,128]{2,1,0:T(8,128)}, f32[8,8,11,128]{3,1,2,0:T(8,128)S(1)}, s32[]{:T(128)}, s32[]{:T(128)}) %tuple.186), condition=%wide.region_5.6_spmd.clone, body=%wide.region_4.5_spmd.clone.sunk | while | flops 1534203904 | bytes 14651523 | solution.py:123
  20.4 1.4 fusion.163
  21.8 1.4 fusion.162
  23.2 1.4 fusion.161
  26.1 1.4 fusion.163
  27.5 1.4 fusion.162
  28.9 1.4 fusion.161
  31.8 1.4 fusion.163
  33.2 1.4 fusion.162
  34.6 1.4 fusion.161
  37.5 1.4 fusion.163
  38.9 1.4 fusion.162
  40.2 1.4 fusion.161
  43.2 1.4 fusion.163
  44.6 1.4 fusion.162
  45.9 1.4 fusion.161
  48.9 1.4 fusion.163
  50.3 1.4 fusion.162
  51.6 1.4 fusion.161
  54.6 1.4 fusion.163
  55.9 1.4 fusion.162
  57.3 1.4 fusion.161
  60.3 1.4 fusion.163
  61.6 1.4 fusion.162
  63.0 1.4 fusion.161
  65.3 1.1 reshape.1448
  69.0 5.3 %collective-permute-start.7 = (f32[3,20,1,128]{3,2,1,0:T(1,128)S(1)}, f32[3,20,1,128]{3,2,1,0:T(1,128)S(1)}, u32[]{:S(2)}, u32[]{:S(2)}) collective-permute-start(f32[3,20,1,128]{3,2,1,0:T(1,128)S(1)} %get-tuple-element.469), channel_id=1, source_target_pairs={{1,0},{2,1},{3,2},{4,3},{5,4},{6,5},{7,6},{8,7},{9,8},{10,9},{11,1... | collective-permute-start | bytes 92168 | tf_op jit(solution)/shard_map/ppermute | solution.py:24
  74.3 1.8 %collective-permute-done.6 = f32[3,20,1,128]{3,2,1,0:T(1,128)S(1)} collective-permute-done((f32[3,20,1,128]{3,2,1,0:T(1,128)S(1)}, f32[3,20,1,128]{3,2,1,0:T(1,128)S(1)}, u32[]{:S(2)}, u32[]{:S(2)}) %collective-permute-start.6) | collective-permute-done | bytes 30752 | tf_op jit(solution)/shard_map/ppermute | solution.py:21
  76.6 1.9 %broadcast_select_fusion = f32[3,1,1,128]{3,2,1,0:T(1,128)S(1)} fusion(pred[]{:T(512)} %and_reduce_fusion, f32[3,20,1,128]{3,2,1,0:T(1,128)S(1)} %collective-permute-done.7, f32[3,16,16,128]{3,2,1,0:T(8,128)S(1)} %scatter-add.34, s32[]{:T(128)} %bitcast.38, s32[]{:T(128)} %bitcast.39), kind=kLoop, calls=%fused_computation.253 | loop fusion | flops 768 | bytes 4617 | tf_op jit(solution)/shard_map/select.13
  78.5 1.3 scatter-add.35
  80.6 1.0 collective-permute-done.8
  82.4 5.8 %collective-permute-start.11 = (f32[6,26,5,128]{3,1,2,0:T(8,128)S(1)}, f32[6,26,5,128]{3,1,2,0:T(8,128)}, u32[]{:S(2)}, u32[]{:S(2)}) collective-permute-start(f32[6,26,5,128]{3,1,2,0:T(8,128)S(1)} %copy.43), channel_id=1, source_target_pairs={{1,0},{2,1},{3,2},{4,3},{5,4},{6,5},{7,6},{8,7},{9,8},{10,9},{11,1... | collective-permute-start | bytes 1198088 | tf_op jit(solution)/shard_map/ppermute | solution.py:24
  88.2 15.7 %collective-permute-done.10 = f32[6,26,5,128]{3,1,2,0:T(8,128)S(1)} collective-permute-done((f32[6,26,5,128]{3,1,2,0:T(8,128)S(1)}, f32[6,26,5,128]{3,1,2,0:T(8,128)S(1)}, u32[]{:S(2)}, u32[]{:S(2)}) %collective-permute-start.10) | collective-permute-done | bytes 399392 | tf_op jit(solution)/shard_map/ppermute | solution.py:21
  104.2 1.3 copy.45
  112.7 48.5 %while.39 = (s32[]{:T(128)}, f32[8,8,3,128]{3,1,0,2:T(8,128)}, f32[8,8,11,128]{3,1,2,0:T(8,128)S(1)}, f32[3,324,128]{2,1,0:T(8,128)}, s32[]{:T(128)}) while((s32[]{:T(128)}, f32[8,8,3,128]{3,1,0,2:T(8,128)}, f32[8,8,11,128]{3,1,2,0:T(8,128)S(1)}, f32[3,324,128]{2,1,0:T(8,128)}, s32[]{:T(128)}) %tuple.192), condition=%wide.region_11.12_spmd, body=%wide.region_7.11_spmd.sunk | while | flops 1533503488 | bytes 11170397 | solution.py:158
  113.3 2.3 %fusion.155 = f32[1024]{0:T(1024)S(1)} fusion(f32[324,1024]{1,0:T(8,128)S(1)} %mul.706, f32[1024]{0:T(1024)S(1)} %get-tuple-element.581, s32[1024]{0:T(1024)S(1)} %add_select_fusion.23, f32[1024]{0:T(1024)S(1)} %get-tuple-element.583, s32[1024]{0:T(1024)S(1)} %get-tuple-element.582, f32[1024]{0:T(1024)S(1)} %get-tuple-element.584, ...), kind=kOutput, calls=%fused_computation.7.clone.1 | convolution fusion | flops 510917632 | bytes 1523712 | tf_op jit(solution)/shard_map/while/body/eval_jaxpr/dot_general | solution.py:151
  115.6 1.3 fusion.154
  116.9 1.3 fusion.153
  119.4 2.3 %fusion.155 = f32[1024]{0:T(1024)S(1)} fusion(f32[324,1024]{1,0:T(8,128)S(1)} %mul.706, f32[1024]{0:T(1024)S(1)} %get-tuple-element.581, s32[1024]{0:T(1024)S(1)} %add_select_fusion.23, f32[1024]{0:T(1024)S(1)} %get-tuple-element.583, s32[1024]{0:T(1024)S(1)} %get-tuple-element.582, f32[1024]{0:T(1024)S(1)} %get-tuple-element.584, ...), kind=kOutput, calls=%fused_computation.7.clone.1 | convolution fusion | flops 510917632 | bytes 1523712 | tf_op jit(solution)/shard_map/while/body/eval_jaxpr/dot_general | solution.py:151
  121.6 1.3 fusion.154
  122.9 1.3 fusion.153
  125.4 2.3 %fusion.155 = f32[1024]{0:T(1024)S(1)} fusion(f32[324,1024]{1,0:T(8,128)S(1)} %mul.706, f32[1024]{0:T(1024)S(1)} %get-tuple-element.581, s32[1024]{0:T(1024)S(1)} %add_select_fusion.23, f32[1024]{0:T(1024)S(1)} %get-tuple-element.583, s32[1024]{0:T(1024)S(1)} %get-tuple-element.582, f32[1024]{0:T(1024)S(1)} %get-tuple-element.584, ...), kind=kOutput, calls=%fused_computation.7.clone.1 | convolution fusion | flops 510917632 | bytes 1523712 | tf_op jit(solution)/shard_map/while/body/eval_jaxpr/dot_general | solution.py:151
  127.7 1.3 fusion.154
  129.0 1.3 fusion.153
  131.5 2.3 %fusion.155 = f32[1024]{0:T(1024)S(1)} fusion(f32[324,1024]{1,0:T(8,128)S(1)} %mul.706, f32[1024]{0:T(1024)S(1)} %get-tuple-element.581, s32[1024]{0:T(1024)S(1)} %add_select_fusion.23, f32[1024]{0:T(1024)S(1)} %get-tuple-element.583, s32[1024]{0:T(1024)S(1)} %get-tuple-element.582, f32[1024]{0:T(1024)S(1)} %get-tuple-element.584, ...), kind=kOutput, calls=%fused_computation.7.clone.1 | convolution fusion | flops 510917632 | bytes 1523712 | tf_op jit(solution)/shard_map/while/body/eval_jaxpr/dot_general | solution.py:151
  133.8 1.3 fusion.154
  135.1 1.3 fusion.153
  137.6 2.3 %fusion.155 = f32[1024]{0:T(1024)S(1)} fusion(f32[324,1024]{1,0:T(8,128)S(1)} %mul.706, f32[1024]{0:T(1024)S(1)} %get-tuple-element.581, s32[1024]{0:T(1024)S(1)} %add_select_fusion.23, f32[1024]{0:T(1024)S(1)} %get-tuple-element.583, s32[1024]{0:T(1024)S(1)} %get-tuple-element.582, f32[1024]{0:T(1024)S(1)} %get-tuple-element.584, ...), kind=kOutput, calls=%fused_computation.7.clone.1 | convolution fusion | flops 510917632 | bytes 1523712 | tf_op jit(solution)/shard_map/while/body/eval_jaxpr/dot_general | solution.py:151
  139.8 1.3 fusion.154
  141.1 1.3 fusion.153
  143.6 2.3 %fusion.155 = f32[1024]{0:T(1024)S(1)} fusion(f32[324,1024]{1,0:T(8,128)S(1)} %mul.706, f32[1024]{0:T(1024)S(1)} %get-tuple-element.581, s32[1024]{0:T(1024)S(1)} %add_select_fusion.23, f32[1024]{0:T(1024)S(1)} %get-tuple-element.583, s32[1024]{0:T(1024)S(1)} %get-tuple-element.582, f32[1024]{0:T(1024)S(1)} %get-tuple-element.584, ...), kind=kOutput, calls=%fused_computation.7.clone.1 | convolution fusion | flops 510917632 | bytes 1523712 | tf_op jit(solution)/shard_map/while/body/eval_jaxpr/dot_general | solution.py:151
  145.9 1.3 fusion.154
  147.2 1.3 fusion.153
  149.7 2.3 %fusion.155 = f32[1024]{0:T(1024)S(1)} fusion(f32[324,1024]{1,0:T(8,128)S(1)} %mul.706, f32[1024]{0:T(1024)S(1)} %get-tuple-element.581, s32[1024]{0:T(1024)S(1)} %add_select_fusion.23, f32[1024]{0:T(1024)S(1)} %get-tuple-element.583, s32[1024]{0:T(1024)S(1)} %get-tuple-element.582, f32[1024]{0:T(1024)S(1)} %get-tuple-element.584, ...), kind=kOutput, calls=%fused_computation.7.clone.1 | convolution fusion | flops 510917632 | bytes 1523712 | tf_op jit(solution)/shard_map/while/body/eval_jaxpr/dot_general | solution.py:151
  151.9 1.3 fusion.154
  153.2 1.3 fusion.153
  155.7 2.3 %fusion.155 = f32[1024]{0:T(1024)S(1)} fusion(f32[324,1024]{1,0:T(8,128)S(1)} %mul.706, f32[1024]{0:T(1024)S(1)} %get-tuple-element.581, s32[1024]{0:T(1024)S(1)} %add_select_fusion.23, f32[1024]{0:T(1024)S(1)} %get-tuple-element.583, s32[1024]{0:T(1024)S(1)} %get-tuple-element.582, f32[1024]{0:T(1024)S(1)} %get-tuple-element.584, ...), kind=kOutput, calls=%fused_computation.7.clone.1 | convolution fusion | flops 510917632 | bytes 1523712 | tf_op jit(solution)/shard_map/while/body/eval_jaxpr/dot_general | solution.py:151
  158.0 1.3 fusion.154
  159.3 1.3 fusion.153
  (344 shorter events, 40.9 us)
Async XLA Ops:
  0.6 8.2 %copy-start.4 = (s32[1,1,48,1]{2,3,1,0:T(1,128)S(1)}, s32[1,1,48,1]{2,3,1,0:T(1,128)}, u32[]{:S(2)}) copy-start(s32[1,1,48,1]{2,3,1,0:T(1,128)} %param.26) | copy-start | bytes 580
  6.7 10.0 %copy-start.5 = (s32[4]{0:T(128)S(1)}, s32[4]{0:T(128)}, u32[]{:S(2)}) copy-start(s32[4]{0:T(128)} %constant.672.clone.1) | copy-start | bytes 52
  8.0 1.6 %collective-permute-start = (f32[1,3,2,11,128]{4,3,2,1,0:T(8,128)S(1)}, f32[1,3,2,11,128]{4,3,2,1,0:T(8,128)S(1)}, u32[]{:S(2)}, u32[]{:S(2)}) collective-permute-start(f32[1,3,2,11,128]{4,3,2,1,0:T(8,128)S(1)} %bitcast.229), channel_id=1, source_target_pairs={{0,16},{16,0},{1,17},{17,1},{2,18},{18,2},{3,19},{19,3},{4,20},{20... | collective-permute-start | bytes 101384 | tf_op jit(solution)/shard_map/ppermute | solution.py:21
  8.5 1.2 collective-permute-start.1
  9.8 9.7 %collective-permute-start.2 = (f32[5,1,2,11,128]{4,3,2,1,0:T(8,128)S(1)}, f32[5,1,2,11,128]{4,3,2,1,0:T(8,128)S(1)}, u32[]{:S(2)}, u32[]{:S(2)}) collective-permute-start(f32[5,1,2,11,128]{4,3,2,1,0:T(8,128)S(1)} %get-tuple-element.473), channel_id=1, source_target_pairs={{0,1},{1,2},{2,3},{3,4},{4,5},{5,6},{6,7},{7,8},{8,9},{9,10},{10,1... | collective-permute-start | bytes 168968 | tf_op jit(solution)/shard_map/ppermute | solution.py:21
  12.6 6.9 %collective-permute-start.3 = (f32[5,1,2,11,128]{4,3,2,1,0:T(8,128)S(1)}, f32[5,1,2,11,128]{4,3,2,1,0:T(8,128)S(1)}, u32[]{:S(2)}, u32[]{:S(2)}) collective-permute-start(f32[5,1,2,11,128]{4,3,2,1,0:T(8,128)S(1)} %get-tuple-element.474), channel_id=1, source_target_pairs={{1,0},{2,1},{3,2},{4,3},{5,4},{6,5},{7,6},{8,7},{9,8},{10,9},{11,1... | collective-permute-start | bytes 168968 | tf_op jit(solution)/shard_map/ppermute | solution.py:24
  23.2 1.4 copy-start
  24.7 0.8 copy-start.1
  28.9 1.4 copy-start
  30.4 0.8 copy-start.1
  34.5 1.4 copy-start
  36.1 0.8 copy-start.1
  40.2 1.4 copy-start
  41.8 0.8 copy-start.1
  45.9 1.4 copy-start
  47.5 0.8 copy-start.1
  51.6 1.4 copy-start
  53.2 0.8 copy-start.1
  57.3 1.4 copy-start
  58.9 0.8 copy-start.1
  63.0 1.4 copy-start
  64.5 0.8 copy-start.1
  66.4 1.3 collective-permute-start.4
  67.1 12.8 %copy-start.2 = (f32[3,16,16,128]{3,2,1,0:T(8,128)S(1)}, f32[3,16,16,128]{3,2,1,0:T(8,128)}, u32[]{:S(2)}) copy-start(f32[3,16,16,128]{3,2,1,0:T(8,128)} %param.31) | copy-start | bytes 1179652
  67.1 1.4 collective-permute-start.5
  68.6 7.5 %collective-permute-start.6 = (f32[3,20,1,128]{3,2,1,0:T(1,128)S(1)}, f32[3,20,1,128]{3,2,1,0:T(1,128)S(1)}, u32[]{:S(2)}, u32[]{:S(2)}) collective-permute-start(f32[3,20,1,128]{3,2,1,0:T(1,128)S(1)} %get-tuple-element.470), channel_id=1, source_target_pairs={{0,1},{1,2},{2,3},{3,4},{4,5},{5,6},{6,7},{7,8},{8,9},{9,10},{10,1... | collective-permute-start | bytes 92168 | tf_op jit(solution)/shard_map/ppermute | solution.py:21
  69.0 7.3 %collective-permute-start.7 = (f32[3,20,1,128]{3,2,1,0:T(1,128)S(1)}, f32[3,20,1,128]{3,2,1,0:T(1,128)S(1)}, u32[]{:S(2)}, u32[]{:S(2)}) collective-permute-start(f32[3,20,1,128]{3,2,1,0:T(1,128)S(1)} %get-tuple-element.469), channel_id=1, source_target_pairs={{1,0},{2,1},{3,2},{4,3},{5,4},{6,5},{7,6},{8,7},{9,8},{10,9},{11,1... | collective-permute-start | bytes 92168 | tf_op jit(solution)/shard_map/ppermute | solution.py:24
  80.0 1.6 collective-permute-start.8
  80.1 1.9 %collective-permute-start.9 = (f32[6,5,16,128]{3,2,1,0:T(8,128)S(1)}, f32[6,5,16,128]{3,2,1,0:T(8,128)S(1)}, u32[]{:S(2)}, u32[]{:S(2)}) collective-permute-start(f32[6,5,16,128]{3,2,1,0:T(8,128)S(1)} %get-tuple-element.464), channel_id=1, source_target_pairs={{16,0},{0,16},{17,1},{1,17},{18,2},{2,18},{19,3},{3,19},{20,4},{4,... | collective-permute-start | bytes 737288 | tf_op jit(solution)/shard_map/ppermute | solution.py:24
  82.2 21.7 %collective-permute-start.10 = (f32[6,26,5,128]{3,1,2,0:T(8,128)S(1)}, f32[6,26,5,128]{3,1,2,0:T(8,128)S(1)}, u32[]{:S(2)}, u32[]{:S(2)}) collective-permute-start(f32[6,26,5,128]{3,1,2,0:T(8,128)S(1)} %copy.42), channel_id=1, source_target_pairs={{0,1},{1,2},{2,3},{3,4},{4,5},{5,6},{6,7},{7,8},{8,9},{9,10},{10,1... | collective-permute-start | bytes 1198088 | tf_op jit(solution)/shard_map/ppermute | solution.py:21
  82.4 21.8 %collective-permute-start.11 = (f32[6,26,5,128]{3,1,2,0:T(8,128)S(1)}, f32[6,26,5,128]{3,1,2,0:T(8,128)}, u32[]{:S(2)}, u32[]{:S(2)}) collective-permute-start(f32[6,26,5,128]{3,1,2,0:T(8,128)S(1)} %copy.43), channel_id=1, source_target_pairs={{1,0},{2,1},{3,2},{4,3},{5,4},{6,5},{7,6},{8,7},{9,8},{10,9},{11,1... | collective-permute-start | bytes 1198088 | tf_op jit(solution)/shard_map/ppermute | solution.py:24
  113.3 2.3 %copy-start.3 = (f32[3,324,128]{2,1,0:T(8,128)S(1)}, f32[3,324,128]{2,1,0:T(8,128)}, u32[]{:S(2)}) copy-start(f32[3,324,128]{2,1,0:T(8,128)} %get-tuple-element.641) | copy-start | bytes 1492996 | tf_op jit(solution)/shard_map/while
  119.3 2.3 %copy-start.3 = (f32[3,324,128]{2,1,0:T(8,128)S(1)}, f32[3,324,128]{2,1,0:T(8,128)}, u32[]{:S(2)}) copy-start(f32[3,324,128]{2,1,0:T(8,128)} %get-tuple-element.641) | copy-start | bytes 1492996 | tf_op jit(solution)/shard_map/while
  125.4 2.3 %copy-start.3 = (f32[3,324,128]{2,1,0:T(8,128)S(1)}, f32[3,324,128]{2,1,0:T(8,128)}, u32[]{:S(2)}) copy-start(f32[3,324,128]{2,1,0:T(8,128)} %get-tuple-element.641) | copy-start | bytes 1492996 | tf_op jit(solution)/shard_map/while
  131.5 2.3 %copy-start.3 = (f32[3,324,128]{2,1,0:T(8,128)S(1)}, f32[3,324,128]{2,1,0:T(8,128)}, u32[]{:S(2)}) copy-start(f32[3,324,128]{2,1,0:T(8,128)} %get-tuple-element.641) | copy-start | bytes 1492996 | tf_op jit(solution)/shard_map/while
  137.5 2.3 %copy-start.3 = (f32[3,324,128]{2,1,0:T(8,128)S(1)}, f32[3,324,128]{2,1,0:T(8,128)}, u32[]{:S(2)}) copy-start(f32[3,324,128]{2,1,0:T(8,128)} %get-tuple-element.641) | copy-start | bytes 1492996 | tf_op jit(solution)/shard_map/while
  143.6 2.3 %copy-start.3 = (f32[3,324,128]{2,1,0:T(8,128)S(1)}, f32[3,324,128]{2,1,0:T(8,128)}, u32[]{:S(2)}) copy-start(f32[3,324,128]{2,1,0:T(8,128)} %get-tuple-element.641) | copy-start | bytes 1492996 | tf_op jit(solution)/shard_map/while
  149.6 2.3 %copy-start.3 = (f32[3,324,128]{2,1,0:T(8,128)S(1)}, f32[3,324,128]{2,1,0:T(8,128)}, u32[]{:S(2)}) copy-start(f32[3,324,128]{2,1,0:T(8,128)} %get-tuple-element.641) | copy-start | bytes 1492996 | tf_op jit(solution)/shard_map/while
  155.7 2.3 %copy-start.3 = (f32[3,324,128]{2,1,0:T(8,128)S(1)}, f32[3,324,128]{2,1,0:T(8,128)}, u32[]{:S(2)}) copy-start(f32[3,324,128]{2,1,0:T(8,128)} %get-tuple-element.641) | copy-start | bytes 1492996 | tf_op jit(solution)/shard_map/while
where the time goes:
time: 163 us; the launch traced here: 161 us
  matrix products  71.3 us (44%)
  local copies, waits for them, and re-layouts  22.5 us (14%)
  other arithmetic  22.2 us (14%)
  waiting for transfers between devices  22 us (13%)
  starting transfers between devices  20.3 us (12%)
  loops' own time  1.81 us (1%)
    dot_general x24, matrix products, resample(): lax.dot_general(field_ext[component], planar, (((0,), (0,)), ((), ())), p...  38.7 us
    dot_general x24, matrix products, deposit(): lax.dot_general(planar * forces[component][None, :], table_z, (((1,), (1,...  32.6 us
    ppermute x6, waiting for transfers between devices, with_halo(): lax.ppermute(lax.slice_in_dim(block, block.shape[dim] - width, None, axis...  20.7 us
    ppermute x6, starting transfers between devices, with_halo(): lax.ppermute(lax.slice_in_dim(block, 0, width, axis=dim), axis, backward)  16.3 us
    while x56, local copies, waits for them, and re-layouts  6.42 us
    dynamic_update_slice x8, other arithmetic, on_device(): _, slip_steps = lax.scan(resample, None, grouped)  4.9 us
    ppermute x6, starting transfers between devices, with_halo(): lax.ppermute(lax.slice_in_dim(block, block.shape[dim] - width, None, axis...  3.99 us
  transfers between devices with their start and end apart: 12, of which 8 were waited for; matrix products, arithmetic and copies ran while one was open for 2% of the time, Pallas kernels for 0%

commit v1 on v0

v1 whole, which is shorter than its diff:
```python
import functools

import jax
import jax.numpy as jnp
from jax import lax
from jax.experimental import pallas as pl
from jax.experimental.pallas import tpu as pltpu
from jax.sharding import PartitionSpec as P

SWEEPS = 4
CAP = 2
DIFFUSE = 1.0
STEP_SIZE = 2.0

REC = 16
STAY = 4
REACH = SWEEPS + 1
EDGE = REACH + 1
SUB = 8
VMEM = pl.BlockSpec(memory_space=pltpu.VMEM)
SMEM = pl.BlockSpec(memory_space=pltpu.SMEM)


def round_up(count, unit):
    return -(-count // unit) * unit


def call(body, outs, args, specs=None, scratch=(), aliases=None, cost=(0, 0), name=None):
    return pl.pallas_call(
        body,
        out_shape=[jax.ShapeDtypeStruct(shape, jnp.float32) for shape in outs],
        in_specs=specs or [VMEM] * len(args),
        out_specs=[VMEM] * len(outs),
        scratch_shapes=list(scratch),
        input_output_aliases=aliases or {},
        cost_estimate=pl.CostEstimate(flops=cost[0], bytes_accessed=cost[1], transcendentals=0),
        name=name,
    )(*args)


def split_by(value, size):
    if size & (size - 1) == 0:
        return value >> (size.bit_length() - 1), value & (size - 1)
    return value // size, value % size


class Tile:
    def __init__(self, wx, wy, nz):
        self.wx, self.wy, self.nz = wx, wy, nz
        self.ye = wy + 2
        self.hp = round_up(self.ye, SUB)
        self.main = self.ye * wx
        self.rows = self.main + 2 * self.hp
        self.yw = wy + 2 * REACH
        self.yp = round_up(self.yw, SUB)
        self.edge_main = EDGE * wx
        self.edge_rows = round_up(3 * (self.edge_main + 2 * EDGE), SUB)

    def decode(self, cell):
        cx, rest = split_by(cell, self.wy * self.nz)
        cy, cz = split_by(rest, self.nz)
        return cx, cy, cz

    def planar(self, cx, cy, weights):
        low, mid, high = weights
        lanes = cx.shape[1]
        ix = lax.broadcasted_iota(jnp.int32, (self.wx, lanes), 0)
        tx = jnp.where(ix == cx + 1, high[0:1], 0.0)
        tx = jnp.where(ix == cx, mid[0:1], tx)
        tx = jnp.where(ix == cx - 1, low[0:1], tx)
        iy = lax.broadcasted_iota(jnp.int32, (self.hp, lanes), 0)
        ty = jnp.where(iy == cy + 2, high[1:2], 0.0)
        ty = jnp.where(iy == cy + 1, mid[1:2], ty)
        ty = jnp.where(iy == cy, low[1:2], ty)
        beyond_low = jnp.where(cx == 0, low[0:1], 0.0)
        beyond_high = jnp.where(cx == self.wx - 1, high[0:1], 0.0)
        parts = [tx * ty[j : j + 1] for j in range(self.ye)]
        return parts + [ty * beyond_low, ty * beyond_high]

    def vertical(self, cz, weights):
        low, mid, high = weights
        iz = lax.broadcasted_iota(jnp.int32, (self.nz, cz.shape[1]), 0)
        below = jnp.where(cz == 0, self.nz - 1, cz - 1)
        above = jnp.where(cz == self.nz - 1, 0, cz + 1)
        tz = jnp.where(iz == above, high[2:3], 0.0)
        tz = jnp.where(iz == cz, mid[2:3], tz)
        return jnp.where(iz == below, low[2:3], tz)


def tsc_weights(sixteenths):
    fraction = (sixteenths + 0.5) * (1.0 / 16.0) - 0.5
    low = 0.5 - fraction
    high = 0.5 + fraction
    return 0.5 * low * low, 0.75 - fraction * fraction, 0.5 * high * high


def halves(value):
    top = value.astype(jnp.bfloat16)
    return top, (value - top.astype(jnp.float32)).astype(jnp.bfloat16)


def deposit_chunk(tile, blocks):
    left, right = [], []
    for cell, sixteenths, force in blocks:
        cx, cy, cz = tile.decode(cell)
        weights = tsc_weights(sixteenths)
        tops, lows = zip(*[halves(part) for part in tile.planar(cx, cy, weights)])
        left.append((jnp.concatenate(tops, axis=0), jnp.concatenate(lows, axis=0)))
        tz = tile.vertical(cz, weights)
        tops, lows = zip(*[halves(tz * force[k : k + 1]) for k in range(3)])
        right.append((jnp.concatenate(tops, axis=0), jnp.concatenate(lows, axis=0)))
    a_top, a_low = (jnp.concatenate(part, axis=1) for part in zip(*left))
    b_top, b_low = (jnp.concatenate(part, axis=1) for part in zip(*right))
    return lax.dot_general(
        jnp.concatenate([a_top, a_top, a_low], axis=1),
        jnp.concatenate([b_top, b_low, b_top], axis=1),
        (((1,), (1,)), ((), ())),
        preferred_element_type=jnp.float32,
    )


def ty_roles(axis, count):
    if count % 2:
        return True, False
    even = lax.axis_index(axis) % 2 == 0
    return even, even


def if_(cond, then, other):
    if isinstance(cond, bool):
        (then if cond else other)()
        return
    pl.when(cond)(then)
    pl.when(jnp.logical_not(cond))(other)


def pack_kernel(tile, slots, codes, cells, offsets, drag, velocity, gas, xsend, own, counts):
    xsend[:, : 3 * CAP] = jnp.zeros((2, 3 * CAP, REC, 128), jnp.float32)
    own[...] = jnp.zeros(own.shape, jnp.float32)
    for code in range(9):
        counts[code] = 0
    per = tile.wy // REC
    for k in range(3):
        for side, x in ((0, 0), (1, tile.wx - 1)):
            for part in range(per):
                start = (k * tile.wx + x) * tile.wy + part * REC
                xsend[side, 3 * CAP + k * per + part] = gas[start : start + REC]

    def visit(slot, carry):
        code = codes[slot]

        @pl.when(code != STAY)
        def _():
            rank = jnp.minimum(counts[code], CAP - 1)
            counts[code] = rank + 1

            def put(ref, side, place):
                ref[side, place, 0:3] = drag[slot]
                ref[side, place, 3:6] = velocity[slot]
                ref[side, place, 6:7] = cells[pl.ds(slot, 1)].astype(jnp.float32)
                ref[side, place, 7:10] = offsets[slot].astype(jnp.float32)
                ref[side, place, 10:11] = jnp.ones((1, 128), jnp.float32)

            step_x, step_y = code // 3, code % 3
            pl.when(step_x == 1)(lambda: put(own, step_y // 2, rank))
            pl.when(step_x != 1)(lambda: put(xsend, step_x // 2, step_y * CAP + rank))

        return carry

    lax.fori_loop(0, slots, visit, 0)


def join_kernel(tile, axis, count, xrecv, own, gas, send_a, send_b):
    a_high, _ = ty_roles(axis, count)
    per_x, per_y = tile.wx // REC, tile.wy // REC

    def fill(ref, high):
        step = 2 * CAP * int(high)
        y = tile.wy - 1 if high else 0
        for s in range(CAP):
            ref[s] = xrecv[1, step + s]
            ref[CAP + s] = own[int(high), s]
            ref[2 * CAP + s] = xrecv[0, step + s]
        for k in range(3):
            for part in range(per_x):
                start = (k * tile.wx + part * REC) * tile.wy + y
                ref[3 * CAP + k * per_x + part] = gas[pl.ds(start, REC, stride=tile.wy), :]
            place = 3 * CAP + k * per_y + y // REC
            corner = 3 * CAP + 3 * per_x
            ref[corner, 2 * k : 2 * k + 1] = xrecv[1, place, y % REC : y % REC + 1]
            ref[corner, 2 * k + 1 : 2 * k + 2] = xrecv[0, place, y % REC : y % REC + 1]

    def even():
        fill(send_a, True)
        fill(send_b, False)

    def odd():
        fill(send_a, False)
        fill(send_b, True)

    for ref in (send_a, send_b):
        ref[3 * CAP + 3 * per_x] = jnp.zeros((REC, 128), jnp.float32)
    if_(a_high, even, odd)


def own_kernel(tile, slots, codes, cells, offsets, drag, acc):
    acc[...] = jnp.zeros(acc.shape, jnp.float32)

    def step(pair, carry):
        blocks = []
        for i in range(2):
            slot = pair * 2 + i
            stays = (codes[slot] == STAY).astype(jnp.float32)
            blocks.append(
                (
                    cells[pl.ds(slot, 1)],
                    offsets[slot].astype(jnp.float32),
                    drag[slot] * stays,
                )
            )
        acc[...] += deposit_chunk(tile, blocks)
        return carry

    lax.fori_loop(0, slots // 2, step, 0)


ARRIVAL_LOW, ARRIVAL_HIGH = (0, 3, 5), (2, 4, 7)


def arrive_kernel(tile, axis, count, recv_a, recv_b, xrecv, acc_in, acc, arrivals, send_a, send_b):
    a_high, a_from_high = ty_roles(axis, count)
    for s in range(CAP):
        arrivals[1 * CAP + s] = xrecv[1, CAP + s]
        arrivals[6 * CAP + s] = xrecv[0, CAP + s]

    def place(ref, order):
        for i, j in enumerate(order):
            for s in range(CAP):
                arrivals[j * CAP + s] = ref[i * CAP + s]

    if_(
        a_from_high,
        lambda: (place(recv_a, ARRIVAL_HIGH), place(recv_b, ARRIVAL_LOW)) and None,
        lambda: (place(recv_a, ARRIVAL_LOW), place(recv_b, ARRIVAL_HIGH)) and None,
    )
    acc[...] = acc_in[...]

    def step(pair, carry):
        blocks = []
        for i in range(2):
            record = arrivals[pair * 2 + i]
            blocks.append(
                (
                    record[6:7].astype(jnp.int32),
                    record[7:10],
                    record[0:3] * record[10:11],
                )
            )
        acc[...] += deposit_chunk(tile, blocks)
        return carry

    lax.fori_loop(0, 8 * CAP // 2, step, 0)

    def edge(ref, high):
        first = tile.ye - EDGE if high else 0
        tail = 3 * tile.edge_main
        for k in range(3):
            lanes = slice(k * tile.nz, (k + 1) * tile.nz)
            ref[k * tile.edge_main : (k + 1) * tile.edge_main] = acc[
                first * tile.wx : (first + EDGE) * tile.wx, lanes
            ]
            for h in range(2):
                start = tile.main + h * tile.hp + first
                row = tail + (2 * k + h) * EDGE
                ref[row : row + EDGE] = acc[start : start + EDGE, lanes]

    def even():
        edge(send_a, True)
        edge(send_b, False)

    def odd():
        edge(send_a, False)
        edge(send_b, True)

    for ref in (send_a, send_b):
        last = tile.edge_rows - SUB
        ref[last:] = jnp.zeros((SUB, tile.nz), jnp.float32)
    if_(a_high, even, odd)


def widen_kernel(tile, axis, count, acc, recv_a, recv_b, mid, beyond, xsend):
    _, a_from_high = ty_roles(axis, count)
    own = slice(REACH - 1, REACH - 1 + tile.ye)
    for k in range(3):
        lanes = slice(k * tile.nz, (k + 1) * tile.nz)
        zero = jnp.zeros((REACH - 1, tile.wx, tile.nz), jnp.float32)
        mid[k, : REACH - 1] = zero
        mid[k, REACH - 1 + tile.ye :] = zero
        mid[k, own] = acc[: tile.main, lanes].reshape(tile.ye, tile.wx, tile.nz)
        for h in range(2):
            start = tile.main + h * tile.hp
            beyond[k, h] = jnp.zeros((tile.yp, tile.nz), jnp.float32)
            beyond[k, h, own] = acc[start : start + tile.ye, lanes]

    def add(ref, high):
        first = tile.yw - EDGE if high else 0
        tail = 3 * tile.edge_main
        for k in range(3):
            rows = ref[k * tile.edge_main : (k + 1) * tile.edge_main]
            mid[k, first : first + EDGE] += rows.reshape(EDGE, tile.wx, tile.nz)
            for h in range(2):
                row = tail + (2 * k + h) * EDGE
                beyond[k, h, first : first + EDGE] += ref[row : row + EDGE]

    if_(
        a_from_high,
        lambda: (add(recv_a, True), add(recv_b, False)) and None,
        lambda: (add(recv_a, False), add(recv_b, True)) and None,
    )
    tail = 3 * tile.yw
    for k in range(3):
        for side, first in ((0, 0), (1, tile.wx - SUB)):
            for y in range(tile.yw):
                xsend[side, k * tile.yw + y] = mid[k, y, first : first + SUB]
            for part in range(tile.yp // SUB):
                xsend[side, tail + k * (tile.yp // SUB) + part] = beyond[
                    k, side, part * SUB : (part + 1) * SUB
                ]


def finish_kernel(
    tile, axis, count, slots, codes, cells, offsets, velocity, gas, xgas, ygas_a, ygas_b,
    arrivals, mid, beyond, xrecv, gas_new, slip, src, ping, pong, field, stack,
):
    _, a_from_high = ty_roles(axis, count)
    wide = tile.wx + 2 * SUB
    tail = 3 * tile.yw
    parts = tile.yp // SUB
    for k in range(3):
        for y in range(tile.yw):
            place = tail + k * parts + y // SUB
            row = y % SUB
            src[k, y, 0:SUB] = xrecv[1, k * tile.yw + y]
            src[k, y, SUB : SUB + tile.wx] = mid[k, y]
            src[k, y, SUB + tile.wx :] = xrecv[0, k * tile.yw + y]
            src[k, y, SUB - 1 : SUB] += beyond[k, 0, y : y + 1]
            src[k, y, SUB + tile.wx : SUB + tile.wx + 1] += beyond[k, 1, y : y + 1]
            src[k, y, SUB : SUB + 1] += xrecv[1, place, row : row + 1]
            src[k, y, SUB + tile.wx - 1 : SUB + tile.wx] += xrecv[0, place, row : row + 1]

    def sweep(old, new, margin):
        def row(y, carry):
            for k in range(3):
                here = old[k, y]
                around = old[k, y - 1] + old[k, y + 1]
                around = around + pltpu.roll(here, 1, 0) + pltpu.roll(here, wide - 1, 0)
                around = around + pltpu.roll(here, 1, 1) + pltpu.roll(here, tile.nz - 1, 1)
                new[k, y] = (src[k, y] + DIFFUSE * around) * (1.0 / (1.0 + 6.0 * DIFFUSE))
            return carry

        lax.fori_loop(margin, tile.yw - margin, row, 0, unroll=2)

    buffers = [src, ping, pong, ping, pong]
    for index in range(SWEEPS):
        sweep(buffers[index], buffers[index + 1], index + 1)
    filtered = buffers[SWEEPS]

    per_x, per_y = tile.wx // REC, tile.wy // REC

    def take_edges(ref, high):
        y = tile.ye - 1 if high else 0
        for k in range(3):
            for part in range(per_x):
                row = y * tile.wx + part * REC
                stack[k, row : row + REC] = ref[3 * CAP + k * per_x + part]
            corner = 3 * CAP + 3 * per_x
            for h in range(2):
                row = tile.main + h * tile.hp + y
                stack[k, row : row + 1] = ref[corner, 2 * k + h : 2 * k + h + 1]

    for k in range(3):
        for h in range(2):
            start = tile.main + h * tile.hp
            stack[k, start : start + tile.hp] = jnp.zeros((tile.hp, tile.nz), jnp.float32)
            for part in range(per_y):
                row = start + 1 + part * REC
                stack[k, row : row + REC] = xgas[1 - h, 3 * CAP + k * per_y + part]
        for y in range(tile.wy):
            stack[k, (y + 1) * tile.wx : (y + 2) * tile.wx] = gas[
                pl.ds(k * tile.wx * tile.wy + y, tile.wx, stride=tile.wy), :
            ]
    if_(
        a_from_high,
        lambda: (take_edges(ygas_a, True), take_edges(ygas_b, False)) and None,
        lambda: (take_edges(ygas_a, False), take_edges(ygas_b, True)) and None,
    )
    depth = field.shape[1]
    for k in range(3):
        for y in range(tile.ye):
            rows = slice(y * tile.wx, (y + 1) * tile.wx)
            value = filtered[k, y + REACH - 1]
            updated = stack[k, rows] + STEP_SIZE * value[SUB : SUB + tile.wx]
            stack[k, rows] = updated
            if 1 <= y <= tile.wy:
                gas_new[pl.ds(k * tile.wx * tile.wy + y - 1, tile.wx, stride=tile.wy), :] = updated
            for h, x in ((0, SUB - 1), (1, SUB + tile.wx)):
                row = tile.main + h * tile.hp + y
                stack[k, row : row + 1] += STEP_SIZE * value[x : x + 1]
        whole = stack[k]
        top = whole.astype(jnp.bfloat16).astype(jnp.float32)
        pad = jnp.zeros((depth - 3 * tile.rows, tile.nz), jnp.float32)
        both = jnp.concatenate([top, top, whole - top, pad], axis=0)
        field[k * tile.nz : (k + 1) * tile.nz] = both.T.astype(jnp.bfloat16)

    def sample(blocks):
        tables, verticals = [], []
        for cell, sixteenths in blocks:
            cx, cy, cz = tile.decode(cell)
            weights = tsc_weights(sixteenths)
            tops, lows = zip(*[halves(part) for part in tile.planar(cx, cy, weights)])
            pad = jnp.zeros((depth - 3 * tile.rows, 128), jnp.bfloat16)
            tables.append(jnp.concatenate(tops + lows + tops + (pad,), axis=0))
            verticals.append(tile.vertical(cz, weights))
        column = jnp.dot(
            field[...], jnp.concatenate(tables, axis=1), preferred_element_type=jnp.float32
        )
        out = []
        for i, vertical in enumerate(verticals):
            part = column[:, i * 128 : (i + 1) * 128]
            sums = [
                jnp.sum(part[k * tile.nz : (k + 1) * tile.nz] * vertical, axis=0, keepdims=True)
                for k in range(3)
            ]
            out.append(jnp.concatenate(sums, axis=0))
        return out

    def own_step(pair, carry):
        first = pair * 2
        blocks = [(cells[pl.ds(first + i, 1)], offsets[first + i].astype(jnp.float32)) for i in range(2)]
        for i, value in enumerate(sample(blocks)):
            stays = (codes[first + i] == STAY).astype(jnp.float32)
            slip[first + i] = (value - velocity[first + i]) * stays
        return carry

    lax.fori_loop(0, slots // 2, own_step, 0)

    def arrival_step(pair, carry):
        first = pair * 2
        records = [arrivals[first + i] for i in range(2)]
        blocks = [(record[6:7].astype(jnp.int32), record[7:10]) for record in records]
        for i, value in enumerate(sample(blocks)):
            slip[slots + first + i] = (value - records[i][3:6]) * records[i][10:11]
        return carry

    lax.fori_loop(0, 8 * CAP // 2, arrival_step, 0)


def exchange_x(buffer, axis, count):
    forward = [(i, (i + 1) % count) for i in range(count)]
    backward = [(target, source) for source, target in forward]
    if count == 2:
        return lax.ppermute(buffer, axis, forward)
    return jnp.stack(
        [lax.ppermute(buffer[0], axis, backward), lax.ppermute(buffer[1], axis, forward)]
    )


def exchange_y(send_a, send_b, axis, count):
    if count % 2:
        perm_a = [(i, (i + 1) % count) for i in range(count)]
        perm_b = [(target, source) for source, target in perm_a]
    else:
        perm_a = [(i, i ^ 1) for i in range(count)]
        perm_b = [(i, (i + 1) % count if i % 2 else (i - 1) % count) for i in range(count)]
    return lax.ppermute(send_a, axis, perm_a), lax.ppermute(send_b, axis, perm_b)


def on_device(count_x, count_y, handoff, cells, offsets, drag, bubble_velocity, gas):
    tile = Tile(gas.shape[1], gas.shape[2], gas.shape[3])
    slots, lanes = cells.shape[2], cells.shape[3]
    codes = handoff.reshape(slots)
    cells = cells.reshape(slots, lanes)
    offsets = offsets.reshape(slots, 3, lanes)
    drag = drag.reshape(slots, 3, lanes)
    velocity = bubble_velocity.reshape(slots, 3, lanes)
    gas_rows = gas.reshape(3 * tile.wx * tile.wy, tile.nz)
    per_x, per_y = tile.wx // REC, tile.wy // REC
    bind = functools.partial
    macs = tile.rows * 3 * tile.nz * 3 * 2 * lanes

    xsend, own = call(
        bind(pack_kernel, tile, slots),
        [(2, 3 * CAP + 3 * per_y, REC, lanes), (2, CAP, REC, lanes)],
        [codes, cells, offsets, drag, velocity, gas_rows],
        [SMEM] + [VMEM] * 5,
        scratch=[pltpu.SMEM((9,), jnp.int32)],
        name="pack",
    )
    xrecv = exchange_x(xsend, "tx", count_x)
    ty_shape = (3 * CAP + 3 * per_x + 1, REC, lanes)
    send_a, send_b = call(
        bind(join_kernel, tile, "ty", count_y), [ty_shape] * 2, [xrecv, own, gas_rows], name="join"
    )
    recv_a, recv_b = exchange_y(send_a, send_b, "ty", count_y)
    (acc,) = call(
        bind(own_kernel, tile, slots),
        [(tile.rows, 3 * tile.nz)],
        [codes, cells, offsets, drag],
        [SMEM] + [VMEM] * 3,
        cost=(macs * slots, slots * lanes * 40),
        name="deposit_own",
    )
    edge_shape = (tile.edge_rows, tile.nz)
    acc, arrivals, edge_a, edge_b = call(
        bind(arrive_kernel, tile, "ty", count_y),
        [acc.shape, (8 * CAP, REC, lanes), edge_shape, edge_shape],
        [recv_a, recv_b, xrecv, acc],
        cost=(macs * 8 * CAP, 8 * CAP * lanes * 40),
        name="deposit_arrivals",
    )
    got_a, got_b = exchange_y(edge_a, edge_b, "ty", count_y)
    mid, beyond, xedge = call(
        bind(widen_kernel, tile, "ty", count_y),
        [
            (3, tile.yw, tile.wx, tile.nz),
            (3, 2, tile.yp, tile.nz),
            (2, 3 * tile.yw + 3 * (tile.yp // SUB), SUB, tile.nz),
        ],
        [acc, got_a, got_b],
        name="widen",
    )
    xgot = exchange_x(xedge, "tx", count_x)
    depth = round_up(3 * tile.rows, 128)
    wide = (3, tile.yw, tile.wx + 2 * SUB, tile.nz)
    gas_new, slip = call(
        bind(finish_kernel, tile, "ty", count_y, slots),
        [gas_rows.shape, (slots + 8 * CAP, 3, lanes)],
        [codes, cells, offsets, velocity, gas_rows, xrecv, recv_a, recv_b, arrivals, mid, beyond, xgot],
        [SMEM] + [VMEM] * 11,
        scratch=[
            pltpu.VMEM(wide, jnp.float32),
            pltpu.VMEM(wide, jnp.float32),
            pltpu.VMEM(wide, jnp.float32),
            pltpu.VMEM((3 * tile.nz, depth), jnp.bfloat16),
            pltpu.VMEM((3, tile.rows, tile.nz), jnp.float32),
        ],
        cost=(macs * (slots + 8 * CAP), (slots + 8 * CAP) * lanes * 40),
        name="finish",
    )
    return gas_new.reshape(gas.shape), slip.reshape(1, 1, slots + 8 * CAP, 3, lanes)


def solution(mesh):
    return jax.shard_map(
        functools.partial(on_device, mesh.shape["tx"], mesh.shape["ty"]),
        mesh=mesh,
        in_specs=(
            P("tx", "ty", None, None),
            P("tx", "ty", None, None),
            P("tx", "ty", None, None, None),
            P("tx", "ty", None, None, None),
            P("tx", "ty", None, None, None),
            P(None, "tx", "ty", None),
        ),
        out_specs=(P(None, "tx", "ty", None), P("tx", "ty", None, None, None)),
        check_vma=False,
    )
```

time: 163 us -> 78 us (0.48)
  matrix products: 71.3 us -> 0 us
  Pallas kernels: 0 us -> 48.6 us
  other arithmetic: 22.2 us -> 0 us
  local copies, waits for them, and re-layouts: 22.5 us -> 7.33 us
  waiting for transfers between devices: 22 us -> 11.4 us
  starting transfers between devices: 20.3 us -> 9.87 us
  loops' own time: 1.81 us -> 0 us
    dot_general x48 -> x0, matrix products: 71.3 us -> none  [the longest x24 38.7 us: resample(): lax.dot_general(field_ext[component], planar, (((0,), (0,)), ((), ())), p...]
    pallas_call x0 -> x6, Pallas kernels: none -> 48.6 us  [call(): pl.pallas_call(body, out_shape=[jax.ShapeDtypeStruct(shape, jnp.float32)...]
    ppermute x12 -> x6, waiting for transfers between devices: 22 us -> 11.4 us  [the longest x2 5.51 us: exchange_y(): lax.ppermute(send_a, axis, perm_a)]
    ppermute x12 -> x6, starting transfers between devices: 20.3 us -> 9.87 us  [the longest x2 6.42 us: exchange_y(): lax.ppermute(send_b, axis, perm_b)]
    while x56 -> x0, local copies, waits for them, and re-layouts: 6.42 us -> none
    unnamed x10 -> x18, local copies, waits for them, and re-layouts: 1.1 us -> 6.57 us
    dynamic_update_slice x8 -> x0, other arithmetic: 4.9 us -> none  [on_device(): _, slip_steps = lax.scan(resample, None, grouped)]
    mul x42 -> x0, other arithmetic: 3.76 us -> none  [the longest x16 3.23 us: tables(): table_x[:, None, :] * table_y[None, :, :]]
  transfers between devices with their start and end apart: 12 -> 6, of which waited for: 8 -> 4; matrix products, arithmetic and copies ran while one was open for 2% -> 0% of each run, Pallas kernels for 0% -> 18%
where the time goes in v1:
time: 78 us; the launch traced here: 77.8 us
  Pallas kernels  48.6 us (62%)
  waiting for transfers between devices  11.4 us (15%)
  starting transfers between devices  9.87 us (13%)
  local copies, waits for them, and re-layouts  7.33 us (9%)
    pallas_call x6, Pallas kernels, call(): pl.pallas_call(body, out_shape=[jax.ShapeDtypeStruct(shape, jnp.float32)...  48.6 us
    unnamed x18, local copies, waits for them, and re-layouts  6.57 us
    ppermute x2, starting transfers between devices, exchange_y(): lax.ppermute(send_b, axis, perm_b)  6.42 us
    ppermute x2, waiting for transfers between devices, exchange_y(): lax.ppermute(send_a, axis, perm_a)  5.51 us
    ppermute x2, waiting for transfers between devices, exchange_x(): return lax.ppermute(buffer, axis, forward)  3.64 us
    ppermute x2, starting transfers between devices, exchange_y(): lax.ppermute(send_a, axis, perm_a)  3.03 us
    ppermute x2, waiting for transfers between devices, exchange_y(): lax.ppermute(send_b, axis, perm_b)  2.21 us
  transfers between devices with their start and end apart: 6, of which 4 were waited for; matrix products, arithmetic and copies ran while one was open for 0% of the time, Pallas kernels for 18%

profile of v1, /device:TPU:0, one launch (start us, length us, event | category | flops | bytes accessed | tf_op | source)
XLA Modules:
  0.0 77.8 jit_solution(17617309552753972259)
XLA Ops:
  0.6 0.0 copy-start.4
  0.6 0.0 copy-start.3
  0.7 1.6 %copy.15 = s32[1,1,48,3,128]{4,3,2,1,0:T(4,128)} copy(s32[1,1,48,3,128]{4,2,3,1,0:T(8,128)} %param.8) | data formatting | bytes 147456 | tf_op args[2]
  2.2 0.0 copy-done.4
  2.3 0.0 copy-done.3
  2.3 0.8 copy_bitcast_fusion
  3.0 2.7 %pack.1 = (f32[2,9,16,128]{3,2,1,0:T(8,128)}, f32[2,2,16,128]{3,2,1,0:T(8,128)}) custom-call(s32[48]{0:T(128)} %bitcast.22, s32[48,128]{1,0:T(8,128)} %bitcast.19, s32[48,3,128]{2,1,0:T(4,128)} %bitcast.15, f32[48,3,128]{2,1,0:T(4,128)} %get-tuple-element.30.drag, f32[48,3,128]{2,1,0:T(4,128)} %get-tuple-element.31.velocity, f32[768,128]{1,0:T(8,128)} %bitcast.12), custom_call_target="tpu_custom_call" | custom-call | tf_op jit(solution)/shard_map/pack/pallas_call | solution.py:29
  5.7 0.4 collective-permute-start
  6.1 1.2 %collective-permute-done.xrecv.xgas = f32[2,9,16,128]{3,2,1,0:T(8,128)S(1)} collective-permute-done((f32[2,9,16,128]{3,2,1,0:T(8,128)}, f32[2,9,16,128]{3,2,1,0:T(8,128)S(1)}, u32[]{:S(2)}, u32[]{:S(2)}) %collective-permute-start) | collective-permute-done | bytes 147488 | tf_op jit(solution)/shard_map/ppermute | solution.py:462
  7.3 0.0 copy-start.2
  7.4 0.7 copy-done.2
  8.0 1.8 %join.1 = (f32[10,16,128]{2,1,0:T(8,128)}, f32[10,16,128]{2,1,0:T(8,128)}) custom-call(f32[2,9,16,128]{3,2,1,0:T(8,128)} %copy-done.2, f32[2,2,16,128]{3,2,1,0:T(8,128)} %get-tuple-element.16.own, f32[768,128]{1,0:T(8,128)} %bitcast.13), custom_call_target="tpu_custom_call" | custom-call | tf_op jit(solution)/shard_map/join/pallas_call | solution.py:29
  9.8 3.0 %collective-permute-start.1 = (f32[10,16,128]{2,1,0:T(8,128)}, f32[10,16,128]{2,1,0:T(8,128)S(1)}, u32[]{:S(2)}, u32[]{:S(2)}) collective-permute-start(f32[10,16,128]{2,1,0:T(8,128)} %get-tuple-element.17), channel_id=1, source_target_pairs={{0,1},{1,0},{2,3},{3,2},{4,5},{5,4},{6,7},{7,6},{8,9},{9,8},{10,11... | collective-permute-start | bytes 245768 | tf_op jit(solution)/shard_map/ppermute | solution.py:475
  12.8 4.6 %collective-permute-start.2 = (f32[10,16,128]{2,1,0:T(8,128)}, f32[10,16,128]{2,1,0:T(8,128)S(1)}, u32[]{:S(2)}, u32[]{:S(2)}) collective-permute-start(f32[10,16,128]{2,1,0:T(8,128)} %get-tuple-element.18), channel_id=1, source_target_pairs={{0,15},{1,2},{2,1},{3,4},{4,3},{5,6},{6,5},{7,8},{8,7},{9,10},{10,... | collective-permute-start | bytes 245768 | tf_op jit(solution)/shard_map/ppermute | solution.py:475
  17.4 13.7 %deposit_own.1.acc_in = f32[336,384]{1,0:T(8,128)} custom-call(s32[48]{0:T(128)} %bitcast.23, s32[48,128]{1,0:T(8,128)} %bitcast.20, s32[48,3,128]{2,1,0:T(4,128)} %bitcast.16, f32[48,3,128]{2,1,0:T(4,128)} %get-tuple-element.30.drag), custom_call_target="tpu_custom_call" | custom-call | flops 4756340736 | bytes 245760 | tf_op jit(solution)/shard_map/deposit_own/pallas_call | solution.py:29
  31.1 0.0 collective-permute-done.1.recv_a.ygas_a
  31.1 0.0 copy-start.6
  31.1 0.0 collective-permute-done.2.recv_b.ygas_b
  31.1 0.6 copy-done.6
  31.7 0.0 copy-start.7
  31.7 0.6 copy-done.7
  32.3 6.2 %deposit_arrivals.1 = (f32[336,384]{1,0:T(8,128)}, f32[16,16,128]{2,1,0:T(8,128)}, f32[328,128]{1,0:T(8,128)}, f32[328,128]{1,0:T(8,128)}) custom-call(f32[10,16,128]{2,1,0:T(8,128)} %copy-done.6, f32[10,16,128]{2,1,0:T(8,128)} %copy-done.7, f32[2,9,16,128]{3,2,1,0:T(8,128)} %copy-done.2, f32[336,384]{1,0:T(8,128)} %deposit_own.1.acc_in), custom_call_target="tpu_custom_call" | custom-call | flops 1585446912 | bytes 81920 | tf_op jit(solution)/shard_map/deposit_arrivals/pallas_call | solution.py:29
  38.6 0.0 collective-permute-start.3
  38.6 1.9 %collective-permute-start.4 = (f32[328,128]{1,0:T(8,128)}, f32[328,128]{1,0:T(8,128)S(1)}, u32[]{:S(2)}, u32[]{:S(2)}) collective-permute-start(f32[328,128]{1,0:T(8,128)} %get-tuple-element.22), channel_id=1, source_target_pairs={{0,15},{1,2},{2,1},{3,4},{4,3},{5,6},{6,5},{7,8},{8,7},{9,10},{10,... | collective-permute-start | bytes 503816 | tf_op jit(solution)/shard_map/ppermute | solution.py:475
  40.4 5.5 %collective-permute-done.3.recv_a = f32[328,128]{1,0:T(8,128)S(1)} collective-permute-done((f32[328,128]{1,0:T(8,128)}, f32[328,128]{1,0:T(8,128)S(1)}, u32[]{:S(2)}, u32[]{:S(2)}) %collective-permute-start.3) | collective-permute-done | bytes 167968 | tf_op jit(solution)/shard_map/ppermute | solution.py:475
  45.9 0.0 copy-start
  45.9 2.2 %collective-permute-done.4.recv_b = f32[328,128]{1,0:T(8,128)S(1)} collective-permute-done((f32[328,128]{1,0:T(8,128)}, f32[328,128]{1,0:T(8,128)S(1)}, u32[]{:S(2)}, u32[]{:S(2)}) %collective-permute-start.4) | collective-permute-done | bytes 167968 | tf_op jit(solution)/shard_map/ppermute | solution.py:475
  48.1 0.0 copy-start.1
  48.1 0.0 copy-done
  48.1 0.7 copy-done.1
  48.8 2.4 %widen.1 = (f32[3,26,16,128]{3,2,1,0:T(8,128)}, f32[3,2,32,128]{3,2,1,0:T(8,128)}, f32[2,90,8,128]{3,2,1,0:T(8,128)}) custom-call(f32[336,384]{1,0:T(8,128)} %get-tuple-element.20.acc, f32[328,128]{1,0:T(8,128)} %copy-done, f32[328,128]{1,0:T(8,128)} %copy-done.1), custom_call_target="tpu_custom_call" | custom-call | tf_op jit(solution)/shard_map/widen/pallas_call | solution.py:29
  51.2 0.0 collective-permute-start.5
  51.2 2.4 %collective-permute-done.5.xrecv = f32[2,90,8,128]{3,2,1,0:T(8,128)S(1)} collective-permute-done((f32[2,90,8,128]{3,2,1,0:T(8,128)}, f32[2,90,8,128]{3,2,1,0:T(8,128)S(1)}, u32[]{:S(2)}, u32[]{:S(2)}) %collective-permute-start.5) | collective-permute-done | bytes 737312 | tf_op jit(solution)/shard_map/ppermute | solution.py:462
  53.6 0.0 copy-start.5
  53.6 0.9 %copy-done.5 = f32[2,90,8,128]{3,2,1,0:T(8,128)} copy-done((f32[2,90,8,128]{3,2,1,0:T(8,128)}, f32[2,90,8,128]{3,2,1,0:T(8,128)S(1)}, u32[]{:S(2)}) %copy-start.5) | copy-done | bytes 737304
  54.5 21.8 %finish.1 = (f32[768,128]{1,0:T(8,128)}, f32[64,3,128]{2,1,0:T(4,128)}) custom-call(s32[48]{0:T(128)} %bitcast.24, s32[48,128]{1,0:T(8,128)} %bitcast.21, s32[48,3,128]{2,1,0:T(4,128)} %bitcast.17, f32[48,3,128]{2,1,0:T(4,128)} %get-tuple-element.31.velocity, f32[768,128]{1,0:T(8,128)} %bitcast.14, f32[2,9,16,128]{3,2,1,0:T(8,128)} %copy-done.2, ...), custom_call_target="tpu_custom_call" | custom-call | flops 6341787648 | bytes 327680 | tf_op jit(solution)/shard_map/finish/pallas_call | solution.py:29
  76.3 1.6 %copy.11 = f32[1,1,64,3,128]{4,2,3,1,0:T(8,128)} copy(f32[1,1,64,3,128]{4,3,2,1,0:T(4,128)} %bitcast.18) | data formatting | bytes 196608
Async XLA Ops:
  0.6 1.6 %copy-start.4 = (f32[1,1,48,3,128]{4,2,3,1,0:T(8,128)S(1)}, f32[1,1,48,3,128]{4,2,3,1,0:T(8,128)}, u32[]{:S(2)}) copy-start(f32[1,1,48,3,128]{4,2,3,1,0:T(8,128)} %param.10) | copy-start | bytes 221188
  0.6 1.6 %copy-start.3 = (f32[1,1,48,3,128]{4,2,3,1,0:T(8,128)S(1)}, f32[1,1,48,3,128]{4,2,3,1,0:T(8,128)}, u32[]{:S(2)}) copy-start(f32[1,1,48,3,128]{4,2,3,1,0:T(8,128)} %param.9) | copy-start | bytes 221188
  5.7 1.6 %collective-permute-start = (f32[2,9,16,128]{3,2,1,0:T(8,128)}, f32[2,9,16,128]{3,2,1,0:T(8,128)S(1)}, u32[]{:S(2)}, u32[]{:S(2)}) collective-permute-start(f32[2,9,16,128]{3,2,1,0:T(8,128)} %get-tuple-element.15), channel_id=1, source_target_pairs={{0,16},{16,0},{1,17},{17,1},{2,18},{18,2},{3,19},{19,3},{4,20},{20... | collective-permute-start | bytes 442376 | tf_op jit(solution)/shard_map/ppermute | solution.py:462
  7.3 0.7 copy-start.2
  9.8 21.3 %collective-permute-start.1 = (f32[10,16,128]{2,1,0:T(8,128)}, f32[10,16,128]{2,1,0:T(8,128)S(1)}, u32[]{:S(2)}, u32[]{:S(2)}) collective-permute-start(f32[10,16,128]{2,1,0:T(8,128)} %get-tuple-element.17), channel_id=1, source_target_pairs={{0,1},{1,0},{2,3},{3,2},{4,5},{5,4},{6,7},{7,6},{8,9},{9,8},{10,11... | collective-permute-start | bytes 245768 | tf_op jit(solution)/shard_map/ppermute | solution.py:475
  12.8 18.3 %collective-permute-start.2 = (f32[10,16,128]{2,1,0:T(8,128)}, f32[10,16,128]{2,1,0:T(8,128)S(1)}, u32[]{:S(2)}, u32[]{:S(2)}) collective-permute-start(f32[10,16,128]{2,1,0:T(8,128)} %get-tuple-element.18), channel_id=1, source_target_pairs={{0,15},{1,2},{2,1},{3,4},{4,3},{5,6},{6,5},{7,8},{8,7},{9,10},{10,... | collective-permute-start | bytes 245768 | tf_op jit(solution)/shard_map/ppermute | solution.py:475
  31.1 0.6 copy-start.6
  31.7 0.6 copy-start.7
  38.6 7.4 %collective-permute-start.3 = (f32[328,128]{1,0:T(8,128)}, f32[328,128]{1,0:T(8,128)S(1)}, u32[]{:S(2)}, u32[]{:S(2)}) collective-permute-start(f32[328,128]{1,0:T(8,128)} %get-tuple-element.21), channel_id=1, source_target_pairs={{0,1},{1,0},{2,3},{3,2},{4,5},{5,4},{6,7},{7,6},{8,9},{9,8},{10,11... | collective-permute-start | bytes 503816 | tf_op jit(solution)/shard_map/ppermute | solution.py:475
  38.6 9.6 %collective-permute-start.4 = (f32[328,128]{1,0:T(8,128)}, f32[328,128]{1,0:T(8,128)S(1)}, u32[]{:S(2)}, u32[]{:S(2)}) collective-permute-start(f32[328,128]{1,0:T(8,128)} %get-tuple-element.22), channel_id=1, source_target_pairs={{0,15},{1,2},{2,1},{3,4},{4,3},{5,6},{6,5},{7,8},{8,7},{9,10},{10,... | collective-permute-start | bytes 503816 | tf_op jit(solution)/shard_map/ppermute | solution.py:475
  45.9 2.2 %copy-start = (f32[328,128]{1,0:T(8,128)}, f32[328,128]{1,0:T(8,128)S(1)}, u32[]{:S(2)}) copy-start(f32[328,128]{1,0:T(8,128)S(1)} %collective-permute-done.3.recv_a) | copy-start | bytes 503812
  48.1 0.7 copy-start.1
  51.2 2.4 %collective-permute-start.5 = (f32[2,90,8,128]{3,2,1,0:T(8,128)}, f32[2,90,8,128]{3,2,1,0:T(8,128)S(1)}, u32[]{:S(2)}, u32[]{:S(2)}) collective-permute-start(f32[2,90,8,128]{3,2,1,0:T(8,128)} %get-tuple-element.25), channel_id=1, source_target_pairs={{0,16},{16,0},{1,17},{17,1},{2,18},{18,2},{3,19},{19,3},{4,20},{20... | collective-permute-start | bytes 2211848 | tf_op jit(solution)/shard_map/ppermute | solution.py:462
  53.6 0.9 %copy-start.5 = (f32[2,90,8,128]{3,2,1,0:T(8,128)}, f32[2,90,8,128]{3,2,1,0:T(8,128)S(1)}, u32[]{:S(2)}) copy-start(f32[2,90,8,128]{3,2,1,0:T(8,128)S(1)} %collective-permute-done.5.xrecv) | copy-start | bytes 2211844

commit v2 on v1

v2 whole, which is shorter than its diff:
```python
import functools

import jax
import jax.numpy as jnp
from jax import lax
from jax.experimental import pallas as pl
from jax.experimental.pallas import tpu as pltpu
from jax.sharding import PartitionSpec as P

SWEEPS = 4
CAP = 2
DIFFUSE = 1.0
STEP_SIZE = 2.0

REC = 16
STAY = 4
REACH = SWEEPS + 1
EDGE = REACH + 1
SUB = 8
VMEM = pl.BlockSpec(memory_space=pltpu.VMEM)
SMEM = pl.BlockSpec(memory_space=pltpu.SMEM)
HBM = pl.BlockSpec(memory_space=pltpu.HBM)
ANY = pl.BlockSpec(memory_space=pl.ANY)
LIMIT = 24 * 1024 * 1024
COLS = 16


def round_up(count, unit):
    return -(-count // unit) * unit


def call(body, outs, args, specs=None, scratch=(), cost=(0, 0), name=None, results=False):
    specs = specs or [VMEM] * len(args)
    kind = jax.ShapeDtypeStruct if results else pltpu.VMEM
    return pl.pallas_call(
        body,
        out_shape=[
            kind(*out) if isinstance(out[0], tuple) else kind(out, jnp.float32) for out in outs
        ],
        in_specs=specs,
        out_specs=[VMEM] * len(outs),
        scratch_shapes=list(scratch),
        compiler_params=pltpu.CompilerParams(vmem_limit_bytes=LIMIT),
        cost_estimate=pl.CostEstimate(flops=cost[0], bytes_accessed=cost[1], transcendentals=0),
        name=name,
    )(
        *[
            arg if spec in (SMEM, ANY) else pltpu.with_memory_space_constraint(arg, spec.memory_space)
            for arg, spec in zip(args, specs)
        ]
    )


def split_by(value, size):
    if size & (size - 1) == 0:
        return value >> (size.bit_length() - 1), value & (size - 1)
    return value // size, value % size


class Tile:
    def __init__(self, wx, wy, nz):
        self.wx, self.wy, self.nz = wx, wy, nz
        self.ye = wy + 2
        self.hp = round_up(self.ye, SUB)
        self.main = self.ye * wx
        self.rows = self.main + 2 * self.hp
        self.yw = wy + 2 * REACH
        self.yp = round_up(self.yw, SUB)
        self.edge_main = EDGE * wx
        self.edge_rows = round_up(3 * (self.edge_main + 2 * EDGE), SUB)

    def decode(self, cell):
        cx, rest = split_by(cell, self.wy * self.nz)
        cy, cz = split_by(rest, self.nz)
        return cx, cy, cz

    def prepare(self, first, cell, sixteenths, fields, columns, force=None):
        count = cell.shape[0]
        cx, cy, cz = self.decode(cell)
        rows = slice(first, first + count)
        fields[0, rows] = cx.astype(jnp.float32)
        fields[1, rows] = cy.astype(jnp.float32)
        for axis in range(2):
            for i, weight in enumerate(tsc_weights(sixteenths[axis])):
                fields[2 + 3 * axis + i, rows] = weight
        below = jnp.where(cz == 0, self.nz - 1, cz - 1).astype(jnp.float32)
        above = jnp.where(cz == self.nz - 1, 0, cz + 1).astype(jnp.float32)
        values = [below, cz.astype(jnp.float32), above, *tsc_weights(sixteenths[2])]
        if force is not None:
            values += force
        for i, value in enumerate(values):
            columns[pl.ds(first * COLS + i, count, stride=COLS), :] = value

    def vertical(self, columns, slot):
        start = pl.multiple_of(slot * COLS, COLS)
        rows = [columns[pl.ds(start, COLS), :][j : j + 1] for j in range(9)]
        iz = lax.broadcasted_iota(jnp.int32, (self.nz, rows[0].shape[1]), 0).astype(jnp.float32)
        tz = jnp.where(iz == rows[2], rows[5], 0.0)
        tz = jnp.where(iz == rows[1], rows[4], tz)
        return jnp.where(iz == rows[0], rows[3], tz), rows[6:9]

    def planar(self, fields, slot):
        lanes = fields.shape[2]
        cx, cy, *weights = [fields[i, pl.ds(slot, 1), :] for i in range(8)]
        ix = lax.broadcasted_iota(jnp.int32, (self.wx, lanes), 0).astype(jnp.float32)
        tx = jnp.where(ix == cx + 1.0, weights[2], 0.0)
        tx = jnp.where(ix == cx, weights[1], tx)
        tx = jnp.where(ix == cx - 1.0, weights[0], tx)
        iy = lax.broadcasted_iota(jnp.int32, (self.hp, lanes), 0).astype(jnp.float32)
        ty = jnp.where(iy == cy + 2.0, weights[5], 0.0)
        ty = jnp.where(iy == cy + 1.0, weights[4], ty)
        ty = jnp.where(iy == cy, weights[3], ty)
        beyond_low = jnp.where(cx == 0.0, weights[0], 0.0)
        beyond_high = jnp.where(cx == self.wx - 1.0, weights[2], 0.0)
        parts = [tx * ty[j : j + 1] for j in range(self.ye)]
        return parts + [jnp.concatenate([ty * beyond_low, ty * beyond_high], axis=0)]


def tsc_weights(sixteenths):
    fraction = (sixteenths + 0.5) * (1.0 / 16.0) - 0.5
    low = 0.5 - fraction
    high = 0.5 + fraction
    return 0.5 * low * low, 0.75 - fraction * fraction, 0.5 * high * high


def halves(value):
    top = value.astype(jnp.bfloat16)
    return top, (value - top.astype(jnp.float32)).astype(jnp.bfloat16)


def put_planar(tile, fields, slot, ref, top_at, low_at):
    row = 0
    for part in tile.planar(fields, slot):
        top, low = halves(part)
        count = part.shape[0]
        for (slab, first), value in ((top_at, top), (low_at, low)):
            ref[slab, first + row : first + row + count] = value
        row += count


def pipeline(steps, build, use):
    build(0, 0)
    assert steps % 2 == 0

    def pair(i, carry):
        use(0, 2 * i)
        build(1, 2 * i + 1)
        use(1, 2 * i + 1)
        build(0, 2 * i + 2)
        return carry

    lax.fori_loop(0, steps // 2 - 1, pair, 0, unroll=True)
    use(0, steps - 2)
    build(1, steps - 1)
    use(1, steps - 1)


def deposit(tile, slots, fields, columns, acc, left, right):
    def build(buffer, step):
        for i in range(2):
            slot = step * 2 + i
            put_planar(tile, fields, slot, left[buffer], (i, 0), (2 + i, 0))
            tz, force = tile.vertical(columns, slot)
            for k in range(3):
                top, low = halves(tz * force[k])
                right[buffer][i, k * tile.nz : (k + 1) * tile.nz] = top
                right[buffer][2 + i, k * tile.nz : (k + 1) * tile.nz] = low

    def use(buffer, step):
        a = [left[buffer][i] for i in range(4)]
        b = [right[buffer][i] for i in range(4)]
        both = [jnp.concatenate([a[i], a[2 + i]], axis=0) for i in range(2)]
        nt = (((1,), (1,)), ((), ()))
        first = lax.dot_general(
            jnp.concatenate(both, axis=1),
            jnp.concatenate(b[:2], axis=1),
            nt,
            preferred_element_type=jnp.float32,
        )
        second = lax.dot_general(
            jnp.concatenate(a[:2], axis=1),
            jnp.concatenate(b[2:], axis=1),
            nt,
            preferred_element_type=jnp.float32,
        )
        acc[...] += first[: tile.rows] + first[tile.rows :] + second

    pipeline(slots // 2, build, use)


def ty_roles(axis, count):
    if count % 2:
        return True, False
    even = lax.axis_index(axis) % 2 == 0
    return even, even


def if_(cond, then, other):
    if isinstance(cond, bool):
        (then if cond else other)()
        return
    pl.when(cond)(then)
    pl.when(jnp.logical_not(cond))(other)


def pack_kernel(
    tile, slots, codes, cells_in, offsets_in, drag_in, velocity_in, gas_in,
    xsend, own, stays, cells, offsets, drag, velocity, gas, counts, sems,
):
    sources = (cells_in, offsets_in, drag_in, velocity_in, gas_in)
    targets = (cells, offsets, drag, velocity, gas)
    copies = [
        pltpu.make_async_copy(source, target, sems.at[i])
        for i, (source, target) in enumerate(zip(sources, targets))
    ]
    for copy in copies:
        copy.start()
    xsend[:, : 3 * CAP] = jnp.zeros((2, 3 * CAP, REC, 128), jnp.float32)
    own[...] = jnp.zeros(own.shape, jnp.float32)
    for code in range(9):
        counts[code] = 0
    for copy in copies:
        copy.wait()
    per = tile.wy // REC
    for k in range(3):
        for side, x in ((0, 0), (1, tile.wx - 1)):
            for part in range(per):
                start = (k * tile.wx + x) * tile.wy + part * REC
                xsend[side, 3 * CAP + k * per + part] = gas[start : start + REC]

    def visit(slot, carry):
        code = codes[slot]
        here = pl.ds(slot, 1)
        stays[here] = jnp.full((1, 128), (code == STAY).astype(jnp.float32), jnp.float32)

        @pl.when(code != STAY)
        def _():
            rank = jnp.minimum(counts[code], CAP - 1)
            counts[code] = rank + 1

            def put(ref, side, place):
                for k in range(3):
                    ref[side, place, k : k + 1] = drag[k, here]
                    ref[side, place, 3 + k : 4 + k] = velocity[k, here]
                    ref[side, place, 7 + k : 8 + k] = offsets[k, here].astype(jnp.float32)
                ref[side, place, 6:7] = cells[here].astype(jnp.float32)
                ref[side, place, 10:11] = jnp.ones((1, 128), jnp.float32)

            step_x, step_y = code // 3, code % 3
            pl.when(step_x == 1)(lambda: put(own, step_y // 2, rank))
            pl.when(step_x != 1)(lambda: put(xsend, step_x // 2, step_y * CAP + rank))

        return carry

    lax.fori_loop(0, slots, visit, 0)


def join_kernel(tile, axis, count, xrecv, own, gas, send_a, send_b):
    a_high, _ = ty_roles(axis, count)
    per_x, per_y = tile.wx // REC, tile.wy // REC

    def fill(ref, high):
        step = 2 * CAP * int(high)
        y = tile.wy - 1 if high else 0
        for s in range(CAP):
            ref[s] = xrecv[1, step + s]
            ref[CAP + s] = own[int(high), s]
            ref[2 * CAP + s] = xrecv[0, step + s]
        for k in range(3):
            for part in range(per_x):
                start = (k * tile.wx + part * REC) * tile.wy + y
                ref[3 * CAP + k * per_x + part] = gas[pl.ds(start, REC, stride=tile.wy), :]
            place = 3 * CAP + k * per_y + y // REC
            corner = 3 * CAP + 3 * per_x
            ref[corner, 2 * k : 2 * k + 1] = xrecv[1, place, y % REC : y % REC + 1]
            ref[corner, 2 * k + 1 : 2 * k + 2] = xrecv[0, place, y % REC : y % REC + 1]

    def even():
        fill(send_a, True)
        fill(send_b, False)

    def odd():
        fill(send_a, False)
        fill(send_b, True)

    for ref in (send_a, send_b):
        ref[3 * CAP + 3 * per_x] = jnp.zeros((REC, 128), jnp.float32)
    if_(a_high, even, odd)


def table_scratch(tile, slots):
    left, right = (4, tile.rows, 128), (4, 3 * tile.nz, 128)
    return [
        pltpu.VMEM((8, slots, 128), jnp.float32),
        pltpu.VMEM((slots * COLS, 128), jnp.float32),
        *[pltpu.VMEM(shape, jnp.bfloat16) for shape in (left, left, right, right)],
    ]


def own_kernel(tile, slots, cells, offsets, drag, stays, acc, fields, columns, la, lb, ra, rb):
    acc[...] = jnp.zeros(acc.shape, jnp.float32)
    sixteenths = [offsets[k].astype(jnp.float32) for k in range(3)]
    force = [drag[k] * stays[...] for k in range(3)]
    columns[...] = jnp.zeros(columns.shape, jnp.float32)
    tile.prepare(0, cells[...], sixteenths, fields, columns, force)
    deposit(tile, slots, fields, columns, acc, (la, lb), (ra, rb))


def record_row(records, row, count):
    return records[pl.ds(row, count, stride=REC), :]


ARRIVAL_LOW, ARRIVAL_HIGH = (0, 3, 5), (2, 4, 7)


def arrive_kernel(
    tile, axis, count, recv_a, recv_b, xrecv, acc_in, acc, arrivals, send_a, send_b,
    fields, columns, la, lb, ra, rb,
):
    a_high, a_from_high = ty_roles(axis, count)
    for s in range(CAP):
        arrivals[(1 * CAP + s) * REC : (1 * CAP + s + 1) * REC] = xrecv[1, CAP + s]
        arrivals[(6 * CAP + s) * REC : (6 * CAP + s + 1) * REC] = xrecv[0, CAP + s]

    def place(ref, order):
        for i, j in enumerate(order):
            for s in range(CAP):
                arrivals[(j * CAP + s) * REC : (j * CAP + s + 1) * REC] = ref[i * CAP + s]

    if_(
        a_from_high,
        lambda: (place(recv_a, ARRIVAL_HIGH), place(recv_b, ARRIVAL_LOW)) and None,
        lambda: (place(recv_a, ARRIVAL_LOW), place(recv_b, ARRIVAL_HIGH)) and None,
    )
    acc[...] = acc_in[...]

    blocks = 8 * CAP
    live = record_row(arrivals, 10, blocks)
    force = [record_row(arrivals, k, blocks) * live for k in range(3)]
    sixteenths = [record_row(arrivals, 7 + k, blocks) for k in range(3)]
    columns[...] = jnp.zeros(columns.shape, jnp.float32)
    cell = record_row(arrivals, 6, blocks).astype(jnp.int32)
    tile.prepare(0, cell, sixteenths, fields, columns, force)
    deposit(tile, blocks, fields, columns, acc, (la, lb), (ra, rb))

    def edge(ref, high):
        first = tile.ye - EDGE if high else 0
        tail = 3 * tile.edge_main
        for k in range(3):
            lanes = slice(k * tile.nz, (k + 1) * tile.nz)
            ref[k * tile.edge_main : (k + 1) * tile.edge_main] = acc[
                first * tile.wx : (first + EDGE) * tile.wx, lanes
            ]
            for h in range(2):
                start = tile.main + h * tile.hp + first
                row = tail + (2 * k + h) * EDGE
                ref[row : row + EDGE] = acc[start : start + EDGE, lanes]

    def even():
        edge(send_a, True)
        edge(send_b, False)

    def odd():
        edge(send_a, False)
        edge(send_b, True)

    for ref in (send_a, send_b):
        last = tile.edge_rows - SUB
        ref[last:] = jnp.zeros((SUB, tile.nz), jnp.float32)
    if_(a_high, even, odd)


def widen_kernel(tile, axis, count, acc, recv_a, recv_b, verticals, mid, beyond, xsend):
    _, a_from_high = ty_roles(axis, count)
    own = slice(REACH - 1, REACH - 1 + tile.ye)
    for k in range(3):
        lanes = slice(k * tile.nz, (k + 1) * tile.nz)
        zero = jnp.zeros((REACH - 1, tile.wx, tile.nz), jnp.float32)
        mid[k, : REACH - 1] = zero
        mid[k, REACH - 1 + tile.ye :] = zero
        mid[k, own] = acc[: tile.main, lanes].reshape(tile.ye, tile.wx, tile.nz)
        for h in range(2):
            start = tile.main + h * tile.hp
            beyond[k, h] = jnp.zeros((tile.yp, tile.nz), jnp.float32)
            beyond[k, h, own] = acc[start : start + tile.ye, lanes]

    def add(ref, high):
        first = tile.yw - EDGE if high else 0
        tail = 3 * tile.edge_main
        for k in range(3):
            rows = ref[k * tile.edge_main : (k + 1) * tile.edge_main]
            mid[k, first : first + EDGE] += rows.reshape(EDGE, tile.wx, tile.nz)
            for h in range(2):
                row = tail + (2 * k + h) * EDGE
                beyond[k, h, first : first + EDGE] += ref[row : row + EDGE]

    if_(
        a_from_high,
        lambda: (add(recv_a, True), add(recv_b, False)) and None,
        lambda: (add(recv_a, False), add(recv_b, True)) and None,
    )
    tail = 3 * tile.yw
    for k in range(3):
        for side, first in ((0, 0), (1, tile.wx - SUB)):
            for y in range(tile.yw):
                xsend[side, k * tile.yw + y] = mid[k, y, first : first + SUB]
            for part in range(tile.yp // SUB):
                xsend[side, tail + k * (tile.yp // SUB) + part] = beyond[
                    k, side, part * SUB : (part + 1) * SUB
                ]


def tables_kernel(tile, slots, cells, offsets, arrivals, tables, verticals, fields, columns):
    blocks = 8 * CAP
    tile.prepare(0, cells[...], [offsets[k].astype(jnp.float32) for k in range(3)], fields, columns)
    sixteenths = [record_row(arrivals, 7 + k, blocks) for k in range(3)]
    cell = record_row(arrivals, 6, blocks).astype(jnp.int32)
    tile.prepare(slots, cell, sixteenths, fields, columns)

    def build(pair, carry):
        for i in range(2):
            slot = pair * 2 + i
            put_planar(tile, fields, slot, tables, (slot, 0), (slot, tile.rows))
            verticals[slot], _ = tile.vertical(columns, slot)
        return carry

    lax.fori_loop(0, (slots + blocks) // 2, build, 0)


def finish_kernel(
    tile, axis, count, slots, stays, velocity, gas, xgas, ygas_a, ygas_b, arrivals,
    tables, verticals, mid, beyond, xrecv, gas_new, slip, src, ping, pong, field, stack,
):
    _, a_from_high = ty_roles(axis, count)
    zero = SUB + SWEEPS
    after = zero + tile.wx
    swept = tile.wx + 2 * SWEEPS
    tail = 3 * tile.yw
    parts = tile.yp // SUB
    for k in range(3):
        for y in range(tile.yw):
            place = tail + k * parts + y // SUB
            row = y % SUB
            src[k, y, zero - SUB : zero] = xrecv[1, k * tile.yw + y]
            src[k, y, zero:after] = mid[k, y]
            src[k, y, after : after + SUB] = xrecv[0, k * tile.yw + y]
            src[k, y, zero - 1 : zero] += beyond[k, 0, y : y + 1]
            src[k, y, after : after + 1] += beyond[k, 1, y : y + 1]
            src[k, y, zero : zero + 1] += xrecv[1, place, row : row + 1]
            src[k, y, after - 1 : after] += xrecv[0, place, row : row + 1]

    def sweep(old, new, margin):
        def row(y, carry):
            for k in range(3):
                here = old[k, y, SUB : SUB + swept]
                around = old[k, y - 1, SUB : SUB + swept] + old[k, y + 1, SUB : SUB + swept]
                around = around + old[k, y, SUB - 1 : SUB - 1 + swept]
                around = around + old[k, y, SUB + 1 : SUB + 1 + swept]
                around = around + pltpu.roll(here, 1, 1) + pltpu.roll(here, tile.nz - 1, 1)
                total = src[k, y, SUB : SUB + swept] + DIFFUSE * around
                new[k, y, SUB : SUB + swept] = total * (1.0 / (1.0 + 6.0 * DIFFUSE))
            return carry

        rows = tile.yw - 2 * margin
        lax.fori_loop(margin, tile.yw - margin, row, 0, unroll=rows // 2)

    buffers = [src, ping, pong, ping, pong]
    for index in range(SWEEPS):
        sweep(buffers[index], buffers[index + 1], index + 1)
    filtered = buffers[SWEEPS]

    per_x, per_y = tile.wx // REC, tile.wy // REC

    def take_edges(ref, high):
        y = tile.ye - 1 if high else 0
        for k in range(3):
            for part in range(per_x):
                row = y * tile.wx + part * REC
                stack[k, row : row + REC] = ref[3 * CAP + k * per_x + part]
            corner = 3 * CAP + 3 * per_x
            for h in range(2):
                row = tile.main + h * tile.hp + y
                stack[k, row : row + 1] = ref[corner, 2 * k + h : 2 * k + h + 1]

    for k in range(3):
        for h in range(2):
            start = tile.main + h * tile.hp
            stack[k, start : start + tile.hp] = jnp.zeros((tile.hp, tile.nz), jnp.float32)
            for part in range(per_y):
                row = start + 1 + part * REC
                stack[k, row : row + REC] = xgas[1 - h, 3 * CAP + k * per_y + part]
        for y in range(tile.wy):
            stack[k, (y + 1) * tile.wx : (y + 2) * tile.wx] = gas[
                pl.ds(k * tile.wx * tile.wy + y, tile.wx, stride=tile.wy), :
            ]
    if_(
        a_from_high,
        lambda: (take_edges(ygas_a, True), take_edges(ygas_b, False)) and None,
        lambda: (take_edges(ygas_a, False), take_edges(ygas_b, True)) and None,
    )
    depth = field.shape[0] * 128
    for k in range(3):
        for y in range(tile.ye):
            rows = slice(y * tile.wx, (y + 1) * tile.wx)
            updated = stack[k, rows] + STEP_SIZE * filtered[k, y + REACH - 1, zero:after]
            stack[k, rows] = updated
            if 1 <= y <= tile.wy:
                gas_new[pl.ds(k * tile.wx * tile.wy + y - 1, tile.wx, stride=tile.wy), :] = updated
            for h, x in ((0, zero - 1), (1, after)):
                row = tile.main + h * tile.hp + y
                stack[k, row : row + 1] += STEP_SIZE * filtered[k, y + REACH - 1, x : x + 1]
        whole = stack[k]
        top = whole.astype(jnp.bfloat16).astype(jnp.float32)
        pad = jnp.zeros((depth - 3 * tile.rows, tile.nz), jnp.float32)
        both = jnp.concatenate([top, top, whole - top, pad], axis=0)
        turned = both.T.astype(jnp.bfloat16)
        for i in range(depth // 128):
            field[i, k * tile.nz : (k + 1) * tile.nz] = turned[:, i * 128 : (i + 1) * 128]

    blocks = 8 * CAP
    total = slots + blocks

    def sample(pair, carry):
        pad = jnp.zeros((depth - 3 * tile.rows, 128), jnp.bfloat16)
        slabs = [tables[pair * 2 + i] for i in range(2)]
        slabs = [jnp.concatenate([slab, slab[: tile.rows], pad], axis=0) for slab in slabs]
        column = jnp.dot(
            jnp.concatenate([field[i] for i in range(depth // 128)], axis=1),
            jnp.concatenate(slabs, axis=1),
            preferred_element_type=jnp.float32,
        )
        for i in range(2):
            vertical = verticals[pair * 2 + i]
            for k in range(3):
                part = column[k * tile.nz : (k + 1) * tile.nz, i * 128 : (i + 1) * 128]
                value = jnp.sum(part * vertical, axis=0, keepdims=True)
                slip[k, pl.ds(pair * 2 + i, 1)] = value
        return carry

    lax.fori_loop(0, total // 2, sample, 0, unroll=8)
    live = record_row(arrivals, 10, blocks)
    for k in range(3):
        slip[k, :slots] = (slip[k, :slots] - velocity[k]) * stays[...]
        slip[k, slots:] = (slip[k, slots:] - record_row(arrivals, 3 + k, blocks)) * live


def exchange_x(buffer, axis, count):
    forward = [(i, (i + 1) % count) for i in range(count)]
    backward = [(target, source) for source, target in forward]
    if count == 2:
        return lax.ppermute(buffer, axis, forward)
    return jnp.stack(
        [lax.ppermute(buffer[0], axis, backward), lax.ppermute(buffer[1], axis, forward)]
    )


def exchange_y(send_a, send_b, axis, count):
    if count % 2:
        perm_a = [(i, (i + 1) % count) for i in range(count)]
        perm_b = [(target, source) for source, target in perm_a]
    else:
        perm_a = [(i, i ^ 1) for i in range(count)]
        perm_b = [(i, (i + 1) % count if i % 2 else (i - 1) % count) for i in range(count)]
    return lax.ppermute(send_a, axis, perm_a), lax.ppermute(send_b, axis, perm_b)


def on_device(count_x, count_y, handoff, cells, offsets, drag, bubble_velocity, gas):
    tile = Tile(gas.shape[1], gas.shape[2], gas.shape[3])
    slots, lanes = cells.shape[2], cells.shape[3]
    codes = handoff.reshape(slots)
    cells = cells.reshape(slots, lanes)
    offsets = offsets.reshape(slots, 3, lanes).transpose(1, 0, 2)
    drag = drag.reshape(slots, 3, lanes).transpose(1, 0, 2)
    velocity = bubble_velocity.reshape(slots, 3, lanes).transpose(1, 0, 2)
    gas_rows = gas.reshape(3 * tile.wx * tile.wy, tile.nz)
    per_x, per_y = tile.wx // REC, tile.wy // REC
    bind = functools.partial
    macs = tile.rows * 3 * tile.nz * 3 * 2 * lanes

    inputs = [cells, offsets, drag, velocity, gas_rows]
    xsend, own, stays, cells, offsets, drag, velocity, gas_rows = call(
        bind(pack_kernel, tile, slots),
        [(2, 3 * CAP + 3 * per_y, REC, lanes), (2, CAP, REC, lanes), (slots, lanes)]
        + [(value.shape, value.dtype) for value in inputs],
        [codes, *inputs],
        [SMEM] + [HBM] * 5,
        scratch=[pltpu.SMEM((9,), jnp.int32), pltpu.SemaphoreType.DMA((5,))],
        name="pack",
    )
    xrecv = exchange_x(xsend, "tx", count_x)
    ty_shape = (3 * CAP + 3 * per_x + 1, REC, lanes)
    send_a, send_b = call(
        bind(join_kernel, tile, "ty", count_y), [ty_shape] * 2, [xrecv, own, gas_rows], name="join"
    )
    recv_a, recv_b = exchange_y(send_a, send_b, "ty", count_y)
    (acc,) = call(
        bind(own_kernel, tile, slots),
        [(tile.rows, 3 * tile.nz)],
        [cells, offsets, drag, stays],
        scratch=table_scratch(tile, slots),
        cost=(macs * slots, slots * lanes * 40),
        name="deposit_own",
    )
    edge_shape = (tile.edge_rows, tile.nz)
    blocks = 8 * CAP
    acc, arrivals, edge_a, edge_b = call(
        bind(arrive_kernel, tile, "ty", count_y),
        [acc.shape, (blocks * REC, lanes), edge_shape, edge_shape],
        [recv_a, recv_b, xrecv, acc],
        scratch=table_scratch(tile, blocks),
        cost=(macs * blocks, blocks * lanes * 40),
        name="deposit_arrivals",
    )
    got_a, got_b = exchange_y(edge_a, edge_b, "ty", count_y)
    total = slots + blocks
    tables, verticals = call(
        bind(tables_kernel, tile, slots),
        [((total, 2 * tile.rows, lanes), jnp.bfloat16), (total, tile.nz, lanes)],
        [cells, offsets, arrivals],
        scratch=[
            pltpu.VMEM((8, total, lanes), jnp.float32),
            pltpu.VMEM((total * COLS, lanes), jnp.float32),
        ],
        cost=(macs * total // 2, total * lanes * 40),
        name="tables",
    )
    mid, beyond, xedge = call(
        bind(widen_kernel, tile, "ty", count_y),
        [
            (3, tile.yw, tile.wx, tile.nz),
            (3, 2, tile.yp, tile.nz),
            (2, 3 * tile.yw + 3 * (tile.yp // SUB), SUB, tile.nz),
        ],
        [acc, got_a, got_b, verticals],
        [VMEM] * 3 + [ANY],
        name="widen",
    )
    xgot = exchange_x(xedge, "tx", count_x)
    depth = round_up(3 * tile.rows, 128)
    wide = (3, tile.yw, round_up(tile.wx + SUB + SWEEPS + SUB, SUB), tile.nz)
    gas_new, slip = call(
        bind(finish_kernel, tile, "ty", count_y, slots),
        [gas_rows.shape, (3, total, lanes)],
        [stays, velocity, gas_rows, xrecv, recv_a, recv_b, arrivals]
        + [tables, verticals, mid, beyond, xgot],
        scratch=[
            *[pltpu.VMEM(wide, jnp.float32)] * 3,
            pltpu.VMEM((depth // 128, 3 * tile.nz, 128), jnp.bfloat16),
            pltpu.VMEM((3, tile.rows, tile.nz), jnp.float32),
        ],
        cost=(macs * total, total * lanes * 40),
        name="finish",
        results=True,
    )
    return gas_new.reshape(gas.shape), slip.transpose(1, 0, 2).reshape(1, 1, total, 3, lanes)


def solution(mesh):
    return jax.shard_map(
        functools.partial(on_device, mesh.shape["tx"], mesh.shape["ty"]),
        mesh=mesh,
        in_specs=(
            P("tx", "ty", None, None),
            P("tx", "ty", None, None),
            P("tx", "ty", None, None, None),
            P("tx", "ty", None, None, None),
            P("tx", "ty", None, None, None),
            P(None, "tx", "ty", None),
        ),
        out_specs=(P(None, "tx", "ty", None), P("tx", "ty", None, None, None)),
        check_vma=False,
    )
```

time: 78 us -> 46.5 us (0.60)
  Pallas kernels: 48.6 us -> 27.4 us
  local copies, waits for them, and re-layouts: 7.33 us -> 0.65 us
  waiting for transfers between devices: 11.4 us -> 8.04 us
    pallas_call x6 -> x7, Pallas kernels: 48.6 us -> 27.4 us  [call(): pl.pallas_call(body, out_shape=[kind(*out) if isinstance(out[0], tuple) e...]
    unnamed x18 -> x2, local copies, waits for them, and re-layouts: 6.57 us -> 0.65 us
    ppermute x2, waiting for transfers between devices: 5.51 us -> 2.34 us  [exchange_y(): lax.ppermute(send_a, axis, perm_a)]
  transfers between devices with their start and end apart: 6 -> 6, of which waited for: 4 -> 4; matrix products, arithmetic and copies ran while one was open for 0% -> 0% of each run, Pallas kernels for 18% -> 23%
where the time goes in v2:
time: 46.5 us; the launch traced here: 46.3 us
  Pallas kernels  27.4 us (59%)
  starting transfers between devices  9.52 us (20%)
  waiting for transfers between devices  8.04 us (17%)
  between operations  0.72 us (2%)
  local copies, waits for them, and re-layouts  0.65 us (1%)
    pallas_call x7, Pallas kernels, call(): pl.pallas_call(body, out_shape=[kind(*out) if isinstance(out[0], tuple) e...  27.4 us
    ppermute x2, starting transfers between devices, exchange_y(): lax.ppermute(send_b, axis, perm_b)  6.47 us
    ppermute x2, waiting for transfers between devices, exchange_x(): return lax.ppermute(buffer, axis, forward)  3.43 us
    ppermute x2, starting transfers between devices, exchange_y(): lax.ppermute(send_a, axis, perm_a)  2.77 us
    ppermute x2, waiting for transfers between devices, exchange_y(): lax.ppermute(send_a, axis, perm_a)  2.34 us
    ppermute x2, waiting for transfers between devices, exchange_y(): lax.ppermute(send_b, axis, perm_b)  2.27 us
  transfers between devices with their start and end apart: 6, of which 4 were waited for; matrix products, arithmetic and copies ran while one was open for 0% of the time, Pallas kernels for 23%

profile of v2, /device:TPU:0, one launch (start us, length us, event | category | flops | bytes accessed | tf_op | source)
XLA Modules:
  0.0 46.3 jit_solution(18409459118421742506)
XLA Ops:
  0.6 0.0 copy-start
  0.6 0.6 %copy-done = s32[1,1,48,1]{2,3,1,0:T(1,128)S(1)} copy-done((s32[1,1,48,1]{2,3,1,0:T(1,128)S(1)}, s32[1,1,48,1]{2,3,1,0:T(1,128)}, u32[]{:S(2)}) %copy-start) | copy-done | bytes 216
  1.3 2.7 %pack.1 = (f32[2,9,16,128]{3,2,1,0:T(8,128)S(1)}, f32[2,2,16,128]{3,2,1,0:T(8,128)S(1)}, f32[48,128]{1,0:T(8,128)S(1)}, s32[48,128]{1,0:T(8,128)S(1)}, s32[3,48,...) custom-call(s32[48]{0:T(128)S(1)} %bitcast.16, ...), custom_call_target="tpu_custom_call" | custom-call | tf_op jit(solution)/shard_map/pack/pallas_call | solution.py:35
  4.0 0.2 collective-permute-start
  4.2 1.2 %collective-permute-done.xrecv.xgas = f32[2,9,16,128]{3,2,1,0:T(8,128)S(1)} collective-permute-done((f32[2,9,16,128]{3,2,1,0:T(8,128)S(1)}, f32[2,9,16,128]{3,2,1,0:T(8,128)S(1)}, u32[]{:S(2)}, u32[]{:S(2)}) %collective-permute-start) | collective-permute-done | bytes 147488 | tf_op jit(solution)/shard_map/ppermute | solution.py:551
  5.5 2.7 %collective-permute-start.1 = (f32[10,16,128]{2,1,0:T(8,128)S(1)}, f32[10,16,128]{2,1,0:T(8,128)S(1)}, u32[]{:S(2)}, u32[]{:S(2)}) collective-permute-start(f32[10,16,128]{2,1,0:T(8,128)S(1)} %get-tuple-element.28), channel_id=1, source_target_pairs={{0,1},{1,0},{2,3},{3,2},{4,5},{5,4},{6,7},{7,6},{8,9},{9,8},{10,11... | collective-permute-start | bytes 245768 | tf_op jit(solution)/shard_map/ppermute | solution.py:564
  8.2 4.7 %collective-permute-start.2 = (f32[10,16,128]{2,1,0:T(8,128)S(1)}, f32[10,16,128]{2,1,0:T(8,128)S(1)}, u32[]{:S(2)}, u32[]{:S(2)}) collective-permute-start(f32[10,16,128]{2,1,0:T(8,128)S(1)} %get-tuple-element.29), channel_id=1, source_target_pairs={{0,15},{1,2},{2,1},{3,4},{4,3},{5,6},{6,5},{7,8},{8,7},{9,10},{10,... | collective-permute-start | bytes 245768 | tf_op jit(solution)/shard_map/ppermute | solution.py:564
  12.9 7.5 %deposit_own.1.acc_in = f32[336,384]{1,0:T(8,128)S(1)} custom-call(s32[48,128]{1,0:T(8,128)S(1)} %get-tuple-element.30.cells, s32[3,48,128]{2,1,0:T(8,128)S(1)} %get-tuple-element.31.offsets, f32[3,48,128]{2,1,0:T(8,128)S(1)} %get-tuple-element.32.drag, f32[48,128]{1,0:T(8,128)S(1)} %get-tuple-element.23.stays), custom_call_target="tpu_custom_call" | custom-call | flops 4756340736 | bytes 245760 | tf_op jit(solution)/shard_map/deposit_own/pallas_call | solution.py:35
  20.4 0.0 collective-permute-done.1.recv_a.ygas_a
  20.4 0.0 collective-permute-done.2.recv_b.ygas_b
  20.4 2.9 %deposit_arrivals.1 = (f32[336,384]{1,0:T(8,128)S(1)}, f32[256,128]{1,0:T(8,128)S(1)}, f32[328,128]{1,0:T(8,128)S(1)}, f32[328,128]{1,0:T(8,128)S(1)}) custom-call(f32[10,16,128]{2,1,0:T(8,128)S(1)} %collective-permute-done.1.recv_a.ygas_a, f32[10,16,128]{2,1,0:T(8,128)S(1)} %collective-permute-done.2.recv_b.ygas_b, ...), custom_call_target="tpu_custom_call" | custom-call | flops 1585446912 | bytes 81920 | tf_op jit(solution)/shard_map/deposit_arrivals/pallas_call | solution.py:35
  23.4 0.1 collective-permute-start.3
  23.5 1.7 %collective-permute-start.4 = (f32[328,128]{1,0:T(8,128)S(1)}, f32[328,128]{1,0:T(8,128)S(1)}, u32[]{:S(2)}, u32[]{:S(2)}) collective-permute-start(f32[328,128]{1,0:T(8,128)S(1)} %get-tuple-element.38), channel_id=1, source_target_pairs={{0,15},{1,2},{2,1},{3,4},{4,3},{5,6},{6,5},{7,8},{8,7},{9,10},{10,... | collective-permute-start | bytes 503816 | tf_op jit(solution)/shard_map/ppermute | solution.py:564
  25.2 3.1 %tables.1 = (bf16[64,672,128]{2,1,0:T(8,128)(2,1)S(1)}, f32[64,128,128]{2,1,0:T(8,128)S(1)}) custom-call(s32[48,128]{1,0:T(8,128)S(1)} %get-tuple-element.30.cells, s32[3,48,128]{2,1,0:T(8,128)S(1)} %get-tuple-element.31.offsets, f32[256,128]{1,0:T(8,128)S(1)} %get-tuple-element.33.arrivals), custom_call_target="tpu_custom_call" | custom-call | flops 3170893824 | bytes 327680 | tf_op jit(solution)/shard_map/tables/pallas_call | solution.py:35
  28.3 2.3 %collective-permute-done.3.recv_a = f32[328,128]{1,0:T(8,128)S(1)} collective-permute-done((f32[328,128]{1,0:T(8,128)S(1)}, f32[328,128]{1,0:T(8,128)S(1)}, u32[]{:S(2)}, u32[]{:S(2)}) %collective-permute-start.3) | collective-permute-done | bytes 167968 | tf_op jit(solution)/shard_map/ppermute | solution.py:564
  30.6 2.3 %collective-permute-done.4.recv_b = f32[328,128]{1,0:T(8,128)S(1)} collective-permute-done((f32[328,128]{1,0:T(8,128)S(1)}, f32[328,128]{1,0:T(8,128)S(1)}, u32[]{:S(2)}, u32[]{:S(2)}) %collective-permute-start.4) | collective-permute-done | bytes 167968 | tf_op jit(solution)/shard_map/ppermute | solution.py:564
  32.9 0.1 widen.1
  33.0 0.1 collective-permute-start.5
  33.1 2.2 %collective-permute-done.5.xrecv = f32[2,90,8,128]{3,2,1,0:T(8,128)S(1)} collective-permute-done((f32[2,90,8,128]{3,2,1,0:T(8,128)S(1)}, f32[2,90,8,128]{3,2,1,0:T(8,128)S(1)}, u32[]{:S(2)}, u32[]{:S(2)}) %collective-permute-start.5) | collective-permute-done | bytes 737312 | tf_op jit(solution)/shard_map/ppermute | solution.py:551
  35.3 11.0 %finish.1 = (f32[768,128]{1,0:T(8,128)}, f32[3,64,128]{2,1,0:T(8,128)}) custom-call(f32[48,128]{1,0:T(8,128)S(1)} %get-tuple-element.23.stays, f32[3,48,128]{2,1,0:T(8,128)S(1)} %get-tuple-element.24.velocity, f32[768,128]{1,0:T(8,128)S(1)} %get-tuple-element.25.gas, f32[2,9,16,128]{3,2,1,0:T(8,128)S(1)} %collective-permute-done.xrecv.xgas, ...), custom_call_target="tpu_custom_call" | custom-call | flops 6341787648 | bytes 327680 | tf_op jit(solution)/shard_map/finish/pallas_call | solution.py:35
  (1 shorter events, 0.0 us)
Async XLA Ops:
  0.6 0.7 %copy-start = (s32[1,1,48,1]{2,3,1,0:T(1,128)S(1)}, s32[1,1,48,1]{2,3,1,0:T(1,128)}, u32[]{:S(2)}) copy-start(s32[1,1,48,1]{2,3,1,0:T(1,128)} %param.6) | copy-start | bytes 580
  4.0 1.4 %collective-permute-start = (f32[2,9,16,128]{3,2,1,0:T(8,128)S(1)}, f32[2,9,16,128]{3,2,1,0:T(8,128)S(1)}, u32[]{:S(2)}, u32[]{:S(2)}) collective-permute-start(f32[2,9,16,128]{3,2,1,0:T(8,128)S(1)} %get-tuple-element.26), channel_id=1, source_target_pairs={{0,16},{16,0},{1,17},{17,1},{2,18},{18,2},{3,19},{19,3},{4,20},{20... | collective-permute-start | bytes 442376 | tf_op jit(solution)/shard_map/ppermute | solution.py:551
  5.5 14.9 %collective-permute-start.1 = (f32[10,16,128]{2,1,0:T(8,128)S(1)}, f32[10,16,128]{2,1,0:T(8,128)S(1)}, u32[]{:S(2)}, u32[]{:S(2)}) collective-permute-start(f32[10,16,128]{2,1,0:T(8,128)S(1)} %get-tuple-element.28), channel_id=1, source_target_pairs={{0,1},{1,0},{2,3},{3,2},{4,5},{5,4},{6,7},{7,6},{8,9},{9,8},{10,11... | collective-permute-start | bytes 245768 | tf_op jit(solution)/shard_map/ppermute | solution.py:564
  8.2 12.3 %collective-permute-start.2 = (f32[10,16,128]{2,1,0:T(8,128)S(1)}, f32[10,16,128]{2,1,0:T(8,128)S(1)}, u32[]{:S(2)}, u32[]{:S(2)}) collective-permute-start(f32[10,16,128]{2,1,0:T(8,128)S(1)} %get-tuple-element.29), channel_id=1, source_target_pairs={{0,15},{1,2},{2,1},{3,4},{4,3},{5,6},{6,5},{7,8},{8,7},{9,10},{10,... | collective-permute-start | bytes 245768 | tf_op jit(solution)/shard_map/ppermute | solution.py:564
  23.4 7.2 %collective-permute-start.3 = (f32[328,128]{1,0:T(8,128)S(1)}, f32[328,128]{1,0:T(8,128)S(1)}, u32[]{:S(2)}, u32[]{:S(2)}) collective-permute-start(f32[328,128]{1,0:T(8,128)S(1)} %get-tuple-element.37), channel_id=1, source_target_pairs={{0,1},{1,0},{2,3},{3,2},{4,5},{5,4},{6,7},{7,6},{8,9},{9,8},{10,11... | collective-permute-start | bytes 503816 | tf_op jit(solution)/shard_map/ppermute | solution.py:564
  23.5 9.4 %collective-permute-start.4 = (f32[328,128]{1,0:T(8,128)S(1)}, f32[328,128]{1,0:T(8,128)S(1)}, u32[]{:S(2)}, u32[]{:S(2)}) collective-permute-start(f32[328,128]{1,0:T(8,128)S(1)} %get-tuple-element.38), channel_id=1, source_target_pairs={{0,15},{1,2},{2,1},{3,4},{4,3},{5,6},{6,5},{7,8},{8,7},{9,10},{10,... | collective-permute-start | bytes 503816 | tf_op jit(solution)/shard_map/ppermute | solution.py:564
  33.0 2.3 %collective-permute-start.5 = (f32[2,90,8,128]{3,2,1,0:T(8,128)S(1)}, f32[2,90,8,128]{3,2,1,0:T(8,128)S(1)}, u32[]{:S(2)}, u32[]{:S(2)}) collective-permute-start(f32[2,90,8,128]{3,2,1,0:T(8,128)S(1)} %get-tuple-element.41), channel_id=1, source_target_pairs={{0,16},{16,0},{1,17},{17,1},{2,18},{18,2},{3,19},{19,3},{4,20},{20... | collective-permute-start | bytes 2211848 | tf_op jit(solution)/shard_map/ppermute | solution.py:551

commit v3 on v2

v3 whole, which is shorter than its diff:
```python
import functools

import jax
import jax.numpy as jnp
from jax import lax
from jax.experimental import pallas as pl
from jax.experimental.pallas import tpu as pltpu
from jax.sharding import PartitionSpec as P

SWEEPS = 4
CAP = 2
DIFFUSE = 1.0
STEP_SIZE = 2.0

REC = 16
STAY = 4
REACH = SWEEPS + 1
EDGE = REACH + 1
SUB = 8
VMEM = pl.BlockSpec(memory_space=pltpu.VMEM)
SMEM = pl.BlockSpec(memory_space=pltpu.SMEM)
HBM = pl.BlockSpec(memory_space=pltpu.HBM)
ANY = pl.BlockSpec(memory_space=pl.ANY)
F8 = jnp.float8_e4m3fn
PEAK = 400.0
PLANAR_SCALE = 512.0
TINY = 1e-20
COARSE = 256
LIMIT = 24 * 1024 * 1024
COLS = 16


def round_up(count, unit):
    return -(-count // unit) * unit


def call(
    body, outs, args, specs=None, out_specs=None, scratch=(), cost=(0, 0), name=None, results=False
):
    specs = specs or [VMEM] * len(args)
    kind = jax.ShapeDtypeStruct if results else pltpu.VMEM
    return pl.pallas_call(
        body,
        out_shape=[
            kind(*out) if isinstance(out[0], tuple) else kind(out, jnp.float32) for out in outs
        ],
        in_specs=specs,
        out_specs=out_specs or [VMEM] * len(outs),
        scratch_shapes=list(scratch),
        compiler_params=pltpu.CompilerParams(vmem_limit_bytes=LIMIT),
        cost_estimate=pl.CostEstimate(flops=cost[0], bytes_accessed=cost[1], transcendentals=0),
        name=name,
    )(
        *[
            arg if spec in (SMEM, ANY) else pltpu.with_memory_space_constraint(arg, spec.memory_space)
            for arg, spec in zip(args, specs)
        ]
    )


def split_by(value, size):
    if size & (size - 1) == 0:
        return value >> (size.bit_length() - 1), value & (size - 1)
    return value // size, value % size


class Tile:
    def __init__(self, wx, wy, nz):
        self.wx, self.wy, self.nz = wx, wy, nz
        self.ye = wy + 2
        self.hp = round_up(self.ye, SUB)
        self.main = self.ye * wx
        self.rows = self.main + 2 * self.hp
        self.rows8 = round_up(self.rows, 4 * SUB)
        self.yw = wy + 2 * REACH
        self.yp = round_up(self.yw, SUB)
        self.edge_main = EDGE * wx
        self.edge_rows = round_up(3 * (self.edge_main + 2 * EDGE), SUB)

    def decode(self, cell):
        cx, rest = split_by(cell, self.wy * self.nz)
        cy, cz = split_by(rest, self.nz)
        return cx, cy, cz

    def prepare(self, first, cell, sixteenths, fields, columns, force=None):
        count = cell.shape[0]
        cx, cy, cz = self.decode(cell)
        rows = slice(first, first + count)
        fields[0, rows] = cx.astype(jnp.float32)
        fields[1, rows] = cy.astype(jnp.float32)
        for axis in range(2):
            scale = 1.0 if axis else PLANAR_SCALE
            for i, weight in enumerate(tsc_weights(sixteenths[axis])):
                fields[2 + 3 * axis + i, rows] = weight * scale
        below = jnp.where(cz == 0, self.nz - 1, cz - 1).astype(jnp.float32)
        above = jnp.where(cz == self.nz - 1, 0, cz + 1).astype(jnp.float32)
        values = [below, cz.astype(jnp.float32), above, *tsc_weights(sixteenths[2])]
        if force is not None:
            values += force
        for i, value in enumerate(values):
            columns[pl.ds(first * COLS + i, count, stride=COLS), :] = value

    def vertical(self, columns, slot):
        start = pl.multiple_of(slot * COLS, COLS)
        rows = [columns[pl.ds(start, COLS), :][j : j + 1] for j in range(9)]
        iz = lax.broadcasted_iota(jnp.int32, (self.nz, rows[0].shape[1]), 0).astype(jnp.float32)
        tz = jnp.where(iz == rows[2], rows[5], 0.0)
        tz = jnp.where(iz == rows[1], rows[4], tz)
        return jnp.where(iz == rows[0], rows[3], tz), rows[6:9]

    def planar(self, fields, slot):
        lanes = fields.shape[2]
        cx, cy, *weights = [fields[i, pl.ds(slot, 1), :] for i in range(8)]
        ix = lax.broadcasted_iota(jnp.int32, (self.wx, lanes), 0).astype(jnp.float32)
        tx = jnp.where(ix == cx + 1.0, weights[2], 0.0)
        tx = jnp.where(ix == cx, weights[1], tx)
        tx = jnp.where(ix == cx - 1.0, weights[0], tx)
        iy = lax.broadcasted_iota(jnp.int32, (self.hp, lanes), 0).astype(jnp.float32)
        ty = jnp.where(iy == cy + 2.0, weights[5], 0.0)
        ty = jnp.where(iy == cy + 1.0, weights[4], ty)
        ty = jnp.where(iy == cy, weights[3], ty)
        beyond_low = jnp.where(cx == 0.0, weights[0], 0.0)
        beyond_high = jnp.where(cx == self.wx - 1.0, weights[2], 0.0)
        parts = [
            jnp.concatenate([tx * ty[j : j + 1], tx * ty[j + 1 : j + 2]], axis=0)
            for j in range(0, self.ye, 2)
        ]
        return parts + [jnp.concatenate([ty * beyond_low, ty * beyond_high], axis=0)]


def tsc_weights(sixteenths):
    fraction = (sixteenths + 0.5) * (1.0 / 16.0) - 0.5
    low = 0.5 - fraction
    high = 0.5 + fraction
    return 0.5 * low * low, 0.75 - fraction * fraction, 0.5 * high * high


def halves(value):
    top = value.astype(jnp.bfloat16)
    return top, value - top.astype(jnp.float32)


def scaled(values, bound):
    peak = functools.reduce(jnp.maximum, [jnp.abs(value) for value in values])
    peak = jnp.maximum(jnp.max(peak, keepdims=True), TINY)
    factor = (PEAK / bound) / peak
    return [value * factor for value in values], peak * (bound / PEAK)


def pipeline(steps, build, use):
    build(0, 0)
    assert steps % 2 == 0

    def pair(i, carry):
        use(0, 2 * i)
        build(1, 2 * i + 1)
        use(1, 2 * i + 1)
        build(0, 2 * i + 2)
        return carry

    lax.fori_loop(0, steps // 2 - 1, pair, 0, unroll=True)
    use(0, steps - 2)
    build(1, steps - 1)
    use(1, steps - 1)


def deposit(tile, slots, fields, columns, acc, cross, left, left8, right, right8):
    def build(buffer, step):
        for i in range(2):
            slot = step * 2 + i
            row = 0
            for part in tile.planar(fields, slot):
                top, low = halves(part)
                rows = slice(row, row + part.shape[0])
                left[buffer][i, rows] = top
                left8[buffer][i, rows] = part.astype(F8)
                left8[buffer][2 + i, rows] = low.astype(F8)
                row += part.shape[0]
            tz, force = tile.vertical(columns, slot)
            for k in range(3):
                value = (tz * force[k]).T
                top, low = halves(value)
                right[buffer][3 * i + k] = top
                right8[buffer][3 * i + k] = low.astype(F8)
                right8[buffer][3 * (2 + i) + k] = value.astype(F8)

    def use(buffer, step):
        def pieces(a_ref, b_ref, count):
            b = [jnp.concatenate([b_ref[3 * i + k] for k in range(3)], axis=1) for i in range(count)]
            return jnp.dot(
                jnp.concatenate([a_ref[i] for i in range(count)], axis=1),
                jnp.concatenate(b, axis=0),
                preferred_element_type=jnp.float32,
            )

        acc[...] += pieces(left[buffer], right[buffer], 2)
        cross[...] += pieces(left8[buffer], right8[buffer], 4)

    pipeline(slots // 2, build, use)


def ty_roles(axis, count):
    if count % 2:
        return True, False
    even = lax.axis_index(axis) % 2 == 0
    return even, even


def if_(cond, then, other):
    if isinstance(cond, bool):
        (then if cond else other)()
        return
    pl.when(cond)(then)
    pl.when(jnp.logical_not(cond))(other)


def pack_kernel(
    tile, axis, count, slots, codes_in, cells_in, offsets_in, drag_in, velocity_in, gas_in,
    send_a, send_b, own, stays, cells, offsets, drag, velocity, gas, codes, leaving, counts, sems,
):
    sources = (codes_in, cells_in, offsets_in, drag_in, velocity_in, gas_in)
    targets = (codes, cells, offsets, drag, velocity, gas)
    copies = [
        pltpu.make_async_copy(source, target, sems.at[i])
        for i, (source, target) in enumerate(zip(sources, targets))
    ]
    for copy in copies:
        copy.start()
    for ref in (send_a, send_b):
        ref[: 3 * CAP] = jnp.zeros((3 * CAP, REC, 128), jnp.float32)
    own[...] = jnp.zeros(own.shape, jnp.float32)
    for code in range(9):
        counts[code] = 0
    copies[0].wait()
    total = 0
    for slot in range(slots):
        code = codes[slot]
        stays[slot : slot + 1] = jnp.full((1, 128), (code == STAY).astype(jnp.float32), jnp.float32)
        leaving[total] = slot
        total = total + (code != STAY).astype(jnp.int32)
    for copy in copies[1:]:
        copy.wait()
    a_high, _ = ty_roles(axis, count)
    per = tile.wx // REC

    def edges(ref, high):
        y = tile.wy - 1 if high else 0
        for k in range(3):
            for part in range(per):
                start = (k * tile.wx + part * REC) * tile.wy + y
                ref[3 * CAP + k * per + part] = gas[pl.ds(start, REC, stride=tile.wy), :]

    def visit(index, carry):
        slot = leaving[index]
        code = codes[slot]
        rank = jnp.minimum(counts[code], CAP - 1)
        counts[code] = rank + 1
        here = pl.ds(slot, 1)

        def put(ref):
            for k in range(3):
                ref[k : k + 1] = drag[k, here]
                ref[3 + k : 4 + k] = velocity[k, here]
                ref[7 + k : 8 + k] = offsets[k, here].astype(jnp.float32)
            ref[6:7] = cells[here].astype(jnp.float32)
            ref[10:11] = jnp.ones((1, 128), jnp.float32)

        row = (code >= 3).astype(jnp.int32) + (code >= 6).astype(jnp.int32)
        column = code - 3 * row
        to_a = (column == 2) == a_high
        place = row * CAP + rank
        pl.when(column == 1)(lambda: put(own.at[(row >= 1).astype(jnp.int32), rank]))
        pl.when((column != 1) & to_a)(lambda: put(send_a.at[place]))
        pl.when((column != 1) & jnp.logical_not(to_a))(lambda: put(send_b.at[place]))
        return carry

    lax.fori_loop(0, total, visit, 0)
    if_(
        a_high,
        lambda: (edges(send_a, True), edges(send_b, False)) and None,
        lambda: (edges(send_a, False), edges(send_b, True)) and None,
    )


def join_kernel(tile, axis, count, recv_a, recv_b, own, gas, acc, xsend):
    _, a_from_high = ty_roles(axis, count)
    per_x, per_y = tile.wx // REC, tile.wy // REC
    corner = 3 * CAP + 3 * per_y
    for side, x in ((0, 0), (1, tile.wx - 1)):
        xsend[side, corner] = jnp.zeros((REC, 128), jnp.float32)
        for s in range(CAP):
            xsend[side, CAP + s] = own[side, s]
        for k in range(3):
            for part in range(per_y):
                start = (k * tile.wx + x) * tile.wy + part * REC
                xsend[side, 3 * CAP + k * per_y + part] = gas[start : start + REC]

    def forward(ref, high):
        first = 2 * CAP if high else 0
        for side, x in ((0, 0), (1, tile.wx - 1)):
            for s in range(CAP):
                xsend[side, first + s] = ref[2 * CAP * side + s]
            for k in range(3):
                place = 3 * CAP + k * per_x + x // REC
                row = 2 * k + int(high)
                xsend[side, corner, row : row + 1] = ref[place, x % REC : x % REC + 1]

    if_(
        a_from_high,
        lambda: (forward(recv_a, True), forward(recv_b, False)) and None,
        lambda: (forward(recv_a, False), forward(recv_b, True)) and None,
    )


def table_scratch(tile, slots):
    rows, turned = (tile.rows, 128), (128, tile.nz)
    return [
        pltpu.VMEM((8, slots, 128), jnp.float32),
        pltpu.VMEM((slots * COLS, 128), jnp.float32),
        *[pltpu.VMEM((2, *rows), jnp.bfloat16)] * 2,
        *[pltpu.VMEM((4, tile.rows8, 128), F8)] * 2,
        *[pltpu.VMEM((6, *turned), jnp.bfloat16)] * 2,
        *[pltpu.VMEM((12, *turned), F8)] * 2,
        pltpu.VMEM((tile.rows8, 3 * tile.nz), jnp.float32),
    ]


def deposit_blocks(tile, cell, sixteenths, force, acc, fields, columns, *buffers):
    acc[...] = jnp.zeros(acc.shape, jnp.float32)
    columns[...] = jnp.zeros(columns.shape, jnp.float32)
    force, factor = scaled(force, 0.75)
    tile.prepare(0, cell, sixteenths, fields, columns, force)
    cross = buffers[8]
    cross[...] = jnp.zeros(cross.shape, jnp.float32)
    pairs = [buffers[i : i + 2] for i in range(0, 8, 2)]
    for buffer in pairs[1]:
        buffer[:, tile.rows :] = jnp.zeros((4, tile.rows8 - tile.rows, 128), F8)
    deposit(tile, cell.shape[0], fields, columns, acc, cross, *pairs)
    acc[...] += cross[: tile.rows]
    return factor * (1.0 / PLANAR_SCALE)


def own_blocks(tile, first, count, cells, offsets, drag, stays, acc, *scratch):
    rows = slice(first, first + count)
    sixteenths = [offsets[k, rows].astype(jnp.float32) for k in range(3)]
    force = [drag[k, rows] * stays[rows] for k in range(3)]
    return deposit_blocks(tile, cells[rows], sixteenths, force, acc, *scratch)


def first_kernel(tile, count, cells, offsets, drag, stays, acc, *scratch):
    factor = own_blocks(tile, 0, count, cells, offsets, drag, stays, acc, *scratch)
    acc[...] = acc[...] * factor


def second_kernel(tile, first, count, cells, offsets, drag, stays, acc_in, xsend, acc, *scratch):
    factor = own_blocks(tile, first, count, cells, offsets, drag, stays, acc, *scratch)
    acc[...] = acc_in[...] + acc[...] * factor


def record_row(records, row, count):
    return records[pl.ds(row, count, stride=REC), :]


def arrive_kernel(
    tile, axis, count, recv_a, recv_b, xrecv, acc_in, acc, arrivals, send_a, send_b, *scratch
):
    a_high, a_from_high = ty_roles(axis, count)

    def place(j, record):
        arrivals[j * REC : (j + 1) * REC] = record

    for i in range(3 * CAP):
        place(i, xrecv[1, i])
        place(5 * CAP + i, xrecv[0, i])

    def middle(ref, j):
        for s in range(CAP):
            place(j * CAP + s, ref[CAP + s])

    if_(
        a_from_high,
        lambda: (middle(recv_a, 4), middle(recv_b, 3)) and None,
        lambda: (middle(recv_a, 3), middle(recv_b, 4)) and None,
    )
    blocks = 8 * CAP
    live = record_row(arrivals, 10, blocks)
    force = [record_row(arrivals, k, blocks) * live for k in range(3)]
    sixteenths = [record_row(arrivals, 7 + k, blocks) for k in range(3)]
    cell = record_row(arrivals, 6, blocks).astype(jnp.int32)
    factor = deposit_blocks(tile, cell, sixteenths, force, acc, *scratch)
    acc[...] = acc_in[...] + acc[...] * factor

    def edge(ref, high):
        first = tile.ye - EDGE if high else 0
        tail = 3 * tile.edge_main
        for k in range(3):
            lanes = slice(k * tile.nz, (k + 1) * tile.nz)
            ref[k * tile.edge_main : (k + 1) * tile.edge_main] = acc[
                first * tile.wx : (first + EDGE) * tile.wx, lanes
            ]
            for h in range(2):
                start = tile.main + h * tile.hp + first
                row = tail + (2 * k + h) * EDGE
                ref[row : row + EDGE] = acc[start : start + EDGE, lanes]

    def even():
        edge(send_a, True)
        edge(send_b, False)

    def odd():
        edge(send_a, False)
        edge(send_b, True)

    for ref in (send_a, send_b):
        last = tile.edge_rows - SUB
        ref[last:] = jnp.zeros((SUB, tile.nz), jnp.float32)
    if_(a_high, even, odd)


def widen_kernel(tile, axis, count, acc, recv_a, recv_b, verticals, mid, beyond, xsend):
    _, a_from_high = ty_roles(axis, count)
    own = slice(REACH - 1, REACH - 1 + tile.ye)
    for k in range(3):
        lanes = slice(k * tile.nz, (k + 1) * tile.nz)
        zero = jnp.zeros((REACH - 1, tile.wx, tile.nz), jnp.float32)
        mid[k, : REACH - 1] = zero
        mid[k, REACH - 1 + tile.ye :] = zero
        mid[k, own] = acc[: tile.main, lanes].reshape(tile.ye, tile.wx, tile.nz)
        for h in range(2):
            start = tile.main + h * tile.hp
            beyond[k, h] = jnp.zeros((tile.yp, tile.nz), jnp.float32)
            beyond[k, h, own] = acc[start : start + tile.ye, lanes]

    def add(ref, high):
        first = tile.yw - EDGE if high else 0
        tail = 3 * tile.edge_main
        for k in range(3):
            rows = ref[k * tile.edge_main : (k + 1) * tile.edge_main]
            mid[k, first : first + EDGE] += rows.reshape(EDGE, tile.wx, tile.nz)
            for h in range(2):
                row = tail + (2 * k + h) * EDGE
                beyond[k, h, first : first + EDGE] += ref[row : row + EDGE]

    if_(
        a_from_high,
        lambda: (add(recv_a, True), add(recv_b, False)) and None,
        lambda: (add(recv_a, False), add(recv_b, True)) and None,
    )
    for k in range(3):
        for y in range(tile.yw):
            row = (k * tile.yw + y) * EDGE
            xsend[0, row : row + 1] = beyond[k, 0, y : y + 1]
            xsend[0, row + 1 : row + EDGE] = mid[k, y, :REACH]
            xsend[1, row : row + REACH] = mid[k, y, tile.wx - REACH :]
            xsend[1, row + REACH : row + EDGE] = beyond[k, 1, y : y + 1]


def tables_kernel(
    tile, slots, cells, offsets, arrivals, tables, tables8, verticals, fields, columns
):
    blocks = 8 * CAP
    tile.prepare(0, cells[...], [offsets[k].astype(jnp.float32) for k in range(3)], fields, columns)
    sixteenths = [record_row(arrivals, 7 + k, blocks) for k in range(3)]
    cell = record_row(arrivals, 6, blocks).astype(jnp.int32)
    tile.prepare(slots, cell, sixteenths, fields, columns)

    def build(pair, carry):
        for i in range(2):
            slot = pair * 2 + i
            row = 0
            for part in tile.planar(fields, slot):
                top, low = halves(part)
                count = part.shape[0]
                tables[slot, row : row + count] = top
                if row < COARSE:
                    tables8[slot, row : row + count] = part.astype(F8)
                    tables8[slot, COARSE + row : COARSE + row + count] = low.astype(F8)
                else:
                    down = tile.rows - COARSE + row
                    tables[slot, down : down + count] = low.astype(jnp.bfloat16)
                row += count
            verticals[slot], _ = tile.vertical(columns, slot)
        return carry

    lax.fori_loop(0, (slots + blocks) // 2, build, 0)


def finish_kernel(
    tile, axis, count, slots, stays, velocity, gas, xgas, ygas_a, ygas_b, arrivals,
    tables, tables8, verticals, mid, beyond, xrecv, gas_out, slip,
    src, ping, pong, field, field8, stack, gas_new, sem,
):
    _, a_from_high = ty_roles(axis, count)
    zero = SUB + SWEEPS
    after = zero + tile.wx
    swept = tile.wx + 2 * SWEEPS
    for k in range(3):
        for y in range(tile.yw):
            row = (k * tile.yw + y) * EDGE
            src[k, y, zero - SUB : zero] = jnp.zeros((SUB, tile.nz), jnp.float32)
            src[k, y, zero:after] = mid[k, y]
            src[k, y, after : after + SUB] = jnp.zeros((SUB, tile.nz), jnp.float32)
            src[k, y, zero - REACH : zero] = xrecv[1, row : row + REACH]
            src[k, y, after : after + REACH] = xrecv[0, row + 1 : row + EDGE]
            src[k, y, zero - 1 : zero] += beyond[k, 0, y : y + 1]
            src[k, y, after : after + 1] += beyond[k, 1, y : y + 1]
            src[k, y, zero : zero + 1] += xrecv[1, row + REACH : row + EDGE]
            src[k, y, after - 1 : after] += xrecv[0, row : row + 1]

    def sweep(old, new, margin):
        def row(y, carry):
            for k in range(3):
                here = old[k, y, SUB : SUB + swept]
                around = old[k, y - 1, SUB : SUB + swept] + old[k, y + 1, SUB : SUB + swept]
                around = around + old[k, y, SUB - 1 : SUB - 1 + swept]
                around = around + old[k, y, SUB + 1 : SUB + 1 + swept]
                around = around + pltpu.roll(here, 1, 1) + pltpu.roll(here, tile.nz - 1, 1)
                total = src[k, y, SUB : SUB + swept] + DIFFUSE * around
                new[k, y, SUB : SUB + swept] = total * (1.0 / (1.0 + 6.0 * DIFFUSE))
            return carry

        rows = tile.yw - 2 * margin
        lax.fori_loop(margin, tile.yw - margin, row, 0, unroll=rows // 2)

    buffers = [src, ping, pong, ping, pong]
    for index in range(SWEEPS):
        sweep(buffers[index], buffers[index + 1], index + 1)
    filtered = buffers[SWEEPS]

    per_x, per_y = tile.wx // REC, tile.wy // REC

    def take_edges(ref, high):
        y = tile.ye - 1 if high else 0
        for k in range(3):
            for part in range(per_x):
                row = y * tile.wx + part * REC
                stack[k, row : row + REC] = ref[3 * CAP + k * per_x + part]
    for k in range(3):
        for h in range(2):
            start = tile.main + h * tile.hp
            stack[k, start : start + tile.hp] = jnp.zeros((tile.hp, tile.nz), jnp.float32)
            for part in range(per_y):
                row = start + 1 + part * REC
                stack[k, row : row + REC] = xgas[1 - h, 3 * CAP + k * per_y + part]
            corner = 3 * CAP + 3 * per_y
            stack[k, start : start + 1] = xgas[1 - h, corner, 2 * k : 2 * k + 1]
            last = start + tile.ye - 1
            stack[k, last : last + 1] = xgas[1 - h, corner, 2 * k + 1 : 2 * k + 2]
        for y in range(tile.wy):
            stack[k, (y + 1) * tile.wx : (y + 2) * tile.wx] = gas[
                pl.ds(k * tile.wx * tile.wy + y, tile.wx, stride=tile.wy), :
            ]
    if_(
        a_from_high,
        lambda: (take_edges(ygas_a, True), take_edges(ygas_b, False)) and None,
        lambda: (take_edges(ygas_a, False), take_edges(ygas_b, True)) and None,
    )
    for k in range(3):
        for y in range(tile.ye):
            rows = slice(y * tile.wx, (y + 1) * tile.wx)
            updated = stack[k, rows] + STEP_SIZE * filtered[k, y + REACH - 1, zero:after]
            stack[k, rows] = updated
            if 1 <= y <= tile.wy:
                gas_new[pl.ds(k * tile.wx * tile.wy + y - 1, tile.wx, stride=tile.wy), :] = updated
            for h, x in ((0, zero - 1), (1, after)):
                row = tile.main + h * tile.hp + y
                stack[k, row : row + 1] += STEP_SIZE * filtered[k, y + REACH - 1, x : x + 1]
    leave = pltpu.make_async_copy(gas_new, gas_out, sem)
    leave.start()
    blocks = 8 * CAP
    total = slots + blocks
    fine = tile.rows - COARSE
    pad_rows = round_up(3 * fine, 128) - 3 * fine
    values, factor = scaled([stack[k] for k in range(3)], 1.0)
    for k, value in enumerate(values):
        top = value.astype(jnp.bfloat16).astype(jnp.float32)
        low = value - top
        pad = jnp.zeros((pad_rows, tile.nz), jnp.float32)
        exact = jnp.concatenate([top, top[COARSE:], low[COARSE:], pad], axis=0).T
        cross = jnp.concatenate([low[:COARSE], value[:COARSE]], axis=0).T
        rows = slice(k * tile.nz, (k + 1) * tile.nz)
        for i in range(field.shape[0]):
            field[i, rows] = exact[:, i * 128 : (i + 1) * 128].astype(jnp.bfloat16)
        for i in range(field8.shape[0]):
            field8[i, rows] = cross[:, i * 128 : (i + 1) * 128].astype(F8)
    factor = factor * (1.0 / PLANAR_SCALE)

    def sample(pair, carry):
        pad = jnp.zeros((pad_rows, 128), jnp.bfloat16)
        slabs = [tables[pair * 2 + i] for i in range(2)]
        slabs = [jnp.concatenate([slab, slab[COARSE : tile.rows], pad], axis=0) for slab in slabs]
        column = jnp.dot(
            jnp.concatenate([field[i] for i in range(field.shape[0])], axis=1),
            jnp.concatenate(slabs, axis=1),
            preferred_element_type=jnp.float32,
        )
        column = column + jnp.dot(
            jnp.concatenate([field8[i] for i in range(field8.shape[0])], axis=1),
            jnp.concatenate([tables8[pair * 2 + i] for i in range(2)], axis=1),
            preferred_element_type=jnp.float32,
        )
        for i in range(2):
            vertical = verticals[pair * 2 + i]
            for k in range(3):
                part = column[k * tile.nz : (k + 1) * tile.nz, i * 128 : (i + 1) * 128]
                value = jnp.sum(part * vertical, axis=0, keepdims=True)
                slip[k, pl.ds(pair * 2 + i, 1)] = value
        return carry

    lax.fori_loop(0, total // 2, sample, 0, unroll=8)
    live = record_row(arrivals, 10, blocks)
    for k in range(3):
        slip[k, :slots] = (slip[k, :slots] * factor - velocity[k]) * stays[...]
        slip[k, slots:] = (slip[k, slots:] * factor - record_row(arrivals, 3 + k, blocks)) * live
    leave.wait()


def exchange_x(buffer, axis, count):
    forward = [(i, (i + 1) % count) for i in range(count)]
    backward = [(target, source) for source, target in forward]
    if count == 2:
        return lax.ppermute(buffer, axis, forward)
    return jnp.stack(
        [lax.ppermute(buffer[0], axis, backward), lax.ppermute(buffer[1], axis, forward)]
    )


def exchange_y(send_a, send_b, axis, count):
    if count % 2:
        perm_a = [(i, (i + 1) % count) for i in range(count)]
        perm_b = [(target, source) for source, target in perm_a]
    else:
        perm_a = [(i, i ^ 1) for i in range(count)]
        perm_b = [(i, (i + 1) % count if i % 2 else (i - 1) % count) for i in range(count)]
    return lax.ppermute(send_a, axis, perm_a), lax.ppermute(send_b, axis, perm_b)


def on_device(count_x, count_y, handoff, cells, offsets, drag, bubble_velocity, gas):
    tile = Tile(gas.shape[1], gas.shape[2], gas.shape[3])
    slots, lanes = cells.shape[2], cells.shape[3]
    codes = handoff.reshape(slots)
    cells = cells.reshape(slots, lanes)
    offsets = offsets.reshape(slots, 3, lanes).transpose(1, 0, 2)
    drag = drag.reshape(slots, 3, lanes).transpose(1, 0, 2)
    velocity = bubble_velocity.reshape(slots, 3, lanes).transpose(1, 0, 2)
    gas_rows = gas.reshape(3 * tile.wx * tile.wy, tile.nz)
    per_x, per_y = tile.wx // REC, tile.wy // REC
    bind = functools.partial
    macs = tile.rows * 3 * tile.nz * 3 * 2 * lanes

    inputs = [cells, offsets, drag, velocity, gas_rows]
    ty_shape = (3 * CAP + 3 * per_x, REC, lanes)
    send_a, send_b, own, stays, cells, offsets, drag, velocity, gas_rows = call(
        bind(pack_kernel, tile, "ty", count_y, slots),
        [ty_shape, ty_shape, (2, CAP, REC, lanes), (slots, lanes)]
        + [(value.shape, value.dtype) for value in inputs],
        [codes, *inputs],
        [HBM] * 6,
        scratch=[
            pltpu.SMEM((slots,), jnp.int32),
            pltpu.SMEM((slots + 1,), jnp.int32),
            pltpu.SMEM((9,), jnp.int32),
            pltpu.SemaphoreType.DMA((6,)),
        ],
        name="pack",
    )
    recv_a, recv_b = exchange_y(send_a, send_b, "ty", count_y)
    cut = slots * 2 // 3 // 4 * 4
    (acc,) = call(
        bind(first_kernel, tile, cut),
        [(tile.rows, 3 * tile.nz)],
        [cells, offsets, drag, stays],
        scratch=table_scratch(tile, cut),
        cost=(macs * cut, cut * lanes * 40),
        name="deposit_first",
    )
    (xsend,) = call(
        bind(join_kernel, tile, "ty", count_y),
        [(2, 3 * CAP + 3 * per_y + 1, REC, lanes)],
        [recv_a, recv_b, own, gas_rows, acc],
        [VMEM] * 4 + [ANY],
        name="join",
    )
    xrecv = exchange_x(xsend, "tx", count_x)
    (acc,) = call(
        bind(second_kernel, tile, cut, slots - cut),
        [acc.shape],
        [cells, offsets, drag, stays, acc, xsend],
        [VMEM] * 5 + [ANY],
        scratch=table_scratch(tile, slots - cut),
        cost=(macs * (slots - cut), (slots - cut) * lanes * 40),
        name="deposit_second",
    )
    edge_shape = (tile.edge_rows, tile.nz)
    blocks = 8 * CAP
    acc, arrivals, edge_a, edge_b = call(
        bind(arrive_kernel, tile, "ty", count_y),
        [acc.shape, (blocks * REC, lanes), edge_shape, edge_shape],
        [recv_a, recv_b, xrecv, acc],
        scratch=table_scratch(tile, blocks),
        cost=(macs * blocks, blocks * lanes * 40),
        name="deposit_arrivals",
    )
    got_a, got_b = exchange_y(edge_a, edge_b, "ty", count_y)
    total = slots + blocks
    fine = tile.rows - COARSE
    tables, tables8, verticals = call(
        bind(tables_kernel, tile, slots),
        [
            ((total, tile.rows + fine, lanes), jnp.bfloat16),
            ((total, 2 * COARSE, lanes), F8),
            (total, tile.nz, lanes),
        ],
        [cells, offsets, arrivals],
        scratch=[
            pltpu.VMEM((8, total, lanes), jnp.float32),
            pltpu.VMEM((total * COLS, lanes), jnp.float32),
        ],
        cost=(macs * total // 2, total * lanes * 40),
        name="tables",
    )
    mid, beyond, xedge = call(
        bind(widen_kernel, tile, "ty", count_y),
        [
            (3, tile.yw, tile.wx, tile.nz),
            (3, 2, tile.yp, tile.nz),
            (2, round_up(3 * tile.yw * EDGE, SUB), tile.nz),
        ],
        [acc, got_a, got_b, verticals],
        [VMEM] * 3 + [ANY],
        name="widen",
    )
    xgot = exchange_x(xedge, "tx", count_x)
    wide = (3, tile.yw, round_up(tile.wx + SUB + SWEEPS + SUB, SUB), tile.nz)
    gas_new, slip = call(
        bind(finish_kernel, tile, "ty", count_y, slots),
        [gas_rows.shape, (3, total, lanes)],
        [stays, velocity, gas_rows, xrecv, recv_a, recv_b, arrivals]
        + [tables, tables8, verticals, mid, beyond, xgot],
        scratch=[
            *[pltpu.VMEM(wide, jnp.float32)] * 3,
            pltpu.VMEM(((COARSE + round_up(3 * fine, 128)) // 128, 3 * tile.nz, 128), jnp.bfloat16),
            pltpu.VMEM((2 * COARSE // 128, 3 * tile.nz, 128), F8),
            pltpu.VMEM((3, tile.rows, tile.nz), jnp.float32),
            pltpu.VMEM(gas_rows.shape, jnp.float32),
            pltpu.SemaphoreType.DMA(()),
        ],
        out_specs=[HBM, VMEM],
        cost=(macs * total, total * lanes * 40),
        name="finish",
        results=True,
    )
    return gas_new.reshape(gas.shape), slip.transpose(1, 0, 2).reshape(1, 1, total, 3, lanes)


def solution(mesh):
    return jax.shard_map(
        functools.partial(on_device, mesh.shape["tx"], mesh.shape["ty"]),
        mesh=mesh,
        in_specs=(
            P("tx", "ty", None, None),
            P("tx", "ty", None, None),
            P("tx", "ty", None, None, None),
            P("tx", "ty", None, None, None),
            P("tx", "ty", None, None, None),
            P(None, "tx", "ty", None),
        ),
        out_specs=(P(None, "tx", "ty", None), P("tx", "ty", None, None, None)),
        check_vma=False,
    )
```

time: 46.5 us -> 42.9 us (0.923)
  waiting for transfers between devices: 8.04 us -> 5.49 us
  Pallas kernels: 27.4 us -> 25.5 us
  starting transfers between devices: 9.52 us -> 10.9 us
  local copies, waits for them, and re-layouts: 0.65 us -> 0 us
    pallas_call x7 -> x8, Pallas kernels: 27.4 us -> 25.5 us  [call(): pl.pallas_call(body, out_shape=[kind(*out) if isinstance(out[0], tuple) e...]
    ppermute x2, waiting for transfers between devices: 3.43 us -> 1.84 us  [exchange_x(): return lax.ppermute(buffer, axis, forward)]
    ppermute x2, starting transfers between devices: 6.47 us -> 7.45 us  [exchange_y(): lax.ppermute(send_b, axis, perm_b)]
    ppermute x2, waiting for transfers between devices: 2.34 us -> 1.37 us  [exchange_y(): lax.ppermute(send_a, axis, perm_a)]
    unnamed x2 -> x0, local copies, waits for them, and re-layouts: 0.65 us -> none
    ppermute x2, starting transfers between devices: 2.77 us -> 3.26 us  [exchange_y(): lax.ppermute(send_a, axis, perm_a)]
  transfers between devices with their start and end apart: 6 -> 6, of which waited for: 4 -> 3; matrix products, arithmetic and copies ran while one was open for 0% -> 0% of each run, Pallas kernels for 23% -> 25%
where the time goes in v3:
time: 42.9 us; the launch traced here: 42.6 us
  Pallas kernels  25.5 us (59%)
  starting transfers between devices  10.9 us (25%)
  waiting for transfers between devices  5.49 us (13%)
  between operations  0.73 us (2%)
    pallas_call x8, Pallas kernels, call(): pl.pallas_call(body, out_shape=[kind(*out) if isinstance(out[0], tuple) e...  25.5 us
    ppermute x2, starting transfers between devices, exchange_y(): lax.ppermute(send_b, axis, perm_b)  7.45 us
    ppermute x2, starting transfers between devices, exchange_y(): lax.ppermute(send_a, axis, perm_a)  3.26 us
    ppermute x2, waiting for transfers between devices, exchange_y(): lax.ppermute(send_b, axis, perm_b)  2.27 us
    ppermute x2, waiting for transfers between devices, exchange_x(): return lax.ppermute(buffer, axis, forward)  1.84 us
    ppermute x2, waiting for transfers between devices, exchange_y(): lax.ppermute(send_a, axis, perm_a)  1.37 us
  transfers between devices with their start and end apart: 6, of which 3 were waited for; matrix products, arithmetic and copies ran while one was open for 0% of the time, Pallas kernels for 25%

profile of v3, /device:TPU:0, one launch (start us, length us, event | category | flops | bytes accessed | tf_op | source)
XLA Modules:
  0.0 42.6 jit_solution(16159053142380117495)
XLA Ops:
  0.6 1.5 %pack.1 = (f32[9,16,128]{2,1,0:T(8,128)S(1)}, f32[9,16,128]{2,1,0:T(8,128)S(1)}, f32[2,2,16,128]{3,2,1,0:T(8,128)S(1)}, f32[48,128]{1,0:T(8,128)S(1)}, s32[48,12...) custom-call(s32[48]{0:T(128)} %bitcast.21, ...), custom_call_target="tpu_custom_call" | custom-call | tf_op jit(solution)/shard_map/pack/pallas_call | solution.py:42
  2.1 3.2 %collective-permute-start = (f32[9,16,128]{2,1,0:T(8,128)S(1)}, f32[9,16,128]{2,1,0:T(8,128)S(1)}, u32[]{:S(2)}, u32[]{:S(2)}) collective-permute-start(f32[9,16,128]{2,1,0:T(8,128)S(1)} %get-tuple-element.26), channel_id=1, source_target_pairs={{0,1},{1,0},{2,3},{3,2},{4,5},{5,4},{6,7},{7,6},{8,9},{9,8},{10,11... | collective-permute-start | bytes 221192 | tf_op jit(solution)/shard_map/ppermute | solution.py:635
  5.3 4.2 %collective-permute-start.1 = (f32[9,16,128]{2,1,0:T(8,128)S(1)}, f32[9,16,128]{2,1,0:T(8,128)S(1)}, u32[]{:S(2)}, u32[]{:S(2)}) collective-permute-start(f32[9,16,128]{2,1,0:T(8,128)S(1)} %get-tuple-element.27), channel_id=1, source_target_pairs={{0,15},{1,2},{2,1},{3,4},{4,3},{5,6},{6,5},{7,8},{8,7},{9,10},{10,... | collective-permute-start | bytes 221192 | tf_op jit(solution)/shard_map/ppermute | solution.py:635
  9.5 4.7 %deposit_first.1.acc.acc_in = f32[336,384]{1,0:T(8,128)S(1)} custom-call(s32[48,128]{1,0:T(8,128)S(1)} %get-tuple-element.29.cells, s32[3,48,128]{2,1,0:T(8,128)S(1)} %get-tuple-element.30.offsets, f32[3,48,128]{2,1,0:T(8,128)S(1)} %get-tuple-element.31.drag, f32[48,128]{1,0:T(8,128)S(1)} %get-tuple-element.23.stays), custom_call_target="tpu_custom_call" | custom-call | flops 3170893824 | bytes 163840 | tf_op jit(solution)/shard_map/deposit_first/pallas_call | solution.py:42
  14.2 0.0 collective-permute-done.recv_a.ygas_a
  14.2 0.0 collective-permute-done.1.recv_b.ygas_b
  14.2 0.1 collective-permute-start.2
  14.3 2.7 %deposit_second.1.acc_in = f32[336,384]{1,0:T(8,128)S(1)} custom-call(s32[48,128]{1,0:T(8,128)S(1)} %get-tuple-element.29.cells, s32[3,48,128]{2,1,0:T(8,128)S(1)} %get-tuple-element.30.offsets, f32[3,48,128]{2,1,0:T(8,128)S(1)} %get-tuple-element.31.drag, f32[48,128]{1,0:T(8,128)S(1)} %get-tuple-element.23.stays, f32[336,384]{1,0:T(8,128)S(1)} %deposit_first.1.acc.acc_in, ...), custom_call_target="tpu_custom_call" | custom-call | flops 1585446912 | bytes 81920 | tf_op jit(solution)/shard_map/deposit_second/pallas_call | solution.py:42
  17.0 0.0 collective-permute-done.2.xrecv.xgas
  17.0 2.8 %deposit_arrivals.1 = (f32[336,384]{1,0:T(8,128)S(1)}, f32[256,128]{1,0:T(8,128)S(1)}, f32[328,128]{1,0:T(8,128)S(1)}, f32[328,128]{1,0:T(8,128)S(1)}) custom-call(f32[9,16,128]{2,1,0:T(8,128)S(1)} %collective-permute-done.recv_a.ygas_a, f32[9,16,128]{2,1,0:T(8,128)S(1)} %collective-permute-done.1.recv_b.ygas_b, ...), custom_call_target="tpu_custom_call" | custom-call | flops 1585446912 | bytes 81920 | tf_op jit(solution)/shard_map/deposit_arrivals/pallas_call | solution.py:42
  19.8 0.1 collective-permute-start.3
  19.9 3.3 %collective-permute-start.4 = (f32[328,128]{1,0:T(8,128)S(1)}, f32[328,128]{1,0:T(8,128)S(1)}, u32[]{:S(2)}, u32[]{:S(2)}) collective-permute-start(f32[328,128]{1,0:T(8,128)S(1)} %get-tuple-element.38), channel_id=1, source_target_pairs={{0,15},{1,2},{2,1},{3,4},{4,3},{5,6},{6,5},{7,8},{8,7},{9,10},{10,... | collective-permute-start | bytes 503816 | tf_op jit(solution)/shard_map/ppermute | solution.py:635
  23.2 3.4 %tables.1 = (bf16[64,416,128]{2,1,0:T(8,128)(2,1)S(1)}, f8e4m3fn[64,512,128]{2,1,0:T(32,128)(4,1)S(1)}, f32[64,128,128]{2,1,0:T(8,128)S(1)}) custom-call(s32[48,128]{1,0:T(8,128)S(1)} %get-tuple-element.29.cells, s32[3,48,128]{2,1,0:T(8,128)S(1)} %get-tuple-element.30.offsets, f32[256,128]{1,0:T(8,128)S(1)} %get-tuple-element.32.arrivals), custom_call_target="tpu_custom_call" | custom-call | flops 3170893824 | bytes 327680 | tf_op jit(solution)/shard_map/tables/pallas_call | solution.py:42
  26.6 1.4 %collective-permute-done.3.recv_a = f32[328,128]{1,0:T(8,128)S(1)} collective-permute-done((f32[328,128]{1,0:T(8,128)S(1)}, f32[328,128]{1,0:T(8,128)S(1)}, u32[]{:S(2)}, u32[]{:S(2)}) %collective-permute-start.3) | collective-permute-done | bytes 167968 | tf_op jit(solution)/shard_map/ppermute | solution.py:635
  28.0 2.3 %collective-permute-done.4.recv_b = f32[328,128]{1,0:T(8,128)S(1)} collective-permute-done((f32[328,128]{1,0:T(8,128)S(1)}, f32[328,128]{1,0:T(8,128)S(1)}, u32[]{:S(2)}, u32[]{:S(2)}) %collective-permute-start.4) | collective-permute-done | bytes 167968 | tf_op jit(solution)/shard_map/ppermute | solution.py:635
  30.3 0.2 widen.1
  30.5 0.1 collective-permute-start.5
  30.6 1.8 %collective-permute-done.5.xrecv = f32[2,472,128]{2,1,0:T(8,128)S(1)} collective-permute-done((f32[2,472,128]{2,1,0:T(8,128)S(1)}, f32[2,472,128]{2,1,0:T(8,128)S(1)}, u32[]{:S(2)}, u32[]{:S(2)}) %collective-permute-start.5) | collective-permute-done | bytes 483360 | tf_op jit(solution)/shard_map/ppermute | solution.py:622
  32.4 10.2 %finish.1 = (f32[768,128]{1,0:T(8,128)}, f32[3,64,128]{2,1,0:T(8,128)}) custom-call(f32[48,128]{1,0:T(8,128)S(1)} %get-tuple-element.23.stays, f32[3,48,128]{2,1,0:T(8,128)S(1)} %get-tuple-element.24.velocity, f32[768,128]{1,0:T(8,128)S(1)} %get-tuple-element.25.gas, f32[2,10,16,128]{3,2,1,0:T(8,128)S(1)} %collective-permute-done.2.xrecv.xgas, ...), custom_call_target="tpu_custom_call" | custom-call | flops 6341787648 | bytes 327680 | tf_op jit(solution)/shard_map/finish/pallas_call | solution.py:42
  (1 shorter events, 0.0 us)
Async XLA Ops:
  2.1 12.0 %collective-permute-start = (f32[9,16,128]{2,1,0:T(8,128)S(1)}, f32[9,16,128]{2,1,0:T(8,128)S(1)}, u32[]{:S(2)}, u32[]{:S(2)}) collective-permute-start(f32[9,16,128]{2,1,0:T(8,128)S(1)} %get-tuple-element.26), channel_id=1, source_target_pairs={{0,1},{1,0},{2,3},{3,2},{4,5},{5,4},{6,7},{7,6},{8,9},{9,8},{10,11... | collective-permute-start | bytes 221192 | tf_op jit(solution)/shard_map/ppermute | solution.py:635
  5.3 8.9 %collective-permute-start.1 = (f32[9,16,128]{2,1,0:T(8,128)S(1)}, f32[9,16,128]{2,1,0:T(8,128)S(1)}, u32[]{:S(2)}, u32[]{:S(2)}) collective-permute-start(f32[9,16,128]{2,1,0:T(8,128)S(1)} %get-tuple-element.27), channel_id=1, source_target_pairs={{0,15},{1,2},{2,1},{3,4},{4,3},{5,6},{6,5},{7,8},{8,7},{9,10},{10,... | collective-permute-start | bytes 221192 | tf_op jit(solution)/shard_map/ppermute | solution.py:635
  14.2 2.8 %collective-permute-start.2 = (f32[2,10,16,128]{3,2,1,0:T(8,128)S(1)}, f32[2,10,16,128]{3,2,1,0:T(8,128)S(1)}, u32[]{:S(2)}, u32[]{:S(2)}) collective-permute-start(f32[2,10,16,128]{3,2,1,0:T(8,128)S(1)} %join.1.xsend), channel_id=1, source_target_pairs={{0,16},{16,0},{1,17},{17,1},{2,18},{18,2},{3,19},{19,3},{4,20},{20... | collective-permute-start | bytes 491528 | tf_op jit(solution)/shard_map/ppermute | solution.py:622
  19.8 8.2 %collective-permute-start.3 = (f32[328,128]{1,0:T(8,128)S(1)}, f32[328,128]{1,0:T(8,128)S(1)}, u32[]{:S(2)}, u32[]{:S(2)}) collective-permute-start(f32[328,128]{1,0:T(8,128)S(1)} %get-tuple-element.37), channel_id=1, source_target_pairs={{0,1},{1,0},{2,3},{3,2},{4,5},{5,4},{6,7},{7,6},{8,9},{9,8},{10,11... | collective-permute-start | bytes 503816 | tf_op jit(solution)/shard_map/ppermute | solution.py:635
  19.9 10.4 %collective-permute-start.4 = (f32[328,128]{1,0:T(8,128)S(1)}, f32[328,128]{1,0:T(8,128)S(1)}, u32[]{:S(2)}, u32[]{:S(2)}) collective-permute-start(f32[328,128]{1,0:T(8,128)S(1)} %get-tuple-element.38), channel_id=1, source_target_pairs={{0,15},{1,2},{2,1},{3,4},{4,3},{5,6},{6,5},{7,8},{8,7},{9,10},{10,... | collective-permute-start | bytes 503816 | tf_op jit(solution)/shard_map/ppermute | solution.py:635
  30.5 1.9 %collective-permute-start.5 = (f32[2,472,128]{2,1,0:T(8,128)S(1)}, f32[2,472,128]{2,1,0:T(8,128)S(1)}, u32[]{:S(2)}, u32[]{:S(2)}) collective-permute-start(f32[2,472,128]{2,1,0:T(8,128)S(1)} %get-tuple-element.41), channel_id=1, source_target_pairs={{0,16},{16,0},{1,17},{17,1},{2,18},{18,2},{3,19},{19,3},{4,20},{20... | collective-permute-start | bytes 1449992 | tf_op jit(solution)/shard_map/ppermute | solution.py:622

commit v4 on v3

--- a/solution.py
+++ b/solution.py
@@ -101,7 +101,7 @@
             columns[pl.ds(first * COLS + i, count, stride=COLS), :] = value
 
     def vertical(self, columns, slot):
-        start = pl.multiple_of(slot * COLS, COLS)
+        start = slot * COLS if isinstance(slot, int) else pl.multiple_of(slot * COLS, COLS)
         rows = [columns[pl.ds(start, COLS), :][j : j + 1] for j in range(9)]
         iz = lax.broadcasted_iota(jnp.int32, (self.nz, rows[0].shape[1]), 0).astype(jnp.float32)
         tz = jnp.where(iz == rows[2], rows[5], 0.0)
@@ -149,19 +149,10 @@
 
 def pipeline(steps, build, use):
     build(0, 0)
-    assert steps % 2 == 0
-
-    def pair(i, carry):
-        use(0, 2 * i)
-        build(1, 2 * i + 1)
-        use(1, 2 * i + 1)
-        build(0, 2 * i + 2)
-        return carry
-
-    lax.fori_loop(0, steps // 2 - 1, pair, 0, unroll=True)
-    use(0, steps - 2)
-    build(1, steps - 1)
-    use(1, steps - 1)
+    for step in range(steps):
+        use(step % 2, step)
+        if step + 1 < steps:
+            build((step + 1) % 2, step + 1)
 
 
 def deposit(tile, slots, fields, columns, acc, cross, left, left8, right, right8):
@@ -193,8 +184,10 @@
                 preferred_element_type=jnp.float32,
             )
 
-        acc[...] += pieces(left[buffer], right[buffer], 2)
-        cross[...] += pieces(left8[buffer], right8[buffer], 4)
+        exact = pieces(left[buffer], right[buffer], 2)
+        coarse = pieces(left8[buffer], right8[buffer], 4)
+        acc[...] = acc[...] + exact if step else exact
+        cross[...] = cross[...] + coarse if step else coarse
 
     pipeline(slots // 2, build, use)
 
@@ -326,12 +319,9 @@
 
 
 def deposit_blocks(tile, cell, sixteenths, force, acc, fields, columns, *buffers):
-    acc[...] = jnp.zeros(acc.shape, jnp.float32)
-    columns[...] = jnp.zeros(columns.shape, jnp.float32)
     force, factor = scaled(force, 0.75)
     tile.prepare(0, cell, sixteenths, fields, columns, force)
     cross = buffers[8]
-    cross[...] = jnp.zeros(cross.shape, jnp.float32)
     pairs = [buffers[i : i + 2] for i in range(0, 8, 2)]
     for buffer in pairs[1]:
         buffer[:, tile.rows :] = jnp.zeros((4, tile.rows8 - tile.rows, 128), F8)
@@ -455,78 +445,7 @@
             xsend[1, row + REACH : row + EDGE] = beyond[k, 1, y : y + 1]
 
 
-def tables_kernel(
-    tile, slots, cells, offsets, arrivals, tables, tables8, verticals, fields, columns
-):
-    blocks = 8 * CAP
-    tile.prepare(0, cells[...], [offsets[k].astype(jnp.float32) for k in range(3)], fields, columns)
-    sixteenths = [record_row(arrivals, 7 + k, blocks) for k in range(3)]
-    cell = record_row(arrivals, 6, blocks).astype(jnp.int32)
-    tile.prepare(slots, cell, sixteenths, fields, columns)
-
-    def build(pair, carry):
-        for i in range(2):
-            slot = pair * 2 + i
-            row = 0
-            for part in tile.planar(fields, slot):
-                top, low = halves(part)
-                count = part.shape[0]
-                tables[slot, row : row + count] = top
-                if row < COARSE:
-                    tables8[slot, row : row + count] = part.astype(F8)
-                    tables8[slot, COARSE + row : COARSE + row + count] = low.astype(F8)
-                else:
-                    down = tile.rows - COARSE + row
-                    tables[slot, down : down + count] = low.astype(jnp.bfloat16)
-                row += count
-            verticals[slot], _ = tile.vertical(columns, slot)
-        return carry
-
-    lax.fori_loop(0, (slots + blocks) // 2, build, 0)
-
-
-def finish_kernel(
-    tile, axis, count, slots, stays, velocity, gas, xgas, ygas_a, ygas_b, arrivals,
-    tables, tables8, verticals, mid, beyond, xrecv, gas_out, slip,
-    src, ping, pong, field, field8, stack, gas_new, sem,
-):
-    _, a_from_high = ty_roles(axis, count)
-    zero = SUB + SWEEPS
-    after = zero + tile.wx
-    swept = tile.wx + 2 * SWEEPS
-    for k in range(3):
-        for y in range(tile.yw):
-            row = (k * tile.yw + y) * EDGE
-            src[k, y, zero - SUB : zero] = jnp.zeros((SUB, tile.nz), jnp.float32)
-            src[k, y, zero:after] = mid[k, y]
-            src[k, y, after : after + SUB] = jnp.zeros((SUB, tile.nz), jnp.float32)
-            src[k, y, zero - REACH : zero] = xrecv[1, row : row + REACH]
-            src[k, y, after : after + REACH] = xrecv[0, row + 1 : row + EDGE]
-            src[k, y, zero - 1 : zero] += beyond[k, 0, y : y + 1]
-            src[k, y, after : after + 1] += beyond[k, 1, y : y + 1]
-            src[k, y, zero : zero + 1] += xrecv[1, row + REACH : row + EDGE]
-            src[k, y, after - 1 : after] += xrecv[0, row : row + 1]
-
-    def sweep(old, new, margin):
-        def row(y, carry):
-            for k in range(3):
-                here = old[k, y, SUB : SUB + swept]
-                around = old[k, y - 1, SUB : SUB + swept] + old[k, y + 1, SUB : SUB + swept]
-                around = around + old[k, y, SUB - 1 : SUB - 1 + swept]
-                around = around + old[k, y, SUB + 1 : SUB + 1 + swept]
-                around = around + pltpu.roll(here, 1, 1) + pltpu.roll(here, tile.nz - 1, 1)
-                total = src[k, y, SUB : SUB + swept] + DIFFUSE * around
-                new[k, y, SUB : SUB + swept] = total * (1.0 / (1.0 + 6.0 * DIFFUSE))
-            return carry
-
-        rows = tile.yw - 2 * margin
-        lax.fori_loop(margin, tile.yw - margin, row, 0, unroll=rows // 2)
-
-    buffers = [src, ping, pong, ping, pong]
-    for index in range(SWEEPS):
-        sweep(buffers[index], buffers[index + 1], index + 1)
-    filtered = buffers[SWEEPS]
-
+def stack_gas(tile, a_from_high, gas, xgas, ygas_a, ygas_b, stack):
     per_x, per_y = tile.wx // REC, tile.wy // REC
 
     def take_edges(ref, high):
@@ -555,23 +474,98 @@
         lambda: (take_edges(ygas_a, True), take_edges(ygas_b, False)) and None,
         lambda: (take_edges(ygas_a, False), take_edges(ygas_b, True)) and None,
     )
+
+
+def tables_kernel(
+    tile, axis, count, slots, cells, offsets, arrivals, gas, xgas, ygas_a, ygas_b,
+    tables, tables8, verticals, stack, fields, columns,
+):
+    blocks = 8 * CAP
+    tile.prepare(0, cells[...], [offsets[k].astype(jnp.float32) for k in range(3)], fields, columns)
+    sixteenths = [record_row(arrivals, 7 + k, blocks) for k in range(3)]
+    cell = record_row(arrivals, 6, blocks).astype(jnp.int32)
+    tile.prepare(slots, cell, sixteenths, fields, columns)
+
+    def build(pair, carry):
+        for i in range(2):
+            slot = pair * 2 + i
+            row = 0
+            for part in tile.planar(fields, slot):
+                top, low = halves(part)
+                height = part.shape[0]
+                tables[slot, row : row + height] = top
+                if row < COARSE:
+                    tables8[slot, row : row + height] = part.astype(F8)
+                    tables8[slot, COARSE + row : COARSE + row + height] = low.astype(F8)
+                else:
+                    down = tile.rows - COARSE + row
+                    tables[slot, down : down + height] = low.astype(jnp.bfloat16)
+                row += height
+            verticals[slot], _ = tile.vertical(columns, slot)
+        return carry
+
+    lax.fori_loop(0, (slots + blocks) // 2, build, 0)
+    _, a_from_high = ty_roles(axis, count)
+    stack_gas(tile, a_from_high, gas, xgas, ygas_a, ygas_b, stack)
+
+
+def finish_kernel(
+    tile, slots, stays, velocity, arrivals, tables, tables8, verticals, stack,
+    mid, beyond, xrecv, gas_out, slip, src, ping, pong, field, field8, ext, gas_new, sem,
+):
+    zero = SUB + SWEEPS
+    after = zero + tile.wx
+    swept = tile.wx + 2 * SWEEPS
     for k in range(3):
+        for y in range(tile.yw):
+            row = (k * tile.yw + y) * EDGE
+            src[k, y, zero - SUB : zero] = jnp.zeros((SUB, tile.nz), jnp.float32)
+            src[k, y, zero:after] = mid[k, y]
+            src[k, y, after : after + SUB] = jnp.zeros((SUB, tile.nz), jnp.float32)
+            src[k, y, zero - REACH : zero] = xrecv[1, row : row + REACH]
+            src[k, y, after : after + REACH] = xrecv[0, row + 1 : row + EDGE]
+            src[k, y, zero - 1 : zero] += beyond[k, 0, y : y + 1]
+            src[k, y, after : after + 1] += beyond[k, 1, y : y + 1]
+            src[k, y, zero : zero + 1] += xrecv[1, row + REACH : row + EDGE]
+            src[k, y, after - 1 : after] += xrecv[0, row : row + 1]
+
+    def sweep(old, new, margin):
+        def row(y):
+            for k in range(3):
+                here = old[k, y, SUB : SUB + swept]
+                around = old[k, y - 1, SUB : SUB + swept] + old[k, y + 1, SUB : SUB + swept]
+                around = around + old[k, y, SUB - 1 : SUB - 1 + swept]
+                around = around + old[k, y, SUB + 1 : SUB + 1 + swept]
+                around = around + pltpu.roll(here, 1, 1) + pltpu.roll(here, tile.nz - 1, 1)
+                total = src[k, y, SUB : SUB + swept] + DIFFUSE * around
+                new[k, y, SUB : SUB + swept] = total * (1.0 / (1.0 + 6.0 * DIFFUSE))
+
+        for y in range(margin, tile.yw - margin):
+            row(y)
+
+    buffers = [src, ping, pong, ping, pong]
+    for index in range(SWEEPS):
+        sweep(buffers[index], buffers[index + 1], index + 1)
+    filtered = buffers[SWEEPS]
+
+    for k in range(3):
+        ext[k, tile.main :] = stack[k, tile.main :]
         for y in range(tile.ye):
             rows = slice(y * tile.wx, (y + 1) * tile.wx)
             updated = stack[k, rows] + STEP_SIZE * filtered[k, y + REACH - 1, zero:after]
-            stack[k, rows] = updated
+            ext[k, rows] = updated
             if 1 <= y <= tile.wy:
                 gas_new[pl.ds(k * tile.wx * tile.wy + y - 1, tile.wx, stride=tile.wy), :] = updated
             for h, x in ((0, zero - 1), (1, after)):
                 row = tile.main + h * tile.hp + y
-                stack[k, row : row + 1] += STEP_SIZE * filtered[k, y + REACH - 1, x : x + 1]
+                ext[k, row : row + 1] += STEP_SIZE * filtered[k, y + REACH - 1, x : x + 1]
     leave = pltpu.make_async_copy(gas_new, gas_out, sem)
     leave.start()
     blocks = 8 * CAP
     total = slots + blocks
     fine = tile.rows - COARSE
     pad_rows = round_up(3 * fine, 128) - 3 * fine
-    values, factor = scaled([stack[k] for k in range(3)], 1.0)
+    values, factor = scaled([ext[k] for k in range(3)], 1.0)
     for k, value in enumerate(values):
         top = value.astype(jnp.bfloat16).astype(jnp.float32)
         low = value - top
@@ -607,7 +601,7 @@
                 slip[k, pl.ds(pair * 2 + i, 1)] = value
         return carry
 
-    lax.fori_loop(0, total // 2, sample, 0, unroll=8)
+    lax.fori_loop(0, total // 2, sample, 0, unroll=16)
     live = record_row(arrivals, 10, blocks)
     for k in range(3):
         slip[k, :slots] = (slip[k, :slots] * factor - velocity[k]) * stays[...]
@@ -704,14 +698,15 @@
     got_a, got_b = exchange_y(edge_a, edge_b, "ty", count_y)
     total = slots + blocks
     fine = tile.rows - COARSE
-    tables, tables8, verticals = call(
-        bind(tables_kernel, tile, slots),
+    tables, tables8, verticals, stack = call(
+        bind(tables_kernel, tile, "ty", count_y, slots),
         [
             ((total, tile.rows + fine, lanes), jnp.bfloat16),
             ((total, 2 * COARSE, lanes), F8),
             (total, tile.nz, lanes),
+            (3, tile.rows, tile.nz),
         ],
-        [cells, offsets, arrivals],
+        [cells, offsets, arrivals, gas_rows, xrecv, recv_a, recv_b],
         scratch=[
             pltpu.VMEM((8, total, lanes), jnp.float32),
             pltpu.VMEM((total * COLS, lanes), jnp.float32),
@@ -733,10 +728,9 @@
     xgot = exchange_x(xedge, "tx", count_x)
     wide = (3, tile.yw, round_up(tile.wx + SUB + SWEEPS + SUB, SUB), tile.nz)
     gas_new, slip = call(
-        bind(finish_kernel, tile, "ty", count_y, slots),
+        bind(finish_kernel, tile, slots),
         [gas_rows.shape, (3, total, lanes)],
-        [stays, velocity, gas_rows, xrecv, recv_a, recv_b, arrivals]
-        + [tables, tables8, verticals, mid, beyond, xgot],
+        [stays, velocity, arrivals, tables, tables8, verticals, stack, mid, beyond, xgot],
         scratch=[
             *[pltpu.VMEM(wide, jnp.float32)] * 3,
             pltpu.VMEM(((COARSE + round_up(3 * fine, 128)) // 128, 3 * tile.nz, 128), jnp.bfloat16),

time: 42.9 us -> 41.5 us (0.967)
  Pallas kernels: 25.5 us -> 24.1 us
    pallas_call x8, Pallas kernels: 25.5 us -> 24.1 us  [call(): pl.pallas_call(body, out_shape=[kind(*out) if isinstance(out[0], tuple) e...]
    ppermute x2, starting transfers between devices: 7.45 us -> 7.9 us  [exchange_y(): lax.ppermute(send_b, axis, perm_b)]
  transfers between devices with their start and end apart: 6 -> 6, of which waited for: 3 -> 3; matrix products, arithmetic and copies ran while one was open for 0% -> 0% of each run, Pallas kernels for 25% -> 26%
where the time goes in v4:
time: 41.5 us; the launch traced here: 41.4 us
  Pallas kernels  24.1 us (58%)
  starting transfers between devices  11 us (27%)
  waiting for transfers between devices  5.36 us (13%)
  between operations  0.89 us (2%)
    pallas_call x8, Pallas kernels, call(): pl.pallas_call(body, out_shape=[kind(*out) if isinstance(out[0], tuple) e...  24.1 us
    ppermute x2, starting transfers between devices, exchange_y(): lax.ppermute(send_b, axis, perm_b)  7.9 us
    ppermute x2, starting transfers between devices, exchange_y(): lax.ppermute(send_a, axis, perm_a)  3 us
    ppermute x2, waiting for transfers between devices, exchange_y(): lax.ppermute(send_b, axis, perm_b)  2.27 us
    ppermute x2, waiting for transfers between devices, exchange_x(): return lax.ppermute(buffer, axis, forward)  1.84 us
    ppermute x2, waiting for transfers between devices, exchange_y(): lax.ppermute(send_a, axis, perm_a)  1.24 us
  transfers between devices with their start and end apart: 6, of which 3 were waited for; matrix products, arithmetic and copies ran while one was open for 0% of the time, Pallas kernels for 26%

profile of v4, /device:TPU:0, one launch (start us, length us, event | category | flops | bytes accessed | tf_op | source)
XLA Modules:
  0.0 41.4 jit_solution(6967024892237962009)
XLA Ops:
  0.6 1.4 %pack.1 = (f32[9,16,128]{2,1,0:T(8,128)S(1)}, f32[9,16,128]{2,1,0:T(8,128)S(1)}, f32[2,2,16,128]{3,2,1,0:T(8,128)S(1)}, f32[48,128]{1,0:T(8,128)S(1)}, s32[48,12...) custom-call(s32[48]{0:T(128)} %bitcast.21, ...), custom_call_target="tpu_custom_call" | custom-call | tf_op jit(solution)/shard_map/pack/pallas_call | solution.py:42
  2.0 2.9 %collective-permute-start = (f32[9,16,128]{2,1,0:T(8,128)S(1)}, f32[9,16,128]{2,1,0:T(8,128)S(1)}, u32[]{:S(2)}, u32[]{:S(2)}) collective-permute-start(f32[9,16,128]{2,1,0:T(8,128)S(1)} %get-tuple-element.26), channel_id=1, source_target_pairs={{0,1},{1,0},{2,3},{3,2},{4,5},{5,4},{6,7},{7,6},{8,9},{9,8},{10,11... | collective-permute-start | bytes 221192 | tf_op jit(solution)/shard_map/ppermute | solution.py:629
  5.0 4.6 %collective-permute-start.1 = (f32[9,16,128]{2,1,0:T(8,128)S(1)}, f32[9,16,128]{2,1,0:T(8,128)S(1)}, u32[]{:S(2)}, u32[]{:S(2)}) collective-permute-start(f32[9,16,128]{2,1,0:T(8,128)S(1)} %get-tuple-element.27), channel_id=1, source_target_pairs={{0,15},{1,2},{2,1},{3,4},{4,3},{5,6},{6,5},{7,8},{8,7},{9,10},{10,... | collective-permute-start | bytes 221192 | tf_op jit(solution)/shard_map/ppermute | solution.py:629
  9.6 4.7 %deposit_first.1.acc.acc_in = f32[336,384]{1,0:T(8,128)S(1)} custom-call(s32[48,128]{1,0:T(8,128)S(1)} %get-tuple-element.30.cells, s32[3,48,128]{2,1,0:T(8,128)S(1)} %get-tuple-element.31.offsets, f32[3,48,128]{2,1,0:T(8,128)S(1)} %get-tuple-element.32.drag, f32[48,128]{1,0:T(8,128)S(1)} %get-tuple-element.24.stays), custom_call_target="tpu_custom_call" | custom-call | flops 3170893824 | bytes 163840 | tf_op jit(solution)/shard_map/deposit_first/pallas_call | solution.py:42
  14.3 0.0 collective-permute-done.recv_a.ygas_a
  14.3 0.0 collective-permute-done.1.recv_b.ygas_b
  14.3 0.1 collective-permute-start.2
  14.4 2.7 %deposit_second.1.acc_in = f32[336,384]{1,0:T(8,128)S(1)} custom-call(s32[48,128]{1,0:T(8,128)S(1)} %get-tuple-element.30.cells, s32[3,48,128]{2,1,0:T(8,128)S(1)} %get-tuple-element.31.offsets, f32[3,48,128]{2,1,0:T(8,128)S(1)} %get-tuple-element.32.drag, f32[48,128]{1,0:T(8,128)S(1)} %get-tuple-element.24.stays, f32[336,384]{1,0:T(8,128)S(1)} %deposit_first.1.acc.acc_in, ...), custom_call_target="tpu_custom_call" | custom-call | flops 1585446912 | bytes 81920 | tf_op jit(solution)/shard_map/deposit_second/pallas_call | solution.py:42
  17.1 0.0 collective-permute-done.2.xrecv.xgas
  17.2 2.8 %deposit_arrivals.1 = (f32[336,384]{1,0:T(8,128)S(1)}, f32[256,128]{1,0:T(8,128)S(1)}, f32[328,128]{1,0:T(8,128)S(1)}, f32[328,128]{1,0:T(8,128)S(1)}) custom-call(f32[9,16,128]{2,1,0:T(8,128)S(1)} %collective-permute-done.recv_a.ygas_a, f32[9,16,128]{2,1,0:T(8,128)S(1)} %collective-permute-done.1.recv_b.ygas_b, ...), custom_call_target="tpu_custom_call" | custom-call | flops 1585446912 | bytes 81920 | tf_op jit(solution)/shard_map/deposit_arrivals/pallas_call | solution.py:42
  19.9 0.1 collective-permute-start.3
  20.0 3.3 %collective-permute-start.4 = (f32[328,128]{1,0:T(8,128)S(1)}, f32[328,128]{1,0:T(8,128)S(1)}, u32[]{:S(2)}, u32[]{:S(2)}) collective-permute-start(f32[328,128]{1,0:T(8,128)S(1)} %get-tuple-element.40), channel_id=1, source_target_pairs={{0,15},{1,2},{2,1},{3,4},{4,3},{5,6},{6,5},{7,8},{8,7},{9,10},{10,... | collective-permute-start | bytes 503816 | tf_op jit(solution)/shard_map/ppermute | solution.py:629
  23.3 3.5 %tables.1 = (bf16[64,416,128]{2,1,0:T(8,128)(2,1)S(1)}, f8e4m3fn[64,512,128]{2,1,0:T(32,128)(4,1)S(1)}, f32[64,128,128]{2,1,0:T(8,128)S(1)}, f32[3,336,128]{2,1,0:T(8,128)S(1)}) custom-call(s32[48,128]{1,0:T(8,128)S(1)} %get-tuple-element.30.cells, s32[3,48,128]{2,1,0:T(8,128)S(1)} %get-tuple-element.31.offsets, f32[256,128]{1,0:T(8,128)S(1)} %get-tuple-element.33.arrivals, ...), custom_call_target="tpu_custom_call" | custom-call | flops 3170893824 | bytes 327680 | tf_op jit(solution)/shard_map/tables/pallas_call | solution.py:42
  26.8 1.2 %collective-permute-done.3.recv_a = f32[328,128]{1,0:T(8,128)S(1)} collective-permute-done((f32[328,128]{1,0:T(8,128)S(1)}, f32[328,128]{1,0:T(8,128)S(1)}, u32[]{:S(2)}, u32[]{:S(2)}) %collective-permute-start.3) | collective-permute-done | bytes 167968 | tf_op jit(solution)/shard_map/ppermute | solution.py:629
  28.1 2.3 %collective-permute-done.4.recv_b = f32[328,128]{1,0:T(8,128)S(1)} collective-permute-done((f32[328,128]{1,0:T(8,128)S(1)}, f32[328,128]{1,0:T(8,128)S(1)}, u32[]{:S(2)}, u32[]{:S(2)}) %collective-permute-start.4) | collective-permute-done | bytes 167968 | tf_op jit(solution)/shard_map/ppermute | solution.py:629
  30.3 0.4 widen.1
  30.7 0.1 collective-permute-start.5
  30.8 1.8 %collective-permute-done.5.xrecv = f32[2,472,128]{2,1,0:T(8,128)S(1)} collective-permute-done((f32[2,472,128]{2,1,0:T(8,128)S(1)}, f32[2,472,128]{2,1,0:T(8,128)S(1)}, u32[]{:S(2)}, u32[]{:S(2)}) %collective-permute-start.5) | collective-permute-done | bytes 483360 | tf_op jit(solution)/shard_map/ppermute | solution.py:616
  32.6 8.6 %finish.1 = (f32[768,128]{1,0:T(8,128)}, f32[3,64,128]{2,1,0:T(8,128)}) custom-call(f32[48,128]{1,0:T(8,128)S(1)} %get-tuple-element.24.stays, f32[3,48,128]{2,1,0:T(8,128)S(1)} %get-tuple-element.25.velocity, f32[256,128]{1,0:T(8,128)S(1)} %get-tuple-element.33.arrivals, bf16[64,416,128]{2,1,0:T(8,128)(2,1)S(1)} %get-tuple-element.34.tables, ...), custom_call_target="tpu_custom_call" | custom-call | flops 6341787648 | bytes 327680 | tf_op jit(solution)/shard_map/finish/pallas_call | solution.py:42
  (1 shorter events, 0.0 us)
Async XLA Ops:
  2.0 12.3 %collective-permute-start = (f32[9,16,128]{2,1,0:T(8,128)S(1)}, f32[9,16,128]{2,1,0:T(8,128)S(1)}, u32[]{:S(2)}, u32[]{:S(2)}) collective-permute-start(f32[9,16,128]{2,1,0:T(8,128)S(1)} %get-tuple-element.26), channel_id=1, source_target_pairs={{0,1},{1,0},{2,3},{3,2},{4,5},{5,4},{6,7},{7,6},{8,9},{9,8},{10,11... | collective-permute-start | bytes 221192 | tf_op jit(solution)/shard_map/ppermute | solution.py:629
  5.0 9.3 %collective-permute-start.1 = (f32[9,16,128]{2,1,0:T(8,128)S(1)}, f32[9,16,128]{2,1,0:T(8,128)S(1)}, u32[]{:S(2)}, u32[]{:S(2)}) collective-permute-start(f32[9,16,128]{2,1,0:T(8,128)S(1)} %get-tuple-element.27), channel_id=1, source_target_pairs={{0,15},{1,2},{2,1},{3,4},{4,3},{5,6},{6,5},{7,8},{8,7},{9,10},{10,... | collective-permute-start | bytes 221192 | tf_op jit(solution)/shard_map/ppermute | solution.py:629
  14.3 2.8 %collective-permute-start.2 = (f32[2,10,16,128]{3,2,1,0:T(8,128)S(1)}, f32[2,10,16,128]{3,2,1,0:T(8,128)S(1)}, u32[]{:S(2)}, u32[]{:S(2)}) collective-permute-start(f32[2,10,16,128]{3,2,1,0:T(8,128)S(1)} %join.1.xsend), channel_id=1, source_target_pairs={{0,16},{16,0},{1,17},{17,1},{2,18},{18,2},{3,19},{19,3},{4,20},{20... | collective-permute-start | bytes 491528 | tf_op jit(solution)/shard_map/ppermute | solution.py:616
  19.9 8.1 %collective-permute-start.3 = (f32[328,128]{1,0:T(8,128)S(1)}, f32[328,128]{1,0:T(8,128)S(1)}, u32[]{:S(2)}, u32[]{:S(2)}) collective-permute-start(f32[328,128]{1,0:T(8,128)S(1)} %get-tuple-element.39), channel_id=1, source_target_pairs={{0,1},{1,0},{2,3},{3,2},{4,5},{5,4},{6,7},{7,6},{8,9},{9,8},{10,11... | collective-permute-start | bytes 503816 | tf_op jit(solution)/shard_map/ppermute | solution.py:629
  20.0 10.3 %collective-permute-start.4 = (f32[328,128]{1,0:T(8,128)S(1)}, f32[328,128]{1,0:T(8,128)S(1)}, u32[]{:S(2)}, u32[]{:S(2)}) collective-permute-start(f32[328,128]{1,0:T(8,128)S(1)} %get-tuple-element.40), channel_id=1, source_target_pairs={{0,15},{1,2},{2,1},{3,4},{4,3},{5,6},{6,5},{7,8},{8,7},{9,10},{10,... | collective-permute-start | bytes 503816 | tf_op jit(solution)/shard_map/ppermute | solution.py:629
  30.7 1.9 %collective-permute-start.5 = (f32[2,472,128]{2,1,0:T(8,128)S(1)}, f32[2,472,128]{2,1,0:T(8,128)S(1)}, u32[]{:S(2)}, u32[]{:S(2)}) collective-permute-start(f32[2,472,128]{2,1,0:T(8,128)S(1)} %get-tuple-element.43), channel_id=1, source_target_pairs={{0,16},{16,0},{1,17},{17,1},{2,18},{18,2},{3,19},{19,3},{4,20},{20... | collective-permute-start | bytes 1449992 | tf_op jit(solution)/shard_map/ppermute | solution.py:616

commit v5 on v4

--- a/solution.py
+++ b/solution.py
@@ -519,15 +519,13 @@
     for k in range(3):
         for y in range(tile.yw):
             row = (k * tile.yw + y) * EDGE
-            src[k, y, zero - SUB : zero] = jnp.zeros((SUB, tile.nz), jnp.float32)
+            src[k, y, zero - REACH : zero - 1] = xrecv[1, row : row + REACH - 1]
+            src[k, y, zero - 1 : zero] = xrecv[1, row + REACH - 1 : row + REACH] + beyond[k, 0, y : y + 1]
             src[k, y, zero:after] = mid[k, y]
-            src[k, y, after : after + SUB] = jnp.zeros((SUB, tile.nz), jnp.float32)
-            src[k, y, zero - REACH : zero] = xrecv[1, row : row + REACH]
-            src[k, y, after : after + REACH] = xrecv[0, row + 1 : row + EDGE]
-            src[k, y, zero - 1 : zero] += beyond[k, 0, y : y + 1]
-            src[k, y, after : after + 1] += beyond[k, 1, y : y + 1]
             src[k, y, zero : zero + 1] += xrecv[1, row + REACH : row + EDGE]
             src[k, y, after - 1 : after] += xrecv[0, row : row + 1]
+            src[k, y, after : after + 1] = xrecv[0, row + 1 : row + 2] + beyond[k, 1, y : y + 1]
+            src[k, y, after + 1 : after + REACH] = xrecv[0, row + 2 : row + EDGE]
 
     def sweep(old, new, margin):
         def row(y):
@@ -601,7 +599,7 @@
                 slip[k, pl.ds(pair * 2 + i, 1)] = value
         return carry
 
-    lax.fori_loop(0, total // 2, sample, 0, unroll=16)
+    lax.fori_loop(0, total // 2, sample, 0, unroll=True)
     live = record_row(arrivals, 10, blocks)
     for k in range(3):
         slip[k, :slots] = (slip[k, :slots] * factor - velocity[k]) * stays[...]

time: 41.5 us -> 42.1 us (1.014)
  no operation moved by 1% of the time
where the time goes in v5:
time: 42.1 us; the launch traced here: 42 us
  Pallas kernels  24.5 us (58%)
  starting transfers between devices  11.2 us (27%)
  waiting for transfers between devices  5.36 us (13%)
  between operations  0.89 us (2%)
    pallas_call x8, Pallas kernels, call(): pl.pallas_call(body, out_shape=[kind(*out) if isinstance(out[0], tuple) e...  24.5 us
    ppermute x2, starting transfers between devices, exchange_y(): lax.ppermute(send_b, axis, perm_b)  8.01 us
    ppermute x2, starting transfers between devices, exchange_y(): lax.ppermute(send_a, axis, perm_a)  3.1 us
    ppermute x2, waiting for transfers between devices, exchange_y(): lax.ppermute(send_b, axis, perm_b)  2.49 us
    ppermute x2, waiting for transfers between devices, exchange_x(): return lax.ppermute(buffer, axis, forward)  1.84 us
    ppermute x2, waiting for transfers between devices, exchange_y(): lax.ppermute(send_a, axis, perm_a)  1.02 us
  transfers between devices with their start and end apart: 6, of which 3 were waited for; matrix products, arithmetic and copies ran while one was open for 0% of the time, Pallas kernels for 26%

profile of v5, /device:TPU:0, one launch (start us, length us, event | category | flops | bytes accessed | tf_op | source)
XLA Modules:
  0.0 42.0 jit_solution(15208411432803707070)
XLA Ops:
  0.6 1.4 %pack.1 = (f32[9,16,128]{2,1,0:T(8,128)S(1)}, f32[9,16,128]{2,1,0:T(8,128)S(1)}, f32[2,2,16,128]{3,2,1,0:T(8,128)S(1)}, f32[48,128]{1,0:T(8,128)S(1)}, s32[48,12...) custom-call(s32[48]{0:T(128)} %bitcast.21, ...), custom_call_target="tpu_custom_call" | custom-call | tf_op jit(solution)/shard_map/pack/pallas_call | solution.py:42
  2.0 3.0 %collective-permute-start = (f32[9,16,128]{2,1,0:T(8,128)S(1)}, f32[9,16,128]{2,1,0:T(8,128)S(1)}, u32[]{:S(2)}, u32[]{:S(2)}) collective-permute-start(f32[9,16,128]{2,1,0:T(8,128)S(1)} %get-tuple-element.26), channel_id=1, source_target_pairs={{0,1},{1,0},{2,3},{3,2},{4,5},{5,4},{6,7},{7,6},{8,9},{9,8},{10,11... | collective-permute-start | bytes 221192 | tf_op jit(solution)/shard_map/ppermute | solution.py:627
  5.1 4.7 %collective-permute-start.1 = (f32[9,16,128]{2,1,0:T(8,128)S(1)}, f32[9,16,128]{2,1,0:T(8,128)S(1)}, u32[]{:S(2)}, u32[]{:S(2)}) collective-permute-start(f32[9,16,128]{2,1,0:T(8,128)S(1)} %get-tuple-element.27), channel_id=1, source_target_pairs={{0,15},{1,2},{2,1},{3,4},{4,3},{5,6},{6,5},{7,8},{8,7},{9,10},{10,... | collective-permute-start | bytes 221192 | tf_op jit(solution)/shard_map/ppermute | solution.py:627
  9.8 4.7 %deposit_first.1.acc.acc_in = f32[336,384]{1,0:T(8,128)S(1)} custom-call(s32[48,128]{1,0:T(8,128)S(1)} %get-tuple-element.30.cells, s32[3,48,128]{2,1,0:T(8,128)S(1)} %get-tuple-element.31.offsets, f32[3,48,128]{2,1,0:T(8,128)S(1)} %get-tuple-element.32.drag, f32[48,128]{1,0:T(8,128)S(1)} %get-tuple-element.24.stays), custom_call_target="tpu_custom_call" | custom-call | flops 3170893824 | bytes 163840 | tf_op jit(solution)/shard_map/deposit_first/pallas_call | solution.py:42
  14.5 0.0 collective-permute-done.recv_a.ygas_a
  14.5 0.0 collective-permute-done.1.recv_b.ygas_b
  14.6 0.1 collective-permute-start.2
  14.6 2.7 %deposit_second.1.acc_in = f32[336,384]{1,0:T(8,128)S(1)} custom-call(s32[48,128]{1,0:T(8,128)S(1)} %get-tuple-element.30.cells, s32[3,48,128]{2,1,0:T(8,128)S(1)} %get-tuple-element.31.offsets, f32[3,48,128]{2,1,0:T(8,128)S(1)} %get-tuple-element.32.drag, f32[48,128]{1,0:T(8,128)S(1)} %get-tuple-element.24.stays, f32[336,384]{1,0:T(8,128)S(1)} %deposit_first.1.acc.acc_in, ...), custom_call_target="tpu_custom_call" | custom-call | flops 1585446912 | bytes 81920 | tf_op jit(solution)/shard_map/deposit_second/pallas_call | solution.py:42
  17.4 0.0 collective-permute-done.2.xrecv.xgas
  17.4 2.8 %deposit_arrivals.1 = (f32[336,384]{1,0:T(8,128)S(1)}, f32[256,128]{1,0:T(8,128)S(1)}, f32[328,128]{1,0:T(8,128)S(1)}, f32[328,128]{1,0:T(8,128)S(1)}) custom-call(f32[9,16,128]{2,1,0:T(8,128)S(1)} %collective-permute-done.recv_a.ygas_a, f32[9,16,128]{2,1,0:T(8,128)S(1)} %collective-permute-done.1.recv_b.ygas_b, ...), custom_call_target="tpu_custom_call" | custom-call | flops 1585446912 | bytes 81920 | tf_op jit(solution)/shard_map/deposit_arrivals/pallas_call | solution.py:42
  20.1 0.1 collective-permute-start.3
  20.2 3.3 %collective-permute-start.4 = (f32[328,128]{1,0:T(8,128)S(1)}, f32[328,128]{1,0:T(8,128)S(1)}, u32[]{:S(2)}, u32[]{:S(2)}) collective-permute-start(f32[328,128]{1,0:T(8,128)S(1)} %get-tuple-element.40), channel_id=1, source_target_pairs={{0,15},{1,2},{2,1},{3,4},{4,3},{5,6},{6,5},{7,8},{8,7},{9,10},{10,... | collective-permute-start | bytes 503816 | tf_op jit(solution)/shard_map/ppermute | solution.py:627
  23.5 3.5 %tables.1 = (bf16[64,416,128]{2,1,0:T(8,128)(2,1)S(1)}, f8e4m3fn[64,512,128]{2,1,0:T(32,128)(4,1)S(1)}, f32[64,128,128]{2,1,0:T(8,128)S(1)}, f32[3,336,128]{2,1,0:T(8,128)S(1)}) custom-call(s32[48,128]{1,0:T(8,128)S(1)} %get-tuple-element.30.cells, s32[3,48,128]{2,1,0:T(8,128)S(1)} %get-tuple-element.31.offsets, f32[256,128]{1,0:T(8,128)S(1)} %get-tuple-element.33.arrivals, ...), custom_call_target="tpu_custom_call" | custom-call | flops 3170893824 | bytes 327680 | tf_op jit(solution)/shard_map/tables/pallas_call | solution.py:42
  27.0 1.0 %collective-permute-done.3.recv_a = f32[328,128]{1,0:T(8,128)S(1)} collective-permute-done((f32[328,128]{1,0:T(8,128)S(1)}, f32[328,128]{1,0:T(8,128)S(1)}, u32[]{:S(2)}, u32[]{:S(2)}) %collective-permute-start.3) | collective-permute-done | bytes 167968 | tf_op jit(solution)/shard_map/ppermute | solution.py:627
  28.1 2.5 %collective-permute-done.4.recv_b = f32[328,128]{1,0:T(8,128)S(1)} collective-permute-done((f32[328,128]{1,0:T(8,128)S(1)}, f32[328,128]{1,0:T(8,128)S(1)}, u32[]{:S(2)}, u32[]{:S(2)}) %collective-permute-start.4) | collective-permute-done | bytes 167968 | tf_op jit(solution)/shard_map/ppermute | solution.py:627
  30.6 0.4 widen.1
  30.9 0.1 collective-permute-start.5
  31.0 1.8 %collective-permute-done.5.xrecv = f32[2,472,128]{2,1,0:T(8,128)S(1)} collective-permute-done((f32[2,472,128]{2,1,0:T(8,128)S(1)}, f32[2,472,128]{2,1,0:T(8,128)S(1)}, u32[]{:S(2)}, u32[]{:S(2)}) %collective-permute-start.5) | collective-permute-done | bytes 483360 | tf_op jit(solution)/shard_map/ppermute | solution.py:614
  32.9 9.0 %finish.1 = (f32[768,128]{1,0:T(8,128)}, f32[3,64,128]{2,1,0:T(8,128)}) custom-call(f32[48,128]{1,0:T(8,128)S(1)} %get-tuple-element.24.stays, f32[3,48,128]{2,1,0:T(8,128)S(1)} %get-tuple-element.25.velocity, f32[256,128]{1,0:T(8,128)S(1)} %get-tuple-element.33.arrivals, bf16[64,416,128]{2,1,0:T(8,128)(2,1)S(1)} %get-tuple-element.34.tables, ...), custom_call_target="tpu_custom_call" | custom-call | flops 6341787648 | bytes 327680 | tf_op jit(solution)/shard_map/finish/pallas_call | solution.py:42
  (1 shorter events, 0.0 us)
Async XLA Ops:
  2.0 12.5 %collective-permute-start = (f32[9,16,128]{2,1,0:T(8,128)S(1)}, f32[9,16,128]{2,1,0:T(8,128)S(1)}, u32[]{:S(2)}, u32[]{:S(2)}) collective-permute-start(f32[9,16,128]{2,1,0:T(8,128)S(1)} %get-tuple-element.26), channel_id=1, source_target_pairs={{0,1},{1,0},{2,3},{3,2},{4,5},{5,4},{6,7},{7,6},{8,9},{9,8},{10,11... | collective-permute-start | bytes 221192 | tf_op jit(solution)/shard_map/ppermute | solution.py:627
  5.1 9.4 %collective-permute-start.1 = (f32[9,16,128]{2,1,0:T(8,128)S(1)}, f32[9,16,128]{2,1,0:T(8,128)S(1)}, u32[]{:S(2)}, u32[]{:S(2)}) collective-permute-start(f32[9,16,128]{2,1,0:T(8,128)S(1)} %get-tuple-element.27), channel_id=1, source_target_pairs={{0,15},{1,2},{2,1},{3,4},{4,3},{5,6},{6,5},{7,8},{8,7},{9,10},{10,... | collective-permute-start | bytes 221192 | tf_op jit(solution)/shard_map/ppermute | solution.py:627
  14.6 2.8 %collective-permute-start.2 = (f32[2,10,16,128]{3,2,1,0:T(8,128)S(1)}, f32[2,10,16,128]{3,2,1,0:T(8,128)S(1)}, u32[]{:S(2)}, u32[]{:S(2)}) collective-permute-start(f32[2,10,16,128]{3,2,1,0:T(8,128)S(1)} %join.1.xsend), channel_id=1, source_target_pairs={{0,16},{16,0},{1,17},{17,1},{2,18},{18,2},{3,19},{19,3},{4,20},{20... | collective-permute-start | bytes 491528 | tf_op jit(solution)/shard_map/ppermute | solution.py:614
  20.1 7.9 %collective-permute-start.3 = (f32[328,128]{1,0:T(8,128)S(1)}, f32[328,128]{1,0:T(8,128)S(1)}, u32[]{:S(2)}, u32[]{:S(2)}) collective-permute-start(f32[328,128]{1,0:T(8,128)S(1)} %get-tuple-element.39), channel_id=1, source_target_pairs={{0,1},{1,0},{2,3},{3,2},{4,5},{5,4},{6,7},{7,6},{8,9},{9,8},{10,11... | collective-permute-start | bytes 503816 | tf_op jit(solution)/shard_map/ppermute | solution.py:627
  20.2 10.3 %collective-permute-start.4 = (f32[328,128]{1,0:T(8,128)S(1)}, f32[328,128]{1,0:T(8,128)S(1)}, u32[]{:S(2)}, u32[]{:S(2)}) collective-permute-start(f32[328,128]{1,0:T(8,128)S(1)} %get-tuple-element.40), channel_id=1, source_target_pairs={{0,15},{1,2},{2,1},{3,4},{4,3},{5,6},{6,5},{7,8},{8,7},{9,10},{10,... | collective-permute-start | bytes 503816 | tf_op jit(solution)/shard_map/ppermute | solution.py:627
  30.9 1.9 %collective-permute-start.5 = (f32[2,472,128]{2,1,0:T(8,128)S(1)}, f32[2,472,128]{2,1,0:T(8,128)S(1)}, u32[]{:S(2)}, u32[]{:S(2)}) collective-permute-start(f32[2,472,128]{2,1,0:T(8,128)S(1)} %get-tuple-element.43), channel_id=1, source_target_pairs={{0,16},{16,0},{1,17},{17,1},{2,18},{18,2},{3,19},{19,3},{4,20},{20... | collective-permute-start | bytes 1449992 | tf_op jit(solution)/shard_map/ppermute | solution.py:614
